TPU v7x, 256 devices: a whole 4x4x8 slice. The times are simulated.
256 devices in a mesh: section: 4 (over y), task: 4 (over x), mp: 16 (over z, core).
Axes of the slice: x: 4, y: 4, z: 8, core: 2. Of those that a mesh axis runs over, the one named last changes fastest.
Arguments:
- hidden_in: bfloat16 [4, 256, 3584], P('task', 'mp'), may hold values from -6 to 6
- lengths: int32 [4], P('task'), may hold values from 128 to 256
- layer_targets: bfloat16 [4, 4, 256, 3584], P('section', 'task', 'mp'), may hold values from -27 to 27
- task_weights: float32 [4], replicated, may hold values from 0.25 to 1
- norm_gains: float32 [4, 2, 3584], P('section'), may hold values from 0.5 to 1.5
- query_weight: bfloat16 [4, 4, 3584, 4096], P('task', 'section', None, 'mp'), may hold values from -0.40089186 to 0.40089186
- key_weight: bfloat16 [4, 4, 3584, 2048], P('task', 'section', None, 'mp'), may hold values from -0.40089186 to 0.40089186
- value_weight: bfloat16 [4, 4, 3584, 2048], P('task', 'section', None, 'mp'), may hold values from -0.09375 to 0.09375
- output_weight: bfloat16 [4, 4, 4096, 3584], P('task', 'section', 'mp'), may hold values from -0.09375 to 0.09375
- query_fisher: bfloat16 [4, 4, 3584, 4096], P('task', 'section', None, 'mp'), may hold values from 0.0099487305 to 10
- key_fisher: bfloat16 [4, 4, 3584, 2048], P('task', 'section', None, 'mp'), may hold values from 0.0099487305 to 10
- value_fisher: bfloat16 [4, 4, 3584, 2048], P('task', 'section', None, 'mp'), may hold values from 0.0099487305 to 10
- output_fisher: bfloat16 [4, 4, 4096, 3584], P('task', 'section', 'mp'), may hold values from 0.0099487305 to 10
Outputs:
- hidden_out: bfloat16 [4, 4, 256, 3584], P('section', 'task', 'mp')
- losses: float32 [4, 4], P('section', 'task')
All inputs are finite; a program needn't handle non-finite values.
Results may differ from a plain program's by a relative error of at most 0.04.
Values may be sent and summed in bfloat16 or wider, within the bound.
No kernel may reach another device: no remote copies, remote signals or barrier semaphores. Data moves between devices by JAX's collectives and lax.ppermute only.
A program may use at most 128 MiB of HBM per device.

v0:
```python
import functools

import jax
import jax.numpy as jnp
from jax import lax
from jax.experimental import pallas as pl
from jax.experimental.pallas import tpu as pltpu
from jax.sharding import PartitionSpec as P

HEAD_DIM = 256
F32 = jnp.float32
BF16 = jnp.bfloat16
SMEM = pltpu.SMEM
VMEM = pltpu.VMEM
HBM = pltpu.HBM


def exchanged(array, axis, mask):
    return lax.ppermute(array, axis, [(i, i ^ mask) for i in range(lax.axis_size(axis))])


def placed(array, space):
    return pltpu.with_memory_space_constraint(array, space)


def result_on_chip(shape, dtype=BF16):
    return VMEM(shape, dtype)


def kernel_call(kernel, operands, spaces, shapes, scratch=(), mib=16):
    operands = [a if space == SMEM else placed(a, space) for a, space in zip(operands, spaces)]
    outs = pl.pallas_call(
        kernel,
        out_shape=tuple(
            result_on_chip(shape[:-1], F32) if shape[-1] is F32 else result_on_chip(shape)
            for shape in shapes
        ),
        in_specs=[pl.BlockSpec(memory_space=space) for space in spaces],
        out_specs=tuple(pl.BlockSpec(memory_space=VMEM) for _ in shapes),
        scratch_shapes=scratch,
        compiler_params=pltpu.CompilerParams(vmem_limit_bytes=mib * 1024 * 1024),
    )(*operands)
    return outs[0] if len(shapes) == 1 else outs


def share_call(plan, scale, jobs, count, finish):
    rows = jobs[0][0][2]
    total = sum(jobs[0][0][3])
    sub = rows // 2
    parts = count * 2
    strip = 64 if sub % 64 == 0 and sub > 64 else 16
    operands = [plan, scale]
    spaces = [SMEM, SMEM]
    scratch = []
    for (weights, fishers, _, widths, _), _, received in jobs:
        n = len(weights)
        operands += [*weights, *fishers, *(array for array, _ in received)]
        spaces += [HBM] * (2 * n) + [VMEM] * len(received)
        scratch += [VMEM((parts, sub, widths[k % n]), BF16) for k in range(2 * n)]
        scratch.append(pltpu.SemaphoreType.DMA((2 * n, parts)))
    shape = (len(jobs), rows, total) if finish else (2, count, rows, total)

    def kernel(plan_ref, scale_ref, *refs):
        ins = list(refs[: len(operands) - 2])
        out_ref = refs[len(operands) - 2]
        held = list(refs[len(operands) - 1 :])
        task_scale = scale_ref[0]
        work = []
        for job, ((weights, _, _, widths, cut), base, received) in enumerate(jobs):
            n = len(weights)
            arrays = [ins.pop(0) for _ in range(2 * n)]
            gots = [ins.pop(0) for _ in received]
            buffers = [held.pop(0) for _ in range(2 * n)]
            sems = held.pop(0)
            blocks = [0 if entry is None else plan_ref[entry] for _, entry in received]

            def copy(k, part, arrays=arrays, buffers=buffers, sems=sems, base=base, cut=cut):
                return pltpu.make_async_copy(
                    cut(arrays[k], plan_ref[base + part // 2], (part % 2) * sub, sub),
                    buffers[k].at[part],
                    sems.at[k, part],
                )

            for part in range(parts):
                for k in range(2 * n):
                    copy(k, part).start()
            work.append((job, n, widths, copy, buffers, gots, blocks))

        for job, n, widths, copy, buffers, gots, blocks in work:

            def one_strip(part, i):
                inside = pl.ds(pl.multiple_of(i * strip, strip), strip)
                lines = pl.ds(pl.multiple_of((part % 2) * sub + i * strip, strip), strip)
                at = 0
                for k in range(n):
                    scaled = buffers[n + k][part, inside, :].astype(F32) * task_scale
                    term = scaled * buffers[k][part, inside, :].astype(F32)
                    sums = [term.astype(BF16), scaled.astype(BF16)]
                    cols = slice(at, at + widths[k])
                    at += widths[k]
                    for got, block in zip(gots, blocks):
                        sums = [
                            v.astype(F32) + got[i, block, lines, cols].astype(F32)
                            for i, v in enumerate(sums)
                        ]
                    if finish:
                        out_ref[job, lines, cols] = (sums[0] / sums[1]).astype(BF16)
                    else:
                        out_ref[0, part // 2, lines, cols] = sums[0].astype(BF16)
                        out_ref[1, part // 2, lines, cols] = sums[1].astype(BF16)

            def one_part(part, carry):
                for k in range(2 * n):
                    copy(k, part).wait()
                lax.fori_loop(0, sub // strip, lambda i, c: (one_strip(part, i), c)[1], 0)
                return carry

            lax.fori_loop(0, parts, one_part, 0)

    return kernel_call(kernel, operands, spaces, [shape], scratch)


def dealing(idx, hidden, target):
    rows, width = hidden.shape
    half = rows // 2

    def kernel(idx_ref, h_ref, t_ref, straight_ref, crossed_ref):
        last = idx_ref[4] == 1
        for at, ref in ((0, h_ref), (half, t_ref)):
            low = ref[:half, :].astype(F32)
            high = ref[half:, :].astype(F32)
            straight_ref[at : at + half, :] = jnp.where(last, high, low).astype(BF16)
            crossed_ref[at : at + half, :] = jnp.where(last, low, high).astype(BF16)

    return kernel_call(
        kernel, [idx, hidden, target], [SMEM, VMEM, VMEM], [(rows, width), (rows, width)]
    )


def entered(idx, gain, straight, crossed, incoming, part, copies):
    rows, width = straight.shape[0] // 2, straight.shape[1]
    arrays = [straight, crossed] + ([] if incoming is None else [incoming])

    def kernel(idx_ref, gain_ref, s_ref, c_ref, *refs):
        out_ref, states_ref = refs[-2:]
        x = jnp.where(
            idx_ref[1] == part, s_ref[:rows, :].astype(F32), c_ref[:rows, :].astype(F32)
        )
        if incoming is not None:
            x = jnp.where(idx_ref[3] == 0, x, refs[0][...].astype(F32))
        scale = lax.rsqrt(jnp.mean(x * x, axis=-1, keepdims=True) + 1e-06)
        y = (x * scale * gain_ref[...]).astype(BF16)
        for k in range(copies):
            out_ref[k * rows : (k + 1) * rows, :] = y
        states_ref[...] = x.astype(BF16)

    return kernel_call(
        kernel,
        [idx, gain, *arrays],
        [SMEM, VMEM] + [VMEM] * len(arrays),
        [(copies * rows, width), (rows, width)],
    )


def left(idx, outs, straight, crossed):
    rows, width = outs[0][0].shape
    flat = [o for group in outs for o in group]

    def kernel(idx_ref, s_ref, c_ref, *refs):
        keep_ref, cross_ref, loss_ref = refs[-3:]
        core = idx_ref[1]
        length = idx_ref[2]
        section = idx_ref[3]
        mp = idx_ref[5]
        total = None
        chosen = []
        for h, group in enumerate(outs):
            ins = refs[h * len(group) : (h + 1) * len(group)]
            out = ins[0][...].astype(F32)
            for layer in range(1, len(group)):
                out = jnp.where(section == layer, ins[layer][...].astype(F32), out)
            chosen.append(out)
            target = jnp.where(
                core == h, s_ref[rows:, :].astype(F32), c_ref[rows:, :].astype(F32)
            )
            row = lax.broadcasted_iota(jnp.int32, (rows, width), 0)
            live = h * (rows * idx_ref[6]) + mp * rows + row < length
            error = jnp.where(live, (out - target) * (out - target), 0.0)
            error = jnp.sum(jnp.sum(error, axis=1, keepdims=True), axis=0, keepdims=True)
            total = error if total is None else total + error
        keep_ref[...] = jnp.where(core == 0, chosen[0], chosen[1]).astype(BF16)
        cross_ref[...] = jnp.where(core == 0, chosen[1], chosen[0]).astype(BF16)
        loss_ref[...] = jnp.broadcast_to(total[:, :, None], loss_ref.shape)

    return kernel_call(
        kernel,
        [idx, straight, crossed, *flat],
        [SMEM] + [VMEM] * (2 + len(flat)),
        [(rows, width), (rows, width), (16, 1, 128, F32)],
    )


def rejoined(idx, kept, crossed):
    rows, width = kept.shape

    def kernel(idx_ref, k_ref, c_ref, out_ref):
        last = idx_ref[4] == 1
        a = k_ref[...].astype(F32)
        b = c_ref[...].astype(F32)
        out_ref[:rows, :] = jnp.where(last, b, a).astype(BF16)
        out_ref[rows:, :] = jnp.where(last, a, b).astype(BF16)

    return kernel_call(kernel, [idx, kept, crossed], [SMEM, VMEM, VMEM], [(2 * rows, width)])


def weight(refs, d, k):
    own, near, low, high, far = refs
    if d == 2:
        return (low, high)[k][...]
    return (own, near, None, far)[d][k]


def part_of(idx_ref, step):
    return jnp.clip(step - idx_ref[3], 0, 1)


def project(idx, step, normed, own, peer, cosine, sine):
    tokens, width = normed.shape
    quarter = width // 4

    def kernel(idx_ref, x_ref, cos_ref, sin_ref, *refs):
        q_ref, kv_ref = refs[-2:]
        x_index = idx_ref[0]
        core = idx_ref[1]
        part_index = part_of(idx_ref, step)
        sums = [None] * 4
        for d in range(4):
            at = pl.multiple_of((x_index ^ d) * quarter, 128)
            part = x_ref[:, pl.ds(at, quarter)]
            for k in range(4):
                w = weight(refs[5 * (k // 2) : 5 * (k // 2) + 5], d, k % 2)
                prod = jnp.dot(part, w, preferred_element_type=F32)
                sums[k] = prod if d == 0 else sums[k] + prod
        q_mine, mine, q_theirs, theirs = sums
        cos = cos_ref[part_index]
        sin = sin_ref[part_index]
        for at, q in ((0, q_mine), (tokens, q_theirs)):
            a = q[:, :128]
            b = q[:, 128:]
            q_ref[at : at + tokens, :128] = (a * cos - b * sin).astype(BF16)
            q_ref[at : at + tokens, 128:] = (b * cos + a * sin).astype(BF16)
        first = core == 0
        k_mine = mine[:, :128].astype(BF16).astype(F32)
        k_theirs = theirs[:, :128].astype(BF16).astype(F32)
        a = jnp.where(first, k_mine, k_theirs)
        b = jnp.where(first, k_theirs, k_mine)
        kv_ref[:, :128] = (a * cos - b * sin).astype(BF16)
        kv_ref[:, 128:256] = (b * cos + a * sin).astype(BF16)
        kv_ref[:, 256:384] = jnp.where(first, mine[:, 128:], theirs[:, 128:]).astype(BF16)
        kv_ref[:, 384:] = jnp.where(first, theirs[:, 128:], mine[:, 128:]).astype(BF16)

    return kernel_call(
        kernel,
        [idx, normed, cosine, sine, *own, *peer],
        [SMEM] + [VMEM] * 13,
        [(2 * tokens, 256), (tokens, 512)],
    )


def attend(idx, step, queries, blocks, own, peer, rows):
    tokens = queries.shape[0] // 2
    quarter = own[0].shape[2]
    part_rows = 2 * tokens

    def kernel(idx_ref, q_ref, *refs):
        out_ref = refs[-1]
        kv_refs = refs[:4]
        weights = refs[4:-1]
        x_index = idx_ref[0]
        core = idx_ref[1]
        length = idx_ref[2]
        part_index = part_of(idx_ref, step)

        def positions(dim, part, which):
            i = lax.broadcasted_iota(jnp.int32, (2 * tokens, tokens), dim) % tokens
            return part * part_rows + (i // rows) * (2 * rows) + which * rows + i % rows

        q_pos = positions(0, part_index, core)
        q = q_ref[...]
        numerators = []
        total = None
        for n, kv_ref in enumerate(kv_refs):
            k_pos = positions(1, part_index - 1 + n // 2, core if n % 2 == 0 else 1 - core)
            allowed = (k_pos <= q_pos) & (k_pos < length) & (k_pos >= 0)
            scores = lax.dot_general(
                q,
                kv_ref[:, :256],
                (((1,), (1,)), ((), ())),
                preferred_element_type=F32,
            ) * HEAD_DIM ** (-0.5)
            capped = 50.0 * jnp.tanh(scores / 50.0)
            numerators.append(jnp.where(allowed, jnp.exp(capped), 0.0))
            added = jnp.sum(numerators[-1], axis=-1, keepdims=True)
            total = added if total is None else total + added
        context = None
        for num, kv_ref in zip(numerators, kv_refs):
            prod = jnp.dot(
                (num / total).astype(BF16), kv_ref[:, 256:], preferred_element_type=F32
            )
            context = prod if context is None else context + prod
        context = context.astype(BF16)
        lefts = [
            context[c * tokens : (c + 1) * tokens, h * 128 : (h + 1) * 128]
            for c in range(2)
            for h in range(2)
        ]
        for d in range(4):
            out = None
            for k in range(4):
                w = weight(weights[5 * (k // 2) : 5 * (k // 2) + 5], d, k % 2)
                prod = jnp.dot(lefts[k], w, preferred_element_type=F32)
                out = prod if out is None else out + prod
            at = pl.multiple_of((x_index ^ d) * quarter, 128)
            out_ref[:, pl.ds(at, quarter)] = out.astype(BF16)

    return kernel_call(
        kernel,
        [idx, queries, *blocks, *own, *peer],
        [SMEM] + [VMEM] * 15,
        [(tokens, 4 * quarter)],
    )


def normed_copies(states, gain, copies):
    rows, width = states.shape

    def kernel(states_ref, gain_ref, out_ref):
        x = states_ref[...].astype(F32)
        scale = lax.rsqrt(jnp.mean(x * x, axis=-1, keepdims=True) + 1e-06)
        y = (x * scale * gain_ref[...]).astype(BF16)
        for k in range(copies):
            out_ref[k * rows : (k + 1) * rows, :] = y

    return kernel_call(kernel, [states, gain], [VMEM] * 2, [(copies * rows, width)])


def finished(pieces, states, gain):
    rows, width = states.shape
    copies = pieces.shape[0] // rows

    def kernel(p_ref, states_ref, gain_ref, out_ref):
        total = p_ref[:rows, :].astype(F32)
        for k in range(1, copies):
            total = total + p_ref[k * rows : (k + 1) * rows, :].astype(F32)
        scale = lax.rsqrt(jnp.mean(total * total, axis=-1, keepdims=True) + 1e-06)
        out = states_ref[...].astype(F32) + total * scale * gain_ref[...]
        out_ref[...] = out.astype(BF16)

    return kernel_call(kernel, [pieces, states, gain], [VMEM] * 3, [states.shape])


NEAR, FAR = 1, 3


def first_halves(plan, scale, sources):
    sent = [share_call(plan, scale, [(s, 8 * i, ())], 2, False) for i, s in enumerate(sources)]
    return sent, [exchanged(s, "task", (NEAR, FAR)[i]) for i, s in enumerate(sent)]


def second_halves(plan, scale, sources, got):
    sent = [
        share_call(plan, scale, [(s, 8 * i + 2, ((got[i], 8 * i + 3),))], 1, False)
        for i, s in enumerate(sources)
    ]
    return sent, [exchanged(s, "task", (FAR, NEAR)[i]) for i, s in enumerate(sent)]


def shares(plan, scale, sources, got, more):
    jobs = [
        (s, 8 * i + 4, ((got[i], 8 * i + 5), (more[i], None))) for i, s in enumerate(sources)
    ]
    return share_call(plan, scale, jobs, 1, True)


def neighbours(own):
    return exchanged(own, "task", NEAR), exchanged(own, "task", FAR)


def completed(own, near, far):
    return own, near, exchanged(far[0], "task", NEAR), exchanged(near[1], "task", FAR), far


def of_partner(pieces):
    return tuple(exchanged(p, "mp", 1) for p in pieces)


def per_device(
    hidden_in,
    lengths,
    layer_targets,
    task_weights,
    norm_gains,
    query_weight,
    key_weight,
    value_weight,
    output_weight,
    query_fisher,
    key_fisher,
    value_fisher,
    output_fisher,
):
    x_index = lax.axis_index("task")
    mp_index = lax.axis_index("mp")
    section_index = lax.axis_index("section")
    core = mp_index % 2
    chips = lax.axis_size("mp") // 2
    groups = [[2 * z + c for z in range(chips)] for c in range(2)]
    sections = lax.axis_size("section")
    width = hidden_in.shape[2]
    parts = 2
    rows = hidden_in.shape[1] // parts
    length = lengths[0]
    pre_gain = norm_gains[0, 0:1]
    post_gain = norm_gains[0, 1:2]
    scale = lax.dynamic_slice_in_dim(task_weights, x_index, 1)

    b = x_index // 2
    a = (x_index % 2) ^ b

    def block_a(h1, h2):
        return jnp.where(h1 == 0, 3 * h2, 1 + h2)

    def block_b(h1, h2):
        return jnp.where(h1 == 0, h2, 3 - h2)

    zero = jnp.zeros_like(a)
    plan = jnp.stack(
        [
            block_a(1 - a, 0),
            block_a(1 - a, 1),
            block_a(a, 1 - b),
            1 - b,
            x_index,
            b,
            zero,
            zero,
            block_b(1 - b, 0),
            block_b(1 - b, 1),
            block_b(b, 1 - a),
            1 - a,
            x_index,
            a,
            zero,
            zero,
        ]
    ).astype(jnp.int32)
    scalars = jnp.stack(
        [x_index, core, length, section_index, mp_index // chips, mp_index, 2 * chips]
    ).astype(jnp.int32)

    def quarters(array):
        array = array[0, 0]
        return array.reshape(4, array.shape[0] // 4, array.shape[1])

    def cut_rows(ref, block, row, sub):
        return ref.at[block, pl.ds(row, sub), :]

    def cut_columns(start):
        def cut(ref, block, row, sub):
            at = pl.multiple_of(block * (width // 4), 128)
            return ref.at[pl.ds(start + row, sub), pl.ds(at, width // 4)]

        return cut

    qkv_sources = (
        ((quarters(query_weight),), (quarters(query_fisher),), width // 4, (256,), cut_rows),
        (
            (quarters(key_weight), quarters(value_weight)),
            (quarters(key_fisher), quarters(value_fisher)),
            width // 4,
            (128, 128),
            cut_rows,
        ),
    )
    out_sources = tuple(
        (
            (output_weight[0, 0],),
            (output_fisher[0, 0],),
            128,
            (width // 4,),
            cut_columns(start),
        )
        for start in (0, 128)
    )

    part_rows = 2 * rows * chips
    positions = (
        part_rows * jnp.arange(parts, dtype=jnp.int32)[:, None, None]
        + 2 * rows * jnp.arange(chips, dtype=jnp.int32)[None, :, None]
        + core * rows
        + jnp.arange(rows, dtype=jnp.int32)[None, None, :]
    ).reshape(parts, -1)
    frequency = 10000.0 ** (-2.0 * jnp.arange(HEAD_DIM // 2, dtype=F32) / HEAD_DIM)
    angles = positions.astype(F32)[:, :, None] * frequency[None, None, :]
    cosine = jnp.cos(angles)
    sine = jnp.sin(angles)

    def spread(array):
        pieces = array.reshape(chips, rows, width)
        moved = lax.all_to_all(pieces, "mp", 0, 0, tiled=True, axis_index_groups=groups)
        return moved.reshape(chips * rows, width)

    straight = [(m, 2 * m) for m in range(chips)]
    straight += [(m, 2 * (m - chips) + 1) for m in range(chips, 2 * chips)]
    crossed = [(m, 2 * m + 1) for m in range(chips)]
    crossed += [(m, 2 * (m - chips)) for m in range(chips, 2 * chips)]

    def over_mp(array, pairs):
        return lax.ppermute(array, "mp", pairs)

    def projected(t, normed):
        queries, kv = project(scalars, t, normed, qkv_own, qkv_peer, cosine, sine)
        return queries, (kv, exchanged(kv, "mp", 1))

    with jax.named_scope("merge"):
        _, qkv_got = first_halves(plan, scale, qkv_sources)
        one, other = dealing(scalars, hidden_in[0], layer_targets[0, 0])
        one, other = over_mp(one, straight), over_mp(other, crossed)
        out_sent, out_got = first_halves(plan, scale, out_sources)
        first, states = entered(scalars, pre_gain, one, other, None, 0, chips)
        first, cosine, sine, _ = lax.optimization_barrier((first, cosine, sine, out_sent))
        first = spread(first)
        qkv_got, first = lax.optimization_barrier((qkv_got, first))
        qkv_sent, qkv_more = second_halves(plan, scale, qkv_sources, qkv_got)
        out_got, _ = lax.optimization_barrier((out_got, qkv_sent))
        out_sent, out_more = second_halves(plan, scale, out_sources, out_got)
        qkv_share = shares(plan, scale, qkv_sources, qkv_got, qkv_more)
        out_more, _ = lax.optimization_barrier((out_more, qkv_share))
        out_share = shares(plan, scale, out_sources, out_got, out_more)
        qkv_first = neighbours(qkv_share)
        qkv_first, _ = lax.optimization_barrier((qkv_first, out_share))
        qkv_own = completed(qkv_share, *qkv_first)
        qkv_peer = of_partner(qkv_own)
        out_first = neighbours(out_share)
    with jax.named_scope("layer"):
        queries, kv = projected(0, first)
    with jax.named_scope("merge"):
        out_own = completed(out_share, *out_first)
        out_peer = of_partner(out_own)

    outs = []
    before = kv
    for t in range(sections + parts - 1):
        with jax.named_scope("layer"):
            if t > 0:
                incoming = lax.ppermute(
                    outs[-1], "section", [(i, i + 1) for i in range(sections - 1)]
                )
                if t < parts:
                    normed, states = entered(scalars, pre_gain, one, other, incoming, t, chips)
                else:
                    normed, states = normed_copies(incoming, pre_gain, chips), incoming
                before = kv
                queries, kv = projected(t, spread(normed))
            partial = attend(scalars, t, queries, (*before, *kv), out_own, out_peer, rows)
            outs.append(finished(spread(partial), states, post_gain))
    with jax.named_scope("loss"):
        kept, moved, error = left(
            scalars, [outs[h : h + sections] for h in range(parts)], one, other
        )
        error = lax.all_to_all(error, "mp", 0, 0, tiled=True)
        kept = over_mp(kept, [(j, i) for i, j in straight])
        moved = over_mp(moved, [(j, i) for i, j in crossed])
        outputs = rejoined(scalars, kept, moved)
        loss = jnp.sum(error[:, 0, 0]) / (length.astype(F32) * width)
    return (outputs[None, None], loss[None, None])


def solution(mesh):
    in_specs = (
        P("task", "mp", None),
        P("task"),
        P("section", "task", "mp", None),
        P(),
        P("section", None, None),
        P("task", "section", None, "mp"),
        P("task", "section", None, "mp"),
        P("task", "section", None, "mp"),
        P("task", "section", "mp", None),
        P("task", "section", None, "mp"),
        P("task", "section", None, "mp"),
        P("task", "section", None, "mp"),
        P("task", "section", "mp", None),
    )
    out_specs = (P("section", "task", "mp", None), P("section", "task"))
    return jax.shard_map(
        per_device, mesh=mesh, in_specs=in_specs, out_specs=out_specs, check_vma=False
    )
```

profile of v0, /device:TPU:1, one launch (start us, length us, event | category | flops | bytes accessed | tf_op | source)
XLA Modules:
  0.0 416.4 jit_solution(2741817960430619725)
XLA Ops:
  3.8 4.9 %collective-permute-start = (bf16[16,3584]{1,0:T(8,128)(2,1)S(1)}, bf16[16,3584]{1,0:T(8,128)(2,1)S(1)}, u32[]{:S(2)}, u32[]{:S(2)}) collective-permute-start(bf16[16,3584]{1,0:T(8,128)(2,1)S(1)} %get-tuple-element.33), channel_id=1, source_target_pairs={{0,0},{1,2},{2,4},{3,6},{4,8},{5,10},{6,12},{7,14},{8,1},{9,3},{10... | collective-permute-start | bytes 344072 | tf_op jit(solution)/shard_map/merge/ppermute | solution.py:519
  13.2 4.1 merge.13
  18.6 4.2 %merge.14 = bf16[2,2,896,256]{3,2,1,0:T(8,128)(2,1)} custom-call(s32[16]{0:T(128)S(1)} %stack.69.plan_ref, f32[1]{0:T(128)} %dynamic_slice.3.scale_ref, bf16[4,896,128]{2,1,0:T(8,128)(2,1)} %bitcast.100, bf16[4,896,128]{2,1,0:T(8,128)(2,1)} %bitcast.103, bf16[4,896,128]{2,1,0:T(8,128)(2,1)} %bitcast.106, bf16[4,896,128]{2,1,0:T(8,128)(2,1)} %bitcast.109), custom_call_target="tpu_custom_call" | custom-call | tf_op jit(solution)/shard_map/merge/pallas_call | solution.py:32
  34.1 7.4 %all-to-all-start = ((bf16[8,8,3584]{2,1,0:T(8,128)(2,1)}), bf16[8,8,3584]{2,1,0:T(8,128)(2,1)S(1)}, u32[]{:S(2)}, u32[]{:S(2)}) async-start(bf16[8,8,3584]{2,1,0:T(8,128)(2,1)} %bitcast.26), calls=%async_computation | async-start | bytes 917504 | tf_op jit(solution)/shard_map/merge/all_to_all | solution.py:510
  42.5 14.3 %all-to-all-done = bf16[8,8,3584]{2,1,0:T(8,128)(2,1)S(1)} async-done(((bf16[8,8,3584]{2,1,0:T(8,128)(2,1)}), bf16[8,8,3584]{2,1,0:T(8,128)(2,1)S(1)}, u32[]{:S(2)}, u32[]{:S(2)}) %all-to-all-start) | async-done | bytes 458784 | tf_op jit(solution)/shard_map/merge/all_to_all | solution.py:510
  59.8 6.8 %collective-permute-done.3.refs_4_.refs_8_ = bf16[2,2,896,256]{3,2,1,0:T(8,128)(2,1)} collective-permute-done((bf16[2,2,896,256]{3,2,1,0:T(8,128)(2,1)}, bf16[2,2,896,256]{3,2,1,0:T(8,128)(2,1)}, u32[]{:S(2)}, u32[]{:S(2)}) %collective-permute-start.3) | collective-permute-done | bytes 1835040 | tf_op jit(solution)/shard_map/merge/ppermute | solution.py:19
  69.3 3.8 merge.19
  75.1 4.4 %collective-permute-done.8.refs_2_ = bf16[2,2,128,896]{3,2,1,0:T(8,128)(2,1)S(1)} collective-permute-done((bf16[2,2,128,896]{3,2,1,0:T(8,128)(2,1)}, bf16[2,2,128,896]{3,2,1,0:T(8,128)(2,1)S(1)}, u32[]{:S(2)}, u32[]{:S(2)}) %collective-permute-start.8) | collective-permute-done | bytes 917536 | tf_op jit(solution)/shard_map/merge/ppermute | solution.py:19
  79.5 6.7 %collective-permute-done.9.refs_2_.refs_6_ = bf16[2,2,128,896]{3,2,1,0:T(8,128)(2,1)} collective-permute-done((bf16[2,2,128,896]{3,2,1,0:T(8,128)(2,1)}, bf16[2,2,128,896]{3,2,1,0:T(8,128)(2,1)}, u32[]{:S(2)}, u32[]{:S(2)}) %collective-permute-start.9) | collective-permute-done | bytes 917536 | tf_op jit(solution)/shard_map/merge/ppermute | solution.py:19
  93.6 5.4 %collective-permute-done.5.refs_9_ = bf16[2,1,896,256]{3,2,1,0:T(8,128)(2,1)S(1)} collective-permute-done((bf16[2,1,896,256]{3,2,1,0:T(8,128)(2,1)S(1)}, bf16[2,1,896,256]{3,2,1,0:T(8,128)(2,1)S(1)}, u32[]{:S(2)}, u32[]{:S(2)}) %collective-permute-start.5) | collective-permute-done | bytes 917536 | tf_op jit(solution)/shard_map/merge/ppermute | solution.py:19
  99.0 6.8 %collective-permute-done.4.refs_3_ = bf16[2,1,896,256]{3,2,1,0:T(8,128)(2,1)S(1)} collective-permute-done((bf16[2,1,896,256]{3,2,1,0:T(8,128)(2,1)S(1)}, bf16[2,1,896,256]{3,2,1,0:T(8,128)(2,1)S(1)}, u32[]{:S(2)}, u32[]{:S(2)}) %collective-permute-start.4) | collective-permute-done | bytes 917536 | tf_op jit(solution)/shard_map/merge/ppermute | solution.py:19
  105.8 5.0 %merge.20.refs_0_ = bf16[2,896,256]{2,1,0:T(8,128)(2,1)S(1)} custom-call(s32[16]{0:T(128)S(1)} %stack.69.plan_ref, f32[1]{0:T(128)} %dynamic_slice.3.scale_ref, bf16[4,896,256]{2,1,0:T(8,128)(2,1)} %bitcast.96, bf16[4,896,256]{2,1,0:T(8,128)(2,1)} %bitcast.99, bf16[2,2,896,256]{3,2,1,0:T(8,128)(2,1)S(1)} %collective-permute-done.2.refs_2_, ...), custom_call_target="tpu_custom_call" | custom-call | tf_op jit(solution)/shard_map/merge/pallas_call | solution.py:32
  113.5 3.6 merge.23.refs_4_
  121.4 9.5 %collective-permute-done.21.refs_8_ = bf16[2,128,896]{2,1,0:T(8,128)(2,1)S(1)} collective-permute-done((bf16[2,128,896]{2,1,0:T(8,128)(2,1)S(1)}, bf16[2,128,896]{2,1,0:T(8,128)(2,1)S(1)}, u32[]{:S(2)}, u32[]{:S(2)}) %collective-permute-start.21) | collective-permute-done | bytes 458784 | tf_op jit(solution)/shard_map/merge/ppermute | solution.py:19
  131.1 21.1 %collective-permute-done.20.refs_5_ = bf16[2,128,896]{2,1,0:T(8,128)(2,1)S(1)} collective-permute-done((bf16[2,128,896]{2,1,0:T(8,128)(2,1)S(1)}, bf16[2,128,896]{2,1,0:T(8,128)(2,1)S(1)}, u32[]{:S(2)}, u32[]{:S(2)}) %collective-permute-start.20) | collective-permute-done | bytes 458784 | tf_op jit(solution)/shard_map/merge/ppermute | solution.py:19
  157.0 3.5 collective-permute-done.23.refs_7_
  162.3 6.5 %collective-permute-done.12.refs_2_ = bf16[896,256]{1,0:T(8,128)(2,1)S(1)} collective-permute-done((bf16[896,256]{1,0:T(8,128)(2,1)S(1)}, bf16[896,256]{1,0:T(8,128)(2,1)S(1)}, u32[]{:S(2)}, u32[]{:S(2)}) %collective-permute-start.12) | collective-permute-done | bytes 458784 | tf_op jit(solution)/shard_map/merge/ppermute | solution.py:19
  181.6 22.1 %all_to_all.55 = bf16[8,8,3584]{2,1,0:T(8,128)(2,1)S(1)} all-to-all(bf16[8,8,3584]{2,1,0:T(8,128)(2,1)S(1)} %bitcast.65), channel_id=1, replica_groups={{0,2,4,6,8,10,12,14},{1,3,5,7,9,11,13,15},{16,18,20,22,24,26,28,30},{17..., dimensions={0} | all-to-all | bytes 917504 | tf_op jit(solution)/shard_map/layer/all_to_all | solution.py:510
  204.0 3.2 collective-permute-start.29
  209.1 16.5 %all_to_all.56 = bf16[8,8,3584]{2,1,0:T(8,128)(2,1)S(1)} all-to-all(bf16[8,8,3584]{2,1,0:T(8,128)(2,1)S(1)} %bitcast.79), channel_id=1, replica_groups={{0,2,4,6,8,10,12,14},{1,3,5,7,9,11,13,15},{16,18,20,22,24,26,28,30},{17..., dimensions={0} | all-to-all | bytes 917504 | tf_op jit(solution)/shard_map/layer/all_to_all | solution.py:510
  233.4 19.0 %all_to_all.57 = bf16[8,8,3584]{2,1,0:T(8,128)(2,1)S(1)} all-to-all(bf16[8,8,3584]{2,1,0:T(8,128)(2,1)S(1)} %bitcast.62), channel_id=1, replica_groups={{0,2,4,6,8,10,12,14},{1,3,5,7,9,11,13,15},{16,18,20,22,24,26,28,30},{17..., dimensions={0} | all-to-all | bytes 917504 | tf_op jit(solution)/shard_map/layer/all_to_all | solution.py:510
  252.5 3.7 collective-permute-start.31
  257.6 16.6 %all_to_all.58 = bf16[8,8,3584]{2,1,0:T(8,128)(2,1)S(1)} all-to-all(bf16[8,8,3584]{2,1,0:T(8,128)(2,1)S(1)} %bitcast.72), channel_id=1, replica_groups={{0,2,4,6,8,10,12,14},{1,3,5,7,9,11,13,15},{16,18,20,22,24,26,28,30},{17..., dimensions={0} | all-to-all | bytes 917504 | tf_op jit(solution)/shard_map/layer/all_to_all | solution.py:510
  282.1 19.0 %all_to_all.59 = bf16[8,8,3584]{2,1,0:T(8,128)(2,1)S(1)} all-to-all(bf16[8,8,3584]{2,1,0:T(8,128)(2,1)S(1)} %bitcast.63), channel_id=1, replica_groups={{0,2,4,6,8,10,12,14},{1,3,5,7,9,11,13,15},{16,18,20,22,24,26,28,30},{17..., dimensions={0} | all-to-all | bytes 917504 | tf_op jit(solution)/shard_map/layer/all_to_all | solution.py:510
  301.3 3.7 collective-permute-start.33
  306.4 16.6 %all_to_all.60 = bf16[8,8,3584]{2,1,0:T(8,128)(2,1)S(1)} all-to-all(bf16[8,8,3584]{2,1,0:T(8,128)(2,1)S(1)} %bitcast.73), channel_id=1, replica_groups={{0,2,4,6,8,10,12,14},{1,3,5,7,9,11,13,15},{16,18,20,22,24,26,28,30},{17..., dimensions={0} | all-to-all | bytes 917504 | tf_op jit(solution)/shard_map/layer/all_to_all | solution.py:510
  330.6 19.0 %all_to_all.61 = bf16[8,8,3584]{2,1,0:T(8,128)(2,1)S(1)} all-to-all(bf16[8,8,3584]{2,1,0:T(8,128)(2,1)S(1)} %bitcast.64), channel_id=1, replica_groups={{0,2,4,6,8,10,12,14},{1,3,5,7,9,11,13,15},{16,18,20,22,24,26,28,30},{17..., dimensions={0} | all-to-all | bytes 917504 | tf_op jit(solution)/shard_map/layer/all_to_all | solution.py:510
  349.8 3.7 collective-permute-start.35
  354.9 16.6 %all_to_all.62 = bf16[8,8,3584]{2,1,0:T(8,128)(2,1)S(1)} all-to-all(bf16[8,8,3584]{2,1,0:T(8,128)(2,1)S(1)} %bitcast.71), channel_id=1, replica_groups={{0,2,4,6,8,10,12,14},{1,3,5,7,9,11,13,15},{16,18,20,22,24,26,28,30},{17..., dimensions={0} | all-to-all | bytes 917504 | tf_op jit(solution)/shard_map/layer/all_to_all | solution.py:510
  379.2 19.0 %all_to_all.63 = bf16[8,8,3584]{2,1,0:T(8,128)(2,1)S(1)} all-to-all(bf16[8,8,3584]{2,1,0:T(8,128)(2,1)S(1)} %bitcast.61), channel_id=1, replica_groups={{0,2,4,6,8,10,12,14},{1,3,5,7,9,11,13,15},{16,18,20,22,24,26,28,30},{17..., dimensions={0} | all-to-all | bytes 917504 | tf_op jit(solution)/shard_map/layer/all_to_all | solution.py:510
  399.7 3.7 all-to-all-start.10
  403.4 7.5 %collective-permute-start.37 = (bf16[8,3584]{1,0:T(8,128)(2,1)S(1)}, bf16[8,3584]{1,0:T(8,128)(2,1)S(1)}, u32[]{:S(2)}, u32[]{:S(2)}) collective-permute-start(bf16[8,3584]{1,0:T(8,128)(2,1)S(1)} %get-tuple-element.61), channel_id=1, source_target_pairs={{0,0},{2,1},{4,2},{6,3},{8,4},{10,5},{12,6},{14,7},{1,8},{3,9},{5,... | collective-permute-start | bytes 172040 | tf_op jit(solution)/shard_map/loss/ppermute | solution.py:519
  (127 shorter events, 105.0 us)
Async XLA Ops:
  3.8 28.8 %collective-permute-start = (bf16[16,3584]{1,0:T(8,128)(2,1)S(1)}, bf16[16,3584]{1,0:T(8,128)(2,1)S(1)}, u32[]{:S(2)}, u32[]{:S(2)}) collective-permute-start(bf16[16,3584]{1,0:T(8,128)(2,1)S(1)} %get-tuple-element.33), channel_id=1, source_target_pairs={{0,0},{1,2},{2,4},{3,6},{4,8},{5,10},{6,12},{7,14},{8,1},{9,3},{10... | collective-permute-start | bytes 344072 | tf_op jit(solution)/shard_map/merge/ppermute | solution.py:519
  8.7 23.9 %collective-permute-start.1 = (bf16[16,3584]{1,0:T(8,128)(2,1)S(1)}, bf16[16,3584]{1,0:T(8,128)(2,1)S(1)}, u32[]{:S(2)}, u32[]{:S(2)}) collective-permute-start(bf16[16,3584]{1,0:T(8,128)(2,1)S(1)} %get-tuple-element.34), channel_id=1, source_target_pairs={{0,1},{1,3},{2,5},{3,7},{4,9},{5,11},{6,13},{7,15},{8,0},{9,2},{10... | collective-permute-start | bytes 344072 | tf_op jit(solution)/shard_map/merge/ppermute | solution.py:519
  17.3 42.5 %collective-permute-start.2 = (bf16[2,2,896,256]{3,2,1,0:T(8,128)(2,1)}, bf16[2,2,896,256]{3,2,1,0:T(8,128)(2,1)S(1)}, u32[]{:S(2)}, u32[]{:S(2)}) collective-permute-start(bf16[2,2,896,256]{3,2,1,0:T(8,128)(2,1)} %merge.13), channel_id=1, source_target_pairs={{0,16},{16,0},{32,48},{48,32},{1,17},{17,1},{33,49},{49,33},{2,18}... | collective-permute-start | bytes 5505032 | tf_op jit(solution)/shard_map/merge/ppermute | solution.py:19
  22.9 43.7 %collective-permute-start.3 = (bf16[2,2,896,256]{3,2,1,0:T(8,128)(2,1)}, bf16[2,2,896,256]{3,2,1,0:T(8,128)(2,1)}, u32[]{:S(2)}, u32[]{:S(2)}) collective-permute-start(bf16[2,2,896,256]{3,2,1,0:T(8,128)(2,1)} %merge.14), channel_id=1, source_target_pairs={{0,48},{16,32},{32,16},{48,0},{1,49},{17,33},{33,17},{49,1},{2,50}... | collective-permute-start | bytes 5505032 | tf_op jit(solution)/shard_map/merge/ppermute | solution.py:19
  34.1 22.7 %all-to-all-start = ((bf16[8,8,3584]{2,1,0:T(8,128)(2,1)}), bf16[8,8,3584]{2,1,0:T(8,128)(2,1)S(1)}, u32[]{:S(2)}, u32[]{:S(2)}) async-start(bf16[8,8,3584]{2,1,0:T(8,128)(2,1)} %bitcast.26), calls=%async_computation | async-start | bytes 917504 | tf_op jit(solution)/shard_map/merge/all_to_all | solution.py:510
  41.5 37.9 %collective-permute-start.8 = (bf16[2,2,128,896]{3,2,1,0:T(8,128)(2,1)}, bf16[2,2,128,896]{3,2,1,0:T(8,128)(2,1)S(1)}, u32[]{:S(2)}, u32[]{:S(2)}) collective-permute-start(bf16[2,2,128,896]{3,2,1,0:T(8,128)(2,1)} %copy-done.3), channel_id=1, source_target_pairs={{0,16},{16,0},{32,48},{48,32},{1,17},{17,1},{33,49},{49,33},{2,18}... | collective-permute-start | bytes 2752520 | tf_op jit(solution)/shard_map/merge/ppermute | solution.py:19
  41.8 44.3 %collective-permute-start.9 = (bf16[2,2,128,896]{3,2,1,0:T(8,128)(2,1)}, bf16[2,2,128,896]{3,2,1,0:T(8,128)(2,1)}, u32[]{:S(2)}, u32[]{:S(2)}) collective-permute-start(bf16[2,2,128,896]{3,2,1,0:T(8,128)(2,1)} %copy-done.2), channel_id=1, source_target_pairs={{0,48},{16,32},{32,16},{48,0},{1,49},{17,33},{33,17},{49,1},{2,50}... | collective-permute-start | bytes 2752520 | tf_op jit(solution)/shard_map/merge/ppermute | solution.py:19
  73.1 25.9 %collective-permute-start.5 = (bf16[2,1,896,256]{3,2,1,0:T(8,128)(2,1)S(1)}, bf16[2,1,896,256]{3,2,1,0:T(8,128)(2,1)S(1)}, u32[]{:S(2)}, u32[]{:S(2)}) collective-permute-start(bf16[2,1,896,256]{3,2,1,0:T(8,128)(2,1)S(1)} %merge.19), channel_id=1, source_target_pairs={{0,16},{16,0},{32,48},{48,32},{1,17},{17,1},{33,49},{49,33},{2,18}... | collective-permute-start | bytes 2752520 | tf_op jit(solution)/shard_map/merge/ppermute | solution.py:19
  73.2 32.6 %collective-permute-start.4 = (bf16[2,1,896,256]{3,2,1,0:T(8,128)(2,1)S(1)}, bf16[2,1,896,256]{3,2,1,0:T(8,128)(2,1)S(1)}, u32[]{:S(2)}, u32[]{:S(2)}) collective-permute-start(bf16[2,1,896,256]{3,2,1,0:T(8,128)(2,1)S(1)} %merge.18), channel_id=1, source_target_pairs={{0,48},{16,32},{32,16},{48,0},{1,49},{17,33},{33,17},{49,1},{2,50}... | collective-permute-start | bytes 2752520 | tf_op jit(solution)/shard_map/merge/ppermute | solution.py:19
  91.6 19.2 %collective-permute-start.11 = (bf16[2,1,128,896]{3,2,1,0:T(8,128)(2,1)S(1)}, bf16[2,1,128,896]{3,2,1,0:T(8,128)(2,1)S(1)}, u32[]{:S(2)}, u32[]{:S(2)}) collective-permute-start(bf16[2,1,128,896]{3,2,1,0:T(8,128)(2,1)S(1)} %merge.22), channel_id=1, source_target_pairs={{0,16},{16,0},{32,48},{48,32},{1,17},{17,1},{33,49},{49,33},{2,18}... | collective-permute-start | bytes 1376264 | tf_op jit(solution)/shard_map/merge/ppermute | solution.py:19
  91.7 21.8 %collective-permute-start.10 = (bf16[2,1,128,896]{3,2,1,0:T(8,128)(2,1)S(1)}, bf16[2,1,128,896]{3,2,1,0:T(8,128)(2,1)S(1)}, u32[]{:S(2)}, u32[]{:S(2)}) collective-permute-start(bf16[2,1,128,896]{3,2,1,0:T(8,128)(2,1)S(1)} %merge.21), channel_id=1, source_target_pairs={{0,48},{16,32},{32,16},{48,0},{1,49},{17,33},{33,17},{49,1},{2,50}... | collective-permute-start | bytes 1376264 | tf_op jit(solution)/shard_map/merge/ppermute | solution.py:19
  117.2 13.8 %collective-permute-start.21 = (bf16[2,128,896]{2,1,0:T(8,128)(2,1)S(1)}, bf16[2,128,896]{2,1,0:T(8,128)(2,1)S(1)}, u32[]{:S(2)}, u32[]{:S(2)}) collective-permute-start(bf16[2,128,896]{2,1,0:T(8,128)(2,1)S(1)} %merge.23.refs_4_), channel_id=1, source_target_pairs={{0,48},{16,32},{32,16},{48,0},{1,49},{17,33},{33,17},{49,1},{2,50}... | collective-permute-start | bytes 1376264 | tf_op jit(solution)/shard_map/merge/ppermute | solution.py:19
  119.1 35.0 %collective-permute-start.7 = (bf16[2,896,256]{2,1,0:T(8,128)(2,1)S(1)}, bf16[2,896,256]{2,1,0:T(8,128)(2,1)S(1)}, u32[]{:S(2)}, u32[]{:S(2)}) collective-permute-start(bf16[2,896,256]{2,1,0:T(8,128)(2,1)S(1)} %merge.20.refs_0_), channel_id=1, source_target_pairs={{0,48},{16,32},{32,16},{48,0},{1,49},{17,33},{33,17},{49,1},{2,50}... | collective-permute-start | bytes 2752520 | tf_op jit(solution)/shard_map/merge/ppermute | solution.py:19
  119.9 34.1 %collective-permute-start.6 = (bf16[2,896,256]{2,1,0:T(8,128)(2,1)S(1)}, bf16[2,896,256]{2,1,0:T(8,128)(2,1)S(1)}, u32[]{:S(2)}, u32[]{:S(2)}) collective-permute-start(bf16[2,896,256]{2,1,0:T(8,128)(2,1)S(1)} %merge.20.refs_0_), channel_id=1, source_target_pairs={{0,16},{16,0},{32,48},{48,32},{1,17},{17,1},{33,49},{49,33},{2,18}... | collective-permute-start | bytes 2752520 | tf_op jit(solution)/shard_map/merge/ppermute | solution.py:19
  119.9 32.2 %collective-permute-start.20 = (bf16[2,128,896]{2,1,0:T(8,128)(2,1)S(1)}, bf16[2,128,896]{2,1,0:T(8,128)(2,1)S(1)}, u32[]{:S(2)}, u32[]{:S(2)}) collective-permute-start(bf16[2,128,896]{2,1,0:T(8,128)(2,1)S(1)} %merge.23.refs_4_), channel_id=1, source_target_pairs={{0,16},{16,0},{32,48},{48,32},{1,17},{17,1},{33,49},{49,33},{2,18}... | collective-permute-start | bytes 1376264 | tf_op jit(solution)/shard_map/merge/ppermute | solution.py:19
  121.4 53.2 %collective-permute-start.14 = (bf16[2,896,256]{2,1,0:T(8,128)(2,1)S(1)}, bf16[2,896,256]{2,1,0:T(8,128)(2,1)S(1)}, u32[]{:S(2)}, u32[]{:S(2)}) collective-permute-start(bf16[2,896,256]{2,1,0:T(8,128)(2,1)S(1)} %merge.20.refs_0_), channel_id=1, source_target_pairs={{0,1},{1,0},{2,3},{3,2},{4,5},{5,4},{6,7},{7,6},{8,9},{9,8},{10,11... | collective-permute-start | bytes 2752520 | tf_op jit(solution)/shard_map/merge/ppermute | solution.py:19
  131.0 26.0 %collective-permute-start.22 = (bf16[128,896]{1,0:T(8,128)(2,1)S(1)}, bf16[128,896]{1,0:T(8,128)(2,1)S(1)}, u32[]{:S(2)}, u32[]{:S(2)}) collective-permute-start(bf16[128,896]{1,0:T(8,128)(2,1)S(1)} %slice_bitcast_fusion.3), channel_id=1, source_target_pairs={{0,16},{16,0},{32,48},{48,32},{1,17},{17,1},{33,49},{49,33},{2,18}... | collective-permute-start | bytes 688136 | tf_op jit(solution)/shard_map/merge/ppermute | solution.py:19
  152.2 8.3 %collective-permute-start.23 = (bf16[128,896]{1,0:T(8,128)(2,1)S(1)}, bf16[128,896]{1,0:T(8,128)(2,1)S(1)}, u32[]{:S(2)}, u32[]{:S(2)}) collective-permute-start(bf16[128,896]{1,0:T(8,128)(2,1)S(1)} %slice_bitcast_fusion.2), channel_id=1, source_target_pairs={{0,48},{16,32},{32,16},{48,0},{1,49},{17,33},{33,17},{49,1},{2,50}... | collective-permute-start | bytes 688136 | tf_op jit(solution)/shard_map/merge/ppermute | solution.py:19
  154.1 20.5 %collective-permute-start.15 = (bf16[2,896,256]{2,1,0:T(8,128)(2,1)S(1)}, bf16[2,896,256]{2,1,0:T(8,128)(2,1)S(1)}, u32[]{:S(2)}, u32[]{:S(2)}) collective-permute-start(bf16[2,896,256]{2,1,0:T(8,128)(2,1)S(1)} %collective-permute-done.6.refs_1_), channel_id=1, source_target_pairs={{0,1},{1,0},{2,3},{3,2},{4,5},{5,4},{6,7},{7,6},{8,9},{9,8},{10,11... | collective-permute-start | bytes 2752520 | tf_op jit(solution)/shard_map/merge/ppermute | solution.py:19
  154.7 20.4 %collective-permute-start.18 = (bf16[2,896,256]{2,1,0:T(8,128)(2,1)S(1)}, bf16[2,896,256]{2,1,0:T(8,128)(2,1)S(1)}, u32[]{:S(2)}, u32[]{:S(2)}) collective-permute-start(bf16[2,896,256]{2,1,0:T(8,128)(2,1)S(1)} %collective-permute-done.7.refs_4_), channel_id=1, source_target_pairs={{0,1},{1,0},{2,3},{3,2},{4,5},{5,4},{6,7},{7,6},{8,9},{9,8},{10,11... | collective-permute-start | bytes 2752520 | tf_op jit(solution)/shard_map/merge/ppermute | solution.py:19
  157.0 11.8 %collective-permute-start.12 = (bf16[896,256]{1,0:T(8,128)(2,1)S(1)}, bf16[896,256]{1,0:T(8,128)(2,1)S(1)}, u32[]{:S(2)}, u32[]{:S(2)}) collective-permute-start(bf16[896,256]{1,0:T(8,128)(2,1)S(1)} %slice_bitcast_fusion.1), channel_id=1, source_target_pairs={{0,16},{16,0},{32,48},{48,32},{1,17},{17,1},{33,49},{49,33},{2,18}... | collective-permute-start | bytes 1376264 | tf_op jit(solution)/shard_map/merge/ppermute | solution.py:19
  160.5 12.2 %collective-permute-start.13 = (bf16[896,256]{1,0:T(8,128)(2,1)S(1)}, bf16[896,256]{1,0:T(8,128)(2,1)S(1)}, u32[]{:S(2)}, u32[]{:S(2)}) collective-permute-start(bf16[896,256]{1,0:T(8,128)(2,1)S(1)} %slice_bitcast_fusion), channel_id=1, source_target_pairs={{0,48},{16,32},{32,16},{48,0},{1,49},{17,33},{33,17},{49,1},{2,50}... | collective-permute-start | bytes 1376264 | tf_op jit(solution)/shard_map/merge/ppermute | solution.py:19
  168.8 6.4 %collective-permute-start.16 = (bf16[896,256]{1,0:T(8,128)(2,1)S(1)}, bf16[896,256]{1,0:T(8,128)(2,1)S(1)}, u32[]{:S(2)}, u32[]{:S(2)}) collective-permute-start(bf16[896,256]{1,0:T(8,128)(2,1)S(1)} %collective-permute-done.12.refs_2_), channel_id=1, source_target_pairs={{0,1},{1,0},{2,3},{3,2},{4,5},{5,4},{6,7},{7,6},{8,9},{9,8},{10,11... | collective-permute-start | bytes 1376264 | tf_op jit(solution)/shard_map/merge/ppermute | solution.py:19
  174.6 4.0 collective-permute-start.28
  204.0 4.4 %collective-permute-start.29 = (bf16[8,3584]{1,0:T(8,128)(2,1)S(1)}, bf16[8,3584]{1,0:T(8,128)(2,1)S(1)}, u32[]{:S(2)}, u32[]{:S(2)}) collective-permute-start(bf16[8,3584]{1,0:T(8,128)(2,1)S(1)} %layer.21.refs_0_), channel_id=1, source_target_pairs={{0,64},{64,128},{128,192},{1,65},{65,129},{129,193},{2,66},{66,130... | collective-permute-start | bytes 172040 | tf_op jit(solution)/shard_map/layer/ppermute | solution.py:556
  227.6 3.9 collective-permute-start.30
  252.5 4.9 %collective-permute-start.31 = (bf16[8,3584]{1,0:T(8,128)(2,1)S(1)}, bf16[8,3584]{1,0:T(8,128)(2,1)S(1)}, u32[]{:S(2)}, u32[]{:S(2)}) collective-permute-start(bf16[8,3584]{1,0:T(8,128)(2,1)S(1)} %layer.25.refs_1_.refs_4_), channel_id=1, source_target_pairs={{0,64},{64,128},{128,192},{1,65},{65,129},{129,193},{2,66},{66,130... | collective-permute-start | bytes 172040 | tf_op jit(solution)/shard_map/layer/ppermute | solution.py:556
  276.2 4.1 collective-permute-start.32
  301.3 4.9 %collective-permute-start.33 = (bf16[8,3584]{1,0:T(8,128)(2,1)S(1)}, bf16[8,3584]{1,0:T(8,128)(2,1)S(1)}, u32[]{:S(2)}, u32[]{:S(2)}) collective-permute-start(bf16[8,3584]{1,0:T(8,128)(2,1)S(1)} %layer.29.refs_2_.refs_5_), channel_id=1, source_target_pairs={{0,64},{64,128},{128,192},{1,65},{65,129},{129,193},{2,66},{66,130... | collective-permute-start | bytes 172040 | tf_op jit(solution)/shard_map/layer/ppermute | solution.py:556
  349.8 4.9 %collective-permute-start.35 = (bf16[8,3584]{1,0:T(8,128)(2,1)S(1)}, bf16[8,3584]{1,0:T(8,128)(2,1)S(1)}, u32[]{:S(2)}, u32[]{:S(2)}) collective-permute-start(bf16[8,3584]{1,0:T(8,128)(2,1)S(1)} %layer.33.refs_3_.refs_6_), channel_id=1, source_target_pairs={{0,64},{64,128},{128,192},{1,65},{65,129},{129,193},{2,66},{66,130... | collective-permute-start | bytes 172040 | tf_op jit(solution)/shard_map/layer/ppermute | solution.py:556
  399.7 11.3 %all-to-all-start.10 = ((f32[16,1,128]{2,1,0:T(1,128)}), f32[16,1,128]{2,1,0:T(1,128)S(1)}, u32[]{:S(2)}, u32[]{:S(2)}) async-start(f32[16,1,128]{2,1,0:T(1,128)} %get-tuple-element.63), calls=%async_computation.10 | async-start | bytes 16384 | tf_op jit(solution)/shard_map/loss/all_to_all | solution.py:571
  403.4 8.9 %collective-permute-start.37 = (bf16[8,3584]{1,0:T(8,128)(2,1)S(1)}, bf16[8,3584]{1,0:T(8,128)(2,1)S(1)}, u32[]{:S(2)}, u32[]{:S(2)}) collective-permute-start(bf16[8,3584]{1,0:T(8,128)(2,1)S(1)} %get-tuple-element.61), channel_id=1, source_target_pairs={{0,0},{2,1},{4,2},{6,3},{8,4},{10,5},{12,6},{14,7},{1,8},{3,9},{5,... | collective-permute-start | bytes 172040 | tf_op jit(solution)/shard_map/loss/ppermute | solution.py:519
  (16 other events, 66.7 us)
where the time goes:
time: 418 us; the launch traced here: 416 us
  blocking collectives  164 us (39%)
  waiting for transfers between devices  107 us (26%)
  starting transfers between devices  74.7 us (18%)
  Pallas kernels  59.4 us (14%)
  local copies, waits for them, and re-layouts  6.19 us (1%)
    all_to_all x9, blocking collectives, spread(): lax.all_to_all(pieces, 'mp', 0, 0, tiled=True, axis_index_groups=groups)  164 us
    ppermute x31, waiting for transfers between devices, exchanged(): lax.ppermute(array, axis, [(i, i ^ mask) for i in range(lax.axis_size(axi...  86.2 us
    pallas_call x33, Pallas kernels, kernel_call(): pl.pallas_call(kernel, out_shape=tuple((result_on_chip(shape[:-1], F32) i...  59.4 us
    ppermute x31, starting transfers between devices, exchanged(): lax.ppermute(array, axis, [(i, i ^ mask) for i in range(lax.axis_size(axi...  33.8 us
    ppermute x4, starting transfers between devices, over_mp(): return lax.ppermute(array, 'mp', pairs)  15.6 us
    all_to_all x1, waiting for transfers between devices, spread(): lax.all_to_all(pieces, 'mp', 0, 0, tiled=True, axis_index_groups=groups)  14.3 us
    ppermute x4, starting transfers between devices, per_device(): lax.ppermute(outs[-1], 'section', [(i, i + 1) for i in range(sections - 1)])  14.2 us
  transfers between devices with their start and end apart: 41, of which 25 were waited for; matrix products, arithmetic and copies ran while one was open for 1% of the time, Pallas kernels for 8%

commit v1 on v0

--- a/solution.py
+++ b/solution.py
@@ -523,28 +523,32 @@
         return queries, (kv, exchanged(kv, "mp", 1))
 
     with jax.named_scope("merge"):
-        _, qkv_got = first_halves(plan, scale, qkv_sources)
-        one, other = dealing(scalars, hidden_in[0], layer_targets[0, 0])
+        out_sent, out_got = first_halves(plan, scale, out_sources)
+        plan, _ = lax.optimization_barrier((plan, out_sent))
+        qkv_sent, qkv_got = first_halves(plan, scale, qkv_sources)
+        rows_in, rows_target, _ = lax.optimization_barrier(
+            (hidden_in[0], layer_targets[0, 0], qkv_sent)
+        )
+        one, other = dealing(scalars, rows_in, rows_target)
         one, other = over_mp(one, straight), over_mp(other, crossed)
-        out_sent, out_got = first_halves(plan, scale, out_sources)
         first, states = entered(scalars, pre_gain, one, other, None, 0, chips)
-        first, cosine, sine, _ = lax.optimization_barrier((first, cosine, sine, out_sent))
+        first, cosine, sine = lax.optimization_barrier((first, cosine, sine))
         first = spread(first)
-        qkv_got, first = lax.optimization_barrier((qkv_got, first))
+        out_got, first = lax.optimization_barrier((out_got, first))
+        out_sent, out_more = second_halves(plan, scale, out_sources, out_got)
+        qkv_got, _ = lax.optimization_barrier((qkv_got, out_sent))
         qkv_sent, qkv_more = second_halves(plan, scale, qkv_sources, qkv_got)
-        out_got, _ = lax.optimization_barrier((out_got, qkv_sent))
-        out_sent, out_more = second_halves(plan, scale, out_sources, out_got)
         qkv_share = shares(plan, scale, qkv_sources, qkv_got, qkv_more)
+        qkv_first = neighbours(qkv_share)
         out_more, _ = lax.optimization_barrier((out_more, qkv_share))
         out_share = shares(plan, scale, out_sources, out_got, out_more)
-        qkv_first = neighbours(qkv_share)
-        qkv_first, _ = lax.optimization_barrier((qkv_first, out_share))
+        out_first = neighbours(out_share)
         qkv_own = completed(qkv_share, *qkv_first)
         qkv_peer = of_partner(qkv_own)
-        out_first = neighbours(out_share)
     with jax.named_scope("layer"):
         queries, kv = projected(0, first)
     with jax.named_scope("merge"):
+        out_first, _ = lax.optimization_barrier((out_first, queries))
         out_own = completed(out_share, *out_first)
         out_peer = of_partner(out_own)
 

time: 418 us -> 425 us (1.017)
  starting transfers between devices: 74.7 us -> 96 us
  waiting for transfers between devices: 107 us -> 94.3 us
    ppermute x31, starting transfers between devices: 33.8 us -> 55.4 us  [exchanged(): lax.ppermute(array, axis, [(i, i ^ mask) for i in range(lax.axis_size(axi...]
    ppermute x31, waiting for transfers between devices: 86.2 us -> 64.8 us  [exchanged(): lax.ppermute(array, axis, [(i, i ^ mask) for i in range(lax.axis_size(axi...]
    ppermute x4, waiting for transfers between devices: 1.73 us -> 10.5 us  [over_mp(): return lax.ppermute(array, 'mp', pairs)]
  transfers between devices with their start and end apart: 41 -> 41, of which waited for: 25 -> 22; matrix products, arithmetic and copies ran while one was open for 1% -> 0% of each run, Pallas kernels for 8% -> 6%
where the time goes in v1:
time: 425 us; the launch traced here: 424 us
  blocking collectives  164 us (39%)
  starting transfers between devices  96 us (23%)
  waiting for transfers between devices  94.3 us (22%)
  Pallas kernels  60.4 us (14%)
    all_to_all x9, blocking collectives, spread(): lax.all_to_all(pieces, 'mp', 0, 0, tiled=True, axis_index_groups=groups)  164 us
    ppermute x31, waiting for transfers between devices, exchanged(): lax.ppermute(array, axis, [(i, i ^ mask) for i in range(lax.axis_size(axi...  64.8 us
    pallas_call x33, Pallas kernels, kernel_call(): pl.pallas_call(kernel, out_shape=tuple((result_on_chip(shape[:-1], F32) i...  60.4 us
    ppermute x31, starting transfers between devices, exchanged(): lax.ppermute(array, axis, [(i, i ^ mask) for i in range(lax.axis_size(axi...  55.4 us
    ppermute x4, starting transfers between devices, per_device(): lax.ppermute(outs[-1], 'section', [(i, i + 1) for i in range(sections - 1)])  14.3 us
    all_to_all x1, waiting for transfers between devices, spread(): lax.all_to_all(pieces, 'mp', 0, 0, tiled=True, axis_index_groups=groups)  14 us
    ppermute x4, starting transfers between devices, over_mp(): return lax.ppermute(array, 'mp', pairs)  13.2 us
    ppermute x4, waiting for transfers between devices, over_mp(): return lax.ppermute(array, 'mp', pairs)  10.5 us
  transfers between devices with their start and end apart: 41, of which 22 were waited for; matrix products, arithmetic and copies ran while one was open for 0% of the time, Pallas kernels for 6%

profile of v1, /device:TPU:1, one launch (start us, length us, event | category | flops | bytes accessed | tf_op | source)
XLA Modules:
  0.0 423.6 jit_solution(6430444450649198355)
XLA Ops:
  13.1 4.2 merge.14
  17.7 4.2 %merge.15 = bf16[2,2,896,256]{3,2,1,0:T(8,128)(2,1)} custom-call(s32[16]{0:T(128)S(1)} %stack.69.plan_ref, f32[1]{0:T(128)} %dynamic_slice.3.scale_ref, bf16[4,896,128]{2,1,0:T(8,128)(2,1)} %bitcast.101, bf16[4,896,128]{2,1,0:T(8,128)(2,1)} %bitcast.104, bf16[4,896,128]{2,1,0:T(8,128)(2,1)} %bitcast.107, bf16[4,896,128]{2,1,0:T(8,128)(2,1)} %bitcast.110), custom_call_target="tpu_custom_call" | custom-call | tf_op jit(solution)/shard_map/merge/pallas_call | solution.py:32
  24.1 4.9 %collective-permute-start = (bf16[16,3584]{1,0:T(8,128)(2,1)S(1)}, bf16[16,3584]{1,0:T(8,128)(2,1)S(1)}, u32[]{:S(2)}, u32[]{:S(2)}) collective-permute-start(bf16[16,3584]{1,0:T(8,128)(2,1)S(1)} %get-tuple-element.39), channel_id=1, source_target_pairs={{0,0},{1,2},{2,4},{3,6},{4,8},{5,10},{6,12},{7,14},{8,1},{9,3},{10... | collective-permute-start | bytes 344072 | tf_op jit(solution)/shard_map/merge/ppermute | solution.py:519
  29.4 7.3 %collective-permute-done.s_ref = bf16[16,3584]{1,0:T(8,128)(2,1)S(1)} collective-permute-done((bf16[16,3584]{1,0:T(8,128)(2,1)S(1)}, bf16[16,3584]{1,0:T(8,128)(2,1)S(1)}, u32[]{:S(2)}, u32[]{:S(2)}) %collective-permute-start) | collective-permute-done | bytes 114720 | tf_op jit(solution)/shard_map/merge/ppermute | solution.py:519
  41.3 9.5 %all-to-all-start = ((bf16[8,8,3584]{2,1,0:T(8,128)(2,1)}), bf16[8,8,3584]{2,1,0:T(8,128)(2,1)S(1)}, u32[]{:S(2)}, u32[]{:S(2)}) async-start(bf16[8,8,3584]{2,1,0:T(8,128)(2,1)} %bitcast.79), calls=%async_computation | async-start | bytes 917504 | tf_op jit(solution)/shard_map/merge/all_to_all | solution.py:510
  50.8 14.0 %all-to-all-done = bf16[8,8,3584]{2,1,0:T(8,128)(2,1)S(1)} async-done(((bf16[8,8,3584]{2,1,0:T(8,128)(2,1)}), bf16[8,8,3584]{2,1,0:T(8,128)(2,1)S(1)}, u32[]{:S(2)}, u32[]{:S(2)}) %all-to-all-start) | async-done | bytes 458784 | tf_op jit(solution)/shard_map/merge/all_to_all | solution.py:510
  75.5 3.8 merge.21
  81.6 17.5 %collective-permute-done.7.refs_9_ = bf16[2,1,896,256]{3,2,1,0:T(8,128)(2,1)S(1)} collective-permute-done((bf16[2,1,896,256]{3,2,1,0:T(8,128)(2,1)S(1)}, bf16[2,1,896,256]{3,2,1,0:T(8,128)(2,1)S(1)}, u32[]{:S(2)}, u32[]{:S(2)}) %collective-permute-start.7) | collective-permute-done | bytes 917536 | tf_op jit(solution)/shard_map/merge/ppermute | solution.py:19
  100.4 5.0 %merge.22.refs_0_ = bf16[2,896,256]{2,1,0:T(8,128)(2,1)S(1)} custom-call(s32[16]{0:T(128)S(1)} %stack.69.plan_ref, f32[1]{0:T(128)} %dynamic_slice.3.scale_ref, bf16[4,896,256]{2,1,0:T(8,128)(2,1)} %bitcast.97, bf16[4,896,256]{2,1,0:T(8,128)(2,1)} %bitcast.100, bf16[2,2,896,256]{3,2,1,0:T(8,128)(2,1)S(1)} %collective-permute-done.4.refs_2_, ...), custom_call_target="tpu_custom_call" | custom-call | tf_op jit(solution)/shard_map/merge/pallas_call | solution.py:32
  109.6 4.2 collective-permute-start.12
  113.8 11.7 %collective-permute-done.9.refs_4_ = bf16[2,896,256]{2,1,0:T(8,128)(2,1)S(1)} collective-permute-done((bf16[2,896,256]{2,1,0:T(8,128)(2,1)S(1)}, bf16[2,896,256]{2,1,0:T(8,128)(2,1)S(1)}, u32[]{:S(2)}, u32[]{:S(2)}) %collective-permute-start.9) | collective-permute-done | bytes 917536 | tf_op jit(solution)/shard_map/merge/ppermute | solution.py:19
  125.5 7.6 %collective-permute-start.16 = (bf16[2,896,256]{2,1,0:T(8,128)(2,1)S(1)}, bf16[2,896,256]{2,1,0:T(8,128)(2,1)S(1)}, u32[]{:S(2)}, u32[]{:S(2)}) collective-permute-start(bf16[2,896,256]{2,1,0:T(8,128)(2,1)S(1)} %collective-permute-done.9.refs_4_), channel_id=1, source_target_pairs={{0,1},{1,0},{2,3},{3,2},{4,5},{5,4},{6,7},{7,6},{8,9},{9,8},{10,11... | collective-permute-start | bytes 2752520 | tf_op jit(solution)/shard_map/merge/ppermute | solution.py:19
  136.4 7.6 %collective-permute-start.13 = (bf16[2,896,256]{2,1,0:T(8,128)(2,1)S(1)}, bf16[2,896,256]{2,1,0:T(8,128)(2,1)S(1)}, u32[]{:S(2)}, u32[]{:S(2)}) collective-permute-start(bf16[2,896,256]{2,1,0:T(8,128)(2,1)S(1)} %collective-permute-done.8.refs_1_), channel_id=1, source_target_pairs={{0,1},{1,0},{2,3},{3,2},{4,5},{5,4},{6,7},{7,6},{8,9},{9,8},{10,11... | collective-permute-start | bytes 2752520 | tf_op jit(solution)/shard_map/merge/ppermute | solution.py:19
  146.3 4.0 collective-permute-start.14
  150.3 7.1 %collective-permute-done.11.refs_3_ = bf16[896,256]{1,0:T(8,128)(2,1)S(1)} collective-permute-done((bf16[896,256]{1,0:T(8,128)(2,1)S(1)}, bf16[896,256]{1,0:T(8,128)(2,1)S(1)}, u32[]{:S(2)}, u32[]{:S(2)}) %collective-permute-start.11) | collective-permute-done | bytes 458784 | tf_op jit(solution)/shard_map/merge/ppermute | solution.py:19
  158.2 3.6 merge.23.refs_4_
  164.3 11.0 %collective-permute-done.21.refs_8_ = bf16[2,128,896]{2,1,0:T(8,128)(2,1)S(1)} collective-permute-done((bf16[2,128,896]{2,1,0:T(8,128)(2,1)S(1)}, bf16[2,128,896]{2,1,0:T(8,128)(2,1)S(1)}, u32[]{:S(2)}, u32[]{:S(2)}) %collective-permute-start.21) | collective-permute-done | bytes 458784 | tf_op jit(solution)/shard_map/merge/ppermute | solution.py:19
  187.9 23.4 %all_to_all.55 = bf16[8,8,3584]{2,1,0:T(8,128)(2,1)S(1)} all-to-all(bf16[8,8,3584]{2,1,0:T(8,128)(2,1)S(1)} %bitcast.65), channel_id=1, replica_groups={{0,2,4,6,8,10,12,14},{1,3,5,7,9,11,13,15},{16,18,20,22,24,26,28,30},{17..., dimensions={0} | all-to-all | bytes 917504 | tf_op jit(solution)/shard_map/layer/all_to_all | solution.py:510
  216.6 15.1 %all_to_all.56 = bf16[8,8,3584]{2,1,0:T(8,128)(2,1)S(1)} all-to-all(bf16[8,8,3584]{2,1,0:T(8,128)(2,1)S(1)} %bitcast.80), channel_id=1, replica_groups={{0,2,4,6,8,10,12,14},{1,3,5,7,9,11,13,15},{16,18,20,22,24,26,28,30},{17..., dimensions={0} | all-to-all | bytes 917504 | tf_op jit(solution)/shard_map/layer/all_to_all | solution.py:510
  233.7 4.4 %collective-permute-start.30 = (bf16[64,512]{1,0:T(8,128)(2,1)S(1)}, bf16[64,512]{1,0:T(8,128)(2,1)S(1)}, u32[]{:S(2)}, u32[]{:S(2)}) collective-permute-start(bf16[64,512]{1,0:T(8,128)(2,1)S(1)} %get-tuple-element.59.refs_2_.refs_0_), channel_id=1, source_target_pairs={{0,1},{1,0},{2,3},{3,2},{4,5},{5,4},{6,7},{7,6},{8,9},{9,8},{10,11... | collective-permute-start | bytes 196616 | tf_op jit(solution)/shard_map/layer/ppermute | solution.py:19
  240.9 19.0 %all_to_all.57 = bf16[8,8,3584]{2,1,0:T(8,128)(2,1)S(1)} all-to-all(bf16[8,8,3584]{2,1,0:T(8,128)(2,1)S(1)} %bitcast.62), channel_id=1, replica_groups={{0,2,4,6,8,10,12,14},{1,3,5,7,9,11,13,15},{16,18,20,22,24,26,28,30},{17..., dimensions={0} | all-to-all | bytes 917504 | tf_op jit(solution)/shard_map/layer/all_to_all | solution.py:510
  260.1 3.7 collective-permute-start.31
  265.1 16.6 %all_to_all.58 = bf16[8,8,3584]{2,1,0:T(8,128)(2,1)S(1)} all-to-all(bf16[8,8,3584]{2,1,0:T(8,128)(2,1)S(1)} %bitcast.72), channel_id=1, replica_groups={{0,2,4,6,8,10,12,14},{1,3,5,7,9,11,13,15},{16,18,20,22,24,26,28,30},{17..., dimensions={0} | all-to-all | bytes 917504 | tf_op jit(solution)/shard_map/layer/all_to_all | solution.py:510
  289.3 19.0 %all_to_all.59 = bf16[8,8,3584]{2,1,0:T(8,128)(2,1)S(1)} all-to-all(bf16[8,8,3584]{2,1,0:T(8,128)(2,1)S(1)} %bitcast.63), channel_id=1, replica_groups={{0,2,4,6,8,10,12,14},{1,3,5,7,9,11,13,15},{16,18,20,22,24,26,28,30},{17..., dimensions={0} | all-to-all | bytes 917504 | tf_op jit(solution)/shard_map/layer/all_to_all | solution.py:510
  308.5 3.7 collective-permute-start.33
  313.5 16.6 %all_to_all.60 = bf16[8,8,3584]{2,1,0:T(8,128)(2,1)S(1)} all-to-all(bf16[8,8,3584]{2,1,0:T(8,128)(2,1)S(1)} %bitcast.73), channel_id=1, replica_groups={{0,2,4,6,8,10,12,14},{1,3,5,7,9,11,13,15},{16,18,20,22,24,26,28,30},{17..., dimensions={0} | all-to-all | bytes 917504 | tf_op jit(solution)/shard_map/layer/all_to_all | solution.py:510
  337.8 19.0 %all_to_all.61 = bf16[8,8,3584]{2,1,0:T(8,128)(2,1)S(1)} all-to-all(bf16[8,8,3584]{2,1,0:T(8,128)(2,1)S(1)} %bitcast.64), channel_id=1, replica_groups={{0,2,4,6,8,10,12,14},{1,3,5,7,9,11,13,15},{16,18,20,22,24,26,28,30},{17..., dimensions={0} | all-to-all | bytes 917504 | tf_op jit(solution)/shard_map/layer/all_to_all | solution.py:510
  357.0 3.7 collective-permute-start.35
  362.1 16.6 %all_to_all.62 = bf16[8,8,3584]{2,1,0:T(8,128)(2,1)S(1)} all-to-all(bf16[8,8,3584]{2,1,0:T(8,128)(2,1)S(1)} %bitcast.71), channel_id=1, replica_groups={{0,2,4,6,8,10,12,14},{1,3,5,7,9,11,13,15},{16,18,20,22,24,26,28,30},{17..., dimensions={0} | all-to-all | bytes 917504 | tf_op jit(solution)/shard_map/layer/all_to_all | solution.py:510
  386.3 19.0 %all_to_all.63 = bf16[8,8,3584]{2,1,0:T(8,128)(2,1)S(1)} all-to-all(bf16[8,8,3584]{2,1,0:T(8,128)(2,1)S(1)} %bitcast.61), channel_id=1, replica_groups={{0,2,4,6,8,10,12,14},{1,3,5,7,9,11,13,15},{16,18,20,22,24,26,28,30},{17..., dimensions={0} | all-to-all | bytes 917504 | tf_op jit(solution)/shard_map/layer/all_to_all | solution.py:510
  406.9 3.7 all-to-all-start.10
  410.6 7.5 %collective-permute-start.37 = (bf16[8,3584]{1,0:T(8,128)(2,1)S(1)}, bf16[8,3584]{1,0:T(8,128)(2,1)S(1)}, u32[]{:S(2)}, u32[]{:S(2)}) collective-permute-start(bf16[8,3584]{1,0:T(8,128)(2,1)S(1)} %get-tuple-element.67), channel_id=1, source_target_pairs={{0,0},{2,1},{4,2},{6,3},{8,4},{10,5},{12,6},{14,7},{1,8},{3,9},{5,... | collective-permute-start | bytes 172040 | tf_op jit(solution)/shard_map/loss/ppermute | solution.py:519
  (125 shorter events, 101.9 us)
Async XLA Ops:
  5.6 45.2 %collective-permute-start.2 = (bf16[2,2,128,896]{3,2,1,0:T(8,128)(2,1)}, bf16[2,2,128,896]{3,2,1,0:T(8,128)(2,1)S(1)}, u32[]{:S(2)}, u32[]{:S(2)}) collective-permute-start(bf16[2,2,128,896]{3,2,1,0:T(8,128)(2,1)} %merge.12), channel_id=1, source_target_pairs={{0,16},{16,0},{32,48},{48,32},{1,17},{17,1},{33,49},{49,33},{2,18}... | collective-permute-start | bytes 2752520 | tf_op jit(solution)/shard_map/merge/ppermute | solution.py:19
  11.2 39.6 %collective-permute-start.3 = (bf16[2,2,128,896]{3,2,1,0:T(8,128)(2,1)}, bf16[2,2,128,896]{3,2,1,0:T(8,128)(2,1)}, u32[]{:S(2)}, u32[]{:S(2)}) collective-permute-start(bf16[2,2,128,896]{3,2,1,0:T(8,128)(2,1)} %merge.13), channel_id=1, source_target_pairs={{0,48},{16,32},{32,16},{48,0},{1,49},{17,33},{33,17},{49,1},{2,50}... | collective-permute-start | bytes 2752520 | tf_op jit(solution)/shard_map/merge/ppermute | solution.py:19
  17.3 53.0 %collective-permute-start.4 = (bf16[2,2,896,256]{3,2,1,0:T(8,128)(2,1)}, bf16[2,2,896,256]{3,2,1,0:T(8,128)(2,1)S(1)}, u32[]{:S(2)}, u32[]{:S(2)}) collective-permute-start(bf16[2,2,896,256]{3,2,1,0:T(8,128)(2,1)} %merge.14), channel_id=1, source_target_pairs={{0,16},{16,0},{32,48},{48,32},{1,17},{17,1},{33,49},{49,33},{2,18}... | collective-permute-start | bytes 5505032 | tf_op jit(solution)/shard_map/merge/ppermute | solution.py:19
  22.0 50.8 %collective-permute-start.5 = (bf16[2,2,896,256]{3,2,1,0:T(8,128)(2,1)}, bf16[2,2,896,256]{3,2,1,0:T(8,128)(2,1)}, u32[]{:S(2)}, u32[]{:S(2)}) collective-permute-start(bf16[2,2,896,256]{3,2,1,0:T(8,128)(2,1)} %merge.15), channel_id=1, source_target_pairs={{0,48},{16,32},{32,16},{48,0},{1,49},{17,33},{33,17},{49,1},{2,50}... | collective-permute-start | bytes 5505032 | tf_op jit(solution)/shard_map/merge/ppermute | solution.py:19
  24.1 12.7 %collective-permute-start = (bf16[16,3584]{1,0:T(8,128)(2,1)S(1)}, bf16[16,3584]{1,0:T(8,128)(2,1)S(1)}, u32[]{:S(2)}, u32[]{:S(2)}) collective-permute-start(bf16[16,3584]{1,0:T(8,128)(2,1)S(1)} %get-tuple-element.39), channel_id=1, source_target_pairs={{0,0},{1,2},{2,4},{3,6},{4,8},{5,10},{6,12},{7,14},{8,1},{9,3},{10... | collective-permute-start | bytes 344072 | tf_op jit(solution)/shard_map/merge/ppermute | solution.py:519
  41.3 23.5 %all-to-all-start = ((bf16[8,8,3584]{2,1,0:T(8,128)(2,1)}), bf16[8,8,3584]{2,1,0:T(8,128)(2,1)S(1)}, u32[]{:S(2)}, u32[]{:S(2)}) async-start(bf16[8,8,3584]{2,1,0:T(8,128)(2,1)} %bitcast.79), calls=%async_computation | async-start | bytes 917504 | tf_op jit(solution)/shard_map/merge/all_to_all | solution.py:510
  79.3 19.8 %collective-permute-start.7 = (bf16[2,1,896,256]{3,2,1,0:T(8,128)(2,1)S(1)}, bf16[2,1,896,256]{3,2,1,0:T(8,128)(2,1)S(1)}, u32[]{:S(2)}, u32[]{:S(2)}) collective-permute-start(bf16[2,1,896,256]{3,2,1,0:T(8,128)(2,1)S(1)} %merge.21), channel_id=1, source_target_pairs={{0,16},{16,0},{32,48},{48,32},{1,17},{17,1},{33,49},{49,33},{2,18}... | collective-permute-start | bytes 2752520 | tf_op jit(solution)/shard_map/merge/ppermute | solution.py:19
  79.4 21.0 %collective-permute-start.6 = (bf16[2,1,896,256]{3,2,1,0:T(8,128)(2,1)S(1)}, bf16[2,1,896,256]{3,2,1,0:T(8,128)(2,1)S(1)}, u32[]{:S(2)}, u32[]{:S(2)}) collective-permute-start(bf16[2,1,896,256]{3,2,1,0:T(8,128)(2,1)S(1)} %merge.20), channel_id=1, source_target_pairs={{0,48},{16,32},{32,16},{48,0},{1,49},{17,33},{33,17},{49,1},{2,50}... | collective-permute-start | bytes 2752520 | tf_op jit(solution)/shard_map/merge/ppermute | solution.py:19
  105.4 20.1 %collective-permute-start.9 = (bf16[2,896,256]{2,1,0:T(8,128)(2,1)S(1)}, bf16[2,896,256]{2,1,0:T(8,128)(2,1)S(1)}, u32[]{:S(2)}, u32[]{:S(2)}) collective-permute-start(bf16[2,896,256]{2,1,0:T(8,128)(2,1)S(1)} %merge.22.refs_0_), channel_id=1, source_target_pairs={{0,48},{16,32},{32,16},{48,0},{1,49},{17,33},{33,17},{49,1},{2,50}... | collective-permute-start | bytes 2752520 | tf_op jit(solution)/shard_map/merge/ppermute | solution.py:19
  107.8 25.2 %collective-permute-start.8 = (bf16[2,896,256]{2,1,0:T(8,128)(2,1)S(1)}, bf16[2,896,256]{2,1,0:T(8,128)(2,1)S(1)}, u32[]{:S(2)}, u32[]{:S(2)}) collective-permute-start(bf16[2,896,256]{2,1,0:T(8,128)(2,1)S(1)} %merge.22.refs_0_), channel_id=1, source_target_pairs={{0,16},{16,0},{32,48},{48,32},{1,17},{17,1},{33,49},{49,33},{2,18}... | collective-permute-start | bytes 2752520 | tf_op jit(solution)/shard_map/merge/ppermute | solution.py:19
  107.8 28.6 %collective-permute-start.19 = (bf16[2,1,128,896]{3,2,1,0:T(8,128)(2,1)S(1)}, bf16[2,1,128,896]{3,2,1,0:T(8,128)(2,1)S(1)}, u32[]{:S(2)}, u32[]{:S(2)}) collective-permute-start(bf16[2,1,128,896]{3,2,1,0:T(8,128)(2,1)S(1)} %merge.19), channel_id=1, source_target_pairs={{0,16},{16,0},{32,48},{48,32},{1,17},{17,1},{33,49},{49,33},{2,18}... | collective-permute-start | bytes 1376264 | tf_op jit(solution)/shard_map/merge/ppermute | solution.py:19
  109.3 34.7 %collective-permute-start.18 = (bf16[2,1,128,896]{3,2,1,0:T(8,128)(2,1)S(1)}, bf16[2,1,128,896]{3,2,1,0:T(8,128)(2,1)S(1)}, u32[]{:S(2)}, u32[]{:S(2)}) collective-permute-start(bf16[2,1,128,896]{3,2,1,0:T(8,128)(2,1)S(1)} %merge.18), channel_id=1, source_target_pairs={{0,48},{16,32},{32,16},{48,0},{1,49},{17,33},{33,17},{49,1},{2,50}... | collective-permute-start | bytes 1376264 | tf_op jit(solution)/shard_map/merge/ppermute | solution.py:19
  109.6 52.2 %collective-permute-start.12 = (bf16[2,896,256]{2,1,0:T(8,128)(2,1)S(1)}, bf16[2,896,256]{2,1,0:T(8,128)(2,1)S(1)}, u32[]{:S(2)}, u32[]{:S(2)}) collective-permute-start(bf16[2,896,256]{2,1,0:T(8,128)(2,1)S(1)} %merge.22.refs_0_), channel_id=1, source_target_pairs={{0,1},{1,0},{2,3},{3,2},{4,5},{5,4},{6,7},{7,6},{8,9},{9,8},{10,11... | collective-permute-start | bytes 2752520 | tf_op jit(solution)/shard_map/merge/ppermute | solution.py:19
  125.5 36.5 %collective-permute-start.16 = (bf16[2,896,256]{2,1,0:T(8,128)(2,1)S(1)}, bf16[2,896,256]{2,1,0:T(8,128)(2,1)S(1)}, u32[]{:S(2)}, u32[]{:S(2)}) collective-permute-start(bf16[2,896,256]{2,1,0:T(8,128)(2,1)S(1)} %collective-permute-done.9.refs_4_), channel_id=1, source_target_pairs={{0,1},{1,0},{2,3},{3,2},{4,5},{5,4},{6,7},{7,6},{8,9},{9,8},{10,11... | collective-permute-start | bytes 2752520 | tf_op jit(solution)/shard_map/merge/ppermute | solution.py:19
  133.1 13.2 %collective-permute-start.10 = (bf16[896,256]{1,0:T(8,128)(2,1)S(1)}, bf16[896,256]{1,0:T(8,128)(2,1)S(1)}, u32[]{:S(2)}, u32[]{:S(2)}) collective-permute-start(bf16[896,256]{1,0:T(8,128)(2,1)S(1)} %slice_bitcast_fusion.1), channel_id=1, source_target_pairs={{0,16},{16,0},{32,48},{48,32},{1,17},{17,1},{33,49},{49,33},{2,18}... | collective-permute-start | bytes 1376264 | tf_op jit(solution)/shard_map/merge/ppermute | solution.py:19
  136.4 25.6 %collective-permute-start.13 = (bf16[2,896,256]{2,1,0:T(8,128)(2,1)S(1)}, bf16[2,896,256]{2,1,0:T(8,128)(2,1)S(1)}, u32[]{:S(2)}, u32[]{:S(2)}) collective-permute-start(bf16[2,896,256]{2,1,0:T(8,128)(2,1)S(1)} %collective-permute-done.8.refs_1_), channel_id=1, source_target_pairs={{0,1},{1,0},{2,3},{3,2},{4,5},{5,4},{6,7},{7,6},{8,9},{9,8},{10,11... | collective-permute-start | bytes 2752520 | tf_op jit(solution)/shard_map/merge/ppermute | solution.py:19
  144.0 13.4 %collective-permute-start.11 = (bf16[896,256]{1,0:T(8,128)(2,1)S(1)}, bf16[896,256]{1,0:T(8,128)(2,1)S(1)}, u32[]{:S(2)}, u32[]{:S(2)}) collective-permute-start(bf16[896,256]{1,0:T(8,128)(2,1)S(1)} %slice_bitcast_fusion), channel_id=1, source_target_pairs={{0,48},{16,32},{32,16},{48,0},{1,49},{17,33},{33,17},{49,1},{2,50}... | collective-permute-start | bytes 1376264 | tf_op jit(solution)/shard_map/merge/ppermute | solution.py:19
  146.3 16.0 %collective-permute-start.14 = (bf16[896,256]{1,0:T(8,128)(2,1)S(1)}, bf16[896,256]{1,0:T(8,128)(2,1)S(1)}, u32[]{:S(2)}, u32[]{:S(2)}) collective-permute-start(bf16[896,256]{1,0:T(8,128)(2,1)S(1)} %collective-permute-done.10.refs_2_), channel_id=1, source_target_pairs={{0,1},{1,0},{2,3},{3,2},{4,5},{5,4},{6,7},{7,6},{8,9},{9,8},{10,11... | collective-permute-start | bytes 1376264 | tf_op jit(solution)/shard_map/merge/ppermute | solution.py:19
  157.4 4.9 %collective-permute-start.15 = (bf16[896,256]{1,0:T(8,128)(2,1)S(1)}, bf16[896,256]{1,0:T(8,128)(2,1)S(1)}, u32[]{:S(2)}, u32[]{:S(2)}) collective-permute-start(bf16[896,256]{1,0:T(8,128)(2,1)S(1)} %collective-permute-done.11.refs_3_), channel_id=1, source_target_pairs={{0,1},{1,0},{2,3},{3,2},{4,5},{5,4},{6,7},{7,6},{8,9},{9,8},{10,11... | collective-permute-start | bytes 1376264 | tf_op jit(solution)/shard_map/merge/ppermute | solution.py:19
  161.8 13.4 %collective-permute-start.21 = (bf16[2,128,896]{2,1,0:T(8,128)(2,1)S(1)}, bf16[2,128,896]{2,1,0:T(8,128)(2,1)S(1)}, u32[]{:S(2)}, u32[]{:S(2)}) collective-permute-start(bf16[2,128,896]{2,1,0:T(8,128)(2,1)S(1)} %merge.23.refs_4_), channel_id=1, source_target_pairs={{0,48},{16,32},{32,16},{48,0},{1,49},{17,33},{33,17},{49,1},{2,50}... | collective-permute-start | bytes 1376264 | tf_op jit(solution)/shard_map/merge/ppermute | solution.py:19
  161.9 13.3 %collective-permute-start.20 = (bf16[2,128,896]{2,1,0:T(8,128)(2,1)S(1)}, bf16[2,128,896]{2,1,0:T(8,128)(2,1)S(1)}, u32[]{:S(2)}, u32[]{:S(2)}) collective-permute-start(bf16[2,128,896]{2,1,0:T(8,128)(2,1)S(1)} %merge.23.refs_4_), channel_id=1, source_target_pairs={{0,16},{16,0},{32,48},{48,32},{1,17},{17,1},{33,49},{49,33},{2,18}... | collective-permute-start | bytes 1376264 | tf_op jit(solution)/shard_map/merge/ppermute | solution.py:19
  162.0 22.7 %collective-permute-start.24 = (bf16[2,128,896]{2,1,0:T(8,128)(2,1)S(1)}, bf16[2,128,896]{2,1,0:T(8,128)(2,1)S(1)}, u32[]{:S(2)}, u32[]{:S(2)}) collective-permute-start(bf16[2,128,896]{2,1,0:T(8,128)(2,1)S(1)} %merge.23.refs_4_), channel_id=1, source_target_pairs={{0,1},{1,0},{2,3},{3,2},{4,5},{5,4},{6,7},{7,6},{8,9},{9,8},{10,11... | collective-permute-start | bytes 1376264 | tf_op jit(solution)/shard_map/merge/ppermute | solution.py:19
  175.3 6.4 %collective-permute-start.22 = (bf16[128,896]{1,0:T(8,128)(2,1)S(1)}, bf16[128,896]{1,0:T(8,128)(2,1)S(1)}, u32[]{:S(2)}, u32[]{:S(2)}) collective-permute-start(bf16[128,896]{1,0:T(8,128)(2,1)S(1)} %slice_bitcast_fusion.3), channel_id=1, source_target_pairs={{0,16},{16,0},{32,48},{48,32},{1,17},{17,1},{33,49},{49,33},{2,18}... | collective-permute-start | bytes 688136 | tf_op jit(solution)/shard_map/merge/ppermute | solution.py:19
  175.4 8.0 %collective-permute-start.23 = (bf16[128,896]{1,0:T(8,128)(2,1)S(1)}, bf16[128,896]{1,0:T(8,128)(2,1)S(1)}, u32[]{:S(2)}, u32[]{:S(2)}) collective-permute-start(bf16[128,896]{1,0:T(8,128)(2,1)S(1)} %slice_bitcast_fusion.2), channel_id=1, source_target_pairs={{0,48},{16,32},{32,16},{48,0},{1,49},{17,33},{33,17},{49,1},{2,50}... | collective-permute-start | bytes 688136 | tf_op jit(solution)/shard_map/merge/ppermute | solution.py:19
  177.0 9.1 %collective-permute-start.25 = (bf16[2,128,896]{2,1,0:T(8,128)(2,1)S(1)}, bf16[2,128,896]{2,1,0:T(8,128)(2,1)S(1)}, u32[]{:S(2)}, u32[]{:S(2)}) collective-permute-start(bf16[2,128,896]{2,1,0:T(8,128)(2,1)S(1)} %collective-permute-done.20.refs_5_), channel_id=1, source_target_pairs={{0,1},{1,0},{2,3},{3,2},{4,5},{5,4},{6,7},{7,6},{8,9},{9,8},{10,11... | collective-permute-start | bytes 1376264 | tf_op jit(solution)/shard_map/merge/ppermute | solution.py:19
  178.3 7.7 %collective-permute-start.28 = (bf16[2,128,896]{2,1,0:T(8,128)(2,1)S(1)}, bf16[2,128,896]{2,1,0:T(8,128)(2,1)S(1)}, u32[]{:S(2)}, u32[]{:S(2)}) collective-permute-start(bf16[2,128,896]{2,1,0:T(8,128)(2,1)S(1)} %collective-permute-done.21.refs_8_), channel_id=1, source_target_pairs={{0,1},{1,0},{2,3},{3,2},{4,5},{5,4},{6,7},{7,6},{8,9},{9,8},{10,11... | collective-permute-start | bytes 1376264 | tf_op jit(solution)/shard_map/merge/ppermute | solution.py:19
  233.7 5.3 %collective-permute-start.30 = (bf16[64,512]{1,0:T(8,128)(2,1)S(1)}, bf16[64,512]{1,0:T(8,128)(2,1)S(1)}, u32[]{:S(2)}, u32[]{:S(2)}) collective-permute-start(bf16[64,512]{1,0:T(8,128)(2,1)S(1)} %get-tuple-element.59.refs_2_.refs_0_), channel_id=1, source_target_pairs={{0,1},{1,0},{2,3},{3,2},{4,5},{5,4},{6,7},{7,6},{8,9},{9,8},{10,11... | collective-permute-start | bytes 196616 | tf_op jit(solution)/shard_map/layer/ppermute | solution.py:19
  260.1 4.9 %collective-permute-start.31 = (bf16[8,3584]{1,0:T(8,128)(2,1)S(1)}, bf16[8,3584]{1,0:T(8,128)(2,1)S(1)}, u32[]{:S(2)}, u32[]{:S(2)}) collective-permute-start(bf16[8,3584]{1,0:T(8,128)(2,1)S(1)} %layer.25.refs_1_.refs_4_), channel_id=1, source_target_pairs={{0,64},{64,128},{128,192},{1,65},{65,129},{129,193},{2,66},{66,130... | collective-permute-start | bytes 172040 | tf_op jit(solution)/shard_map/layer/ppermute | solution.py:560
  308.5 4.9 %collective-permute-start.33 = (bf16[8,3584]{1,0:T(8,128)(2,1)S(1)}, bf16[8,3584]{1,0:T(8,128)(2,1)S(1)}, u32[]{:S(2)}, u32[]{:S(2)}) collective-permute-start(bf16[8,3584]{1,0:T(8,128)(2,1)S(1)} %layer.29.refs_2_.refs_5_), channel_id=1, source_target_pairs={{0,64},{64,128},{128,192},{1,65},{65,129},{129,193},{2,66},{66,130... | collective-permute-start | bytes 172040 | tf_op jit(solution)/shard_map/layer/ppermute | solution.py:560
  357.0 4.9 %collective-permute-start.35 = (bf16[8,3584]{1,0:T(8,128)(2,1)S(1)}, bf16[8,3584]{1,0:T(8,128)(2,1)S(1)}, u32[]{:S(2)}, u32[]{:S(2)}) collective-permute-start(bf16[8,3584]{1,0:T(8,128)(2,1)S(1)} %layer.33.refs_3_.refs_6_), channel_id=1, source_target_pairs={{0,64},{64,128},{128,192},{1,65},{65,129},{129,193},{2,66},{66,130... | collective-permute-start | bytes 172040 | tf_op jit(solution)/shard_map/layer/ppermute | solution.py:560
  406.9 11.3 %all-to-all-start.10 = ((f32[16,1,128]{2,1,0:T(1,128)}), f32[16,1,128]{2,1,0:T(1,128)S(1)}, u32[]{:S(2)}, u32[]{:S(2)}) async-start(f32[16,1,128]{2,1,0:T(1,128)} %get-tuple-element.69), calls=%async_computation.10 | async-start | bytes 16384 | tf_op jit(solution)/shard_map/loss/all_to_all | solution.py:575
  410.6 8.9 %collective-permute-start.37 = (bf16[8,3584]{1,0:T(8,128)(2,1)S(1)}, bf16[8,3584]{1,0:T(8,128)(2,1)S(1)}, u32[]{:S(2)}, u32[]{:S(2)}) collective-permute-start(bf16[8,3584]{1,0:T(8,128)(2,1)S(1)} %get-tuple-element.67), channel_id=1, source_target_pairs={{0,0},{2,1},{4,2},{6,3},{8,4},{10,5},{12,6},{14,7},{1,8},{3,9},{5,... | collective-permute-start | bytes 172040 | tf_op jit(solution)/shard_map/loss/ppermute | solution.py:519
  (15 other events, 85.2 us)

commit v2 on v1

--- a/solution.py
+++ b/solution.py
@@ -39,6 +39,7 @@
         out_specs=tuple(pl.BlockSpec(memory_space=VMEM) for _ in shapes),
         scratch_shapes=scratch,
         compiler_params=pltpu.CompilerParams(vmem_limit_bytes=mib * 1024 * 1024),
+        cost_estimate=pl.CostEstimate(flops=1, transcendentals=0, bytes_accessed=1),
     )(*operands)
     return outs[0] if len(shapes) == 1 else outs
 
@@ -538,20 +539,21 @@
         out_sent, out_more = second_halves(plan, scale, out_sources, out_got)
         qkv_got, _ = lax.optimization_barrier((qkv_got, out_sent))
         qkv_sent, qkv_more = second_halves(plan, scale, qkv_sources, qkv_got)
+        out_more, _ = lax.optimization_barrier((out_more, qkv_sent))
+        out_share = shares(plan, scale, out_sources, out_got, out_more)
+        out_first = neighbours(out_share)
+        qkv_more, _ = lax.optimization_barrier((qkv_more, out_share))
         qkv_share = shares(plan, scale, qkv_sources, qkv_got, qkv_more)
         qkv_first = neighbours(qkv_share)
-        out_more, _ = lax.optimization_barrier((out_more, qkv_share))
-        out_share = shares(plan, scale, out_sources, out_got, out_more)
-        out_first = neighbours(out_share)
-        qkv_own = completed(qkv_share, *qkv_first)
+        out_first, _ = lax.optimization_barrier((out_first, qkv_share))
+        out_own = completed(out_share, *out_first)
+        out_peer = of_partner(out_own)
+        share, near, low, high, far = completed(qkv_share, *qkv_first)
+        low, high, _ = lax.optimization_barrier((low, high, out_peer))
+        qkv_own = (share, near, low, high, far)
         qkv_peer = of_partner(qkv_own)
     with jax.named_scope("layer"):
         queries, kv = projected(0, first)
-    with jax.named_scope("merge"):
-        out_first, _ = lax.optimization_barrier((out_first, queries))
-        out_own = completed(out_share, *out_first)
-        out_peer = of_partner(out_own)
-
     outs = []
     before = kv
     for t in range(sections + parts - 1):

time: 425 us -> 422 us (level)
  starting transfers between devices: 96 us -> 85.9 us
  waiting for transfers between devices: 94.3 us -> 102 us
    ppermute x31, starting transfers between devices: 55.4 us -> 45.3 us  [exchanged(): lax.ppermute(array, axis, [(i, i ^ mask) for i in range(lax.axis_size(axi...]
    ppermute x31, waiting for transfers between devices: 64.8 us -> 72.3 us  [exchanged(): lax.ppermute(array, axis, [(i, i ^ mask) for i in range(lax.axis_size(axi...]
  transfers between devices with their start and end apart: 41 -> 41, of which waited for: 22 -> 22; matrix products, arithmetic and copies ran while one was open for 0% -> 0% of each run, Pallas kernels for 6% -> 7%
where the time goes in v2:
time: 422 us; the launch traced here: 421 us
  blocking collectives  164 us (39%)
  waiting for transfers between devices  102 us (24%)
  starting transfers between devices  85.9 us (20%)
  Pallas kernels  60.4 us (14%)
    all_to_all x9, blocking collectives, spread(): lax.all_to_all(pieces, 'mp', 0, 0, tiled=True, axis_index_groups=groups)  164 us
    ppermute x31, waiting for transfers between devices, exchanged(): lax.ppermute(array, axis, [(i, i ^ mask) for i in range(lax.axis_size(axi...  72.3 us
    pallas_call x33, Pallas kernels, kernel_call(): pl.pallas_call(kernel, out_shape=tuple((result_on_chip(shape[:-1], F32) i...  60.4 us
    ppermute x31, starting transfers between devices, exchanged(): lax.ppermute(array, axis, [(i, i ^ mask) for i in range(lax.axis_size(axi...  45.3 us
    ppermute x4, starting transfers between devices, per_device(): lax.ppermute(outs[-1], 'section', [(i, i + 1) for i in range(sections - 1)])  14.2 us
    all_to_all x1, waiting for transfers between devices, spread(): lax.all_to_all(pieces, 'mp', 0, 0, tiled=True, axis_index_groups=groups)  14 us
    ppermute x4, starting transfers between devices, over_mp(): return lax.ppermute(array, 'mp', pairs)  13.2 us
    ppermute x4, waiting for transfers between devices, over_mp(): return lax.ppermute(array, 'mp', pairs)  10.5 us
  transfers between devices with their start and end apart: 41, of which 22 were waited for; matrix products, arithmetic and copies ran while one was open for 0% of the time, Pallas kernels for 7%

profile of v2, /device:TPU:1, one launch (start us, length us, event | category | flops | bytes accessed | tf_op | source)
XLA Modules:
  0.0 420.7 jit_solution(5923073403983952487)
XLA Ops:
  13.1 4.1 merge.14
  17.7 4.3 %merge.15 = bf16[2,2,896,256]{3,2,1,0:T(8,128)(2,1)} custom-call(s32[16]{0:T(128)S(1)} %stack.69.plan_ref, f32[1]{0:T(128)} %dynamic_slice.3.scale_ref, bf16[4,896,128]{2,1,0:T(8,128)(2,1)} %bitcast.101, bf16[4,896,128]{2,1,0:T(8,128)(2,1)} %bitcast.104, bf16[4,896,128]{2,1,0:T(8,128)(2,1)} %bitcast.107, bf16[4,896,128]{2,1,0:T(8,128)(2,1)} %bitcast.110), custom_call_target="tpu_custom_call" | custom-call | flops 1 | bytes 1 | tf_op jit(solution)/shard_map/merge/pallas_call | solution.py:32
  24.0 4.9 %collective-permute-start = (bf16[16,3584]{1,0:T(8,128)(2,1)S(1)}, bf16[16,3584]{1,0:T(8,128)(2,1)S(1)}, u32[]{:S(2)}, u32[]{:S(2)}) collective-permute-start(bf16[16,3584]{1,0:T(8,128)(2,1)S(1)} %get-tuple-element.43), channel_id=1, source_target_pairs={{0,0},{1,2},{2,4},{3,6},{4,8},{5,10},{6,12},{7,14},{8,1},{9,3},{10... | collective-permute-start | bytes 344072 | tf_op jit(solution)/shard_map/merge/ppermute | solution.py:520
  29.4 7.3 %collective-permute-done.s_ref = bf16[16,3584]{1,0:T(8,128)(2,1)S(1)} collective-permute-done((bf16[16,3584]{1,0:T(8,128)(2,1)S(1)}, bf16[16,3584]{1,0:T(8,128)(2,1)S(1)}, u32[]{:S(2)}, u32[]{:S(2)}) %collective-permute-start) | collective-permute-done | bytes 114720 | tf_op jit(solution)/shard_map/merge/ppermute | solution.py:520
  41.3 9.5 %all-to-all-start = ((bf16[8,8,3584]{2,1,0:T(8,128)(2,1)}), bf16[8,8,3584]{2,1,0:T(8,128)(2,1)S(1)}, u32[]{:S(2)}, u32[]{:S(2)}) async-start(bf16[8,8,3584]{2,1,0:T(8,128)(2,1)} %bitcast.79), calls=%async_computation | async-start | bytes 917504 | tf_op jit(solution)/shard_map/merge/all_to_all | solution.py:511
  50.8 14.0 %all-to-all-done = bf16[8,8,3584]{2,1,0:T(8,128)(2,1)S(1)} async-done(((bf16[8,8,3584]{2,1,0:T(8,128)(2,1)}), bf16[8,8,3584]{2,1,0:T(8,128)(2,1)S(1)}, u32[]{:S(2)}, u32[]{:S(2)}) %all-to-all-start) | async-done | bytes 458784 | tf_op jit(solution)/shard_map/merge/all_to_all | solution.py:511
  72.8 3.8 merge.21
  83.1 23.1 %collective-permute-done.9.refs_7_ = bf16[2,1,128,896]{3,2,1,0:T(8,128)(2,1)S(1)} collective-permute-done((bf16[2,1,128,896]{3,2,1,0:T(8,128)(2,1)S(1)}, bf16[2,1,128,896]{3,2,1,0:T(8,128)(2,1)S(1)}, u32[]{:S(2)}, u32[]{:S(2)}) %collective-permute-start.9) | collective-permute-done | bytes 458784 | tf_op jit(solution)/shard_map/merge/ppermute | solution.py:19
  106.2 4.0 collective-permute-done.8.refs_3_
  110.2 3.6 merge.22.refs_4_
  116.3 5.0 %merge.23.refs_0_ = bf16[2,896,256]{2,1,0:T(8,128)(2,1)S(1)} custom-call(s32[16]{0:T(128)S(1)} %stack.69.plan_ref, f32[1]{0:T(128)} %dynamic_slice.3.scale_ref, bf16[4,896,256]{2,1,0:T(8,128)(2,1)} %bitcast.97, bf16[4,896,256]{2,1,0:T(8,128)(2,1)} %bitcast.100, bf16[2,2,896,256]{3,2,1,0:T(8,128)(2,1)S(1)} %collective-permute-done.4.refs_2_, ...), custom_call_target="tpu_custom_call" | custom-call | flops 1 | bytes 1 | tf_op jit(solution)/shard_map/merge/pallas_call | solution.py:32
  123.0 3.8 collective-permute-start.14
  127.2 5.9 %collective-permute-start.17 = (bf16[2,128,896]{2,1,0:T(8,128)(2,1)S(1)}, bf16[2,128,896]{2,1,0:T(8,128)(2,1)S(1)}, u32[]{:S(2)}, u32[]{:S(2)}) collective-permute-start(bf16[2,128,896]{2,1,0:T(8,128)(2,1)S(1)} %collective-permute-done.15.refs_5_), channel_id=1, source_target_pairs={{0,1},{1,0},{2,3},{3,2},{4,5},{5,4},{6,7},{7,6},{8,9},{9,8},{10,11... | collective-permute-start | bytes 1376264 | tf_op jit(solution)/shard_map/merge/ppermute | solution.py:19
  133.1 16.8 %collective-permute-done.18.refs_6_ = bf16[128,896]{1,0:T(8,128)(2,1)S(1)} collective-permute-done((bf16[128,896]{1,0:T(8,128)(2,1)S(1)}, bf16[128,896]{1,0:T(8,128)(2,1)S(1)}, u32[]{:S(2)}, u32[]{:S(2)}) %collective-permute-start.18) | collective-permute-done | bytes 229408 | tf_op jit(solution)/shard_map/merge/ppermute | solution.py:19
  149.9 4.0 collective-permute-start.22
  154.2 8.1 %collective-permute-done.20.refs_7_ = bf16[128,896]{1,0:T(8,128)(2,1)S(1)} collective-permute-done((bf16[128,896]{1,0:T(8,128)(2,1)S(1)}, bf16[128,896]{1,0:T(8,128)(2,1)S(1)}, u32[]{:S(2)}, u32[]{:S(2)}) %collective-permute-start.20) | collective-permute-done | bytes 229408 | tf_op jit(solution)/shard_map/merge/ppermute | solution.py:19
  164.9 9.8 %collective-permute-done.12.refs_2_ = bf16[896,256]{1,0:T(8,128)(2,1)S(1)} collective-permute-done((bf16[896,256]{1,0:T(8,128)(2,1)S(1)}, bf16[896,256]{1,0:T(8,128)(2,1)S(1)}, u32[]{:S(2)}, u32[]{:S(2)}) %collective-permute-start.12) | collective-permute-done | bytes 458784 | tf_op jit(solution)/shard_map/merge/ppermute | solution.py:19
  184.8 23.3 %all_to_all.55 = bf16[8,8,3584]{2,1,0:T(8,128)(2,1)S(1)} all-to-all(bf16[8,8,3584]{2,1,0:T(8,128)(2,1)S(1)} %bitcast.65), channel_id=1, replica_groups={{0,2,4,6,8,10,12,14},{1,3,5,7,9,11,13,15},{16,18,20,22,24,26,28,30},{17..., dimensions={0} | all-to-all | bytes 917504 | tf_op jit(solution)/shard_map/layer/all_to_all | solution.py:511
  213.4 15.1 %all_to_all.56 = bf16[8,8,3584]{2,1,0:T(8,128)(2,1)S(1)} all-to-all(bf16[8,8,3584]{2,1,0:T(8,128)(2,1)S(1)} %bitcast.80), channel_id=1, replica_groups={{0,2,4,6,8,10,12,14},{1,3,5,7,9,11,13,15},{16,18,20,22,24,26,28,30},{17..., dimensions={0} | all-to-all | bytes 917504 | tf_op jit(solution)/shard_map/layer/all_to_all | solution.py:511
  230.4 4.5 %collective-permute-start.30 = (bf16[64,512]{1,0:T(8,128)(2,1)S(1)}, bf16[64,512]{1,0:T(8,128)(2,1)S(1)}, u32[]{:S(2)}, u32[]{:S(2)}) collective-permute-start(bf16[64,512]{1,0:T(8,128)(2,1)S(1)} %get-tuple-element.67.refs_2_.refs_0_), channel_id=1, source_target_pairs={{0,1},{1,0},{2,3},{3,2},{4,5},{5,4},{6,7},{7,6},{8,9},{9,8},{10,11... | collective-permute-start | bytes 196616 | tf_op jit(solution)/shard_map/layer/ppermute | solution.py:19
  237.7 19.0 %all_to_all.57 = bf16[8,8,3584]{2,1,0:T(8,128)(2,1)S(1)} all-to-all(bf16[8,8,3584]{2,1,0:T(8,128)(2,1)S(1)} %bitcast.62), channel_id=1, replica_groups={{0,2,4,6,8,10,12,14},{1,3,5,7,9,11,13,15},{16,18,20,22,24,26,28,30},{17..., dimensions={0} | all-to-all | bytes 917504 | tf_op jit(solution)/shard_map/layer/all_to_all | solution.py:511
  256.8 3.7 collective-permute-start.31
  261.9 16.6 %all_to_all.58 = bf16[8,8,3584]{2,1,0:T(8,128)(2,1)S(1)} all-to-all(bf16[8,8,3584]{2,1,0:T(8,128)(2,1)S(1)} %bitcast.72), channel_id=1, replica_groups={{0,2,4,6,8,10,12,14},{1,3,5,7,9,11,13,15},{16,18,20,22,24,26,28,30},{17..., dimensions={0} | all-to-all | bytes 917504 | tf_op jit(solution)/shard_map/layer/all_to_all | solution.py:511
  286.4 19.0 %all_to_all.59 = bf16[8,8,3584]{2,1,0:T(8,128)(2,1)S(1)} all-to-all(bf16[8,8,3584]{2,1,0:T(8,128)(2,1)S(1)} %bitcast.63), channel_id=1, replica_groups={{0,2,4,6,8,10,12,14},{1,3,5,7,9,11,13,15},{16,18,20,22,24,26,28,30},{17..., dimensions={0} | all-to-all | bytes 917504 | tf_op jit(solution)/shard_map/layer/all_to_all | solution.py:511
  305.6 3.7 collective-permute-start.33
  310.7 16.6 %all_to_all.60 = bf16[8,8,3584]{2,1,0:T(8,128)(2,1)S(1)} all-to-all(bf16[8,8,3584]{2,1,0:T(8,128)(2,1)S(1)} %bitcast.73), channel_id=1, replica_groups={{0,2,4,6,8,10,12,14},{1,3,5,7,9,11,13,15},{16,18,20,22,24,26,28,30},{17..., dimensions={0} | all-to-all | bytes 917504 | tf_op jit(solution)/shard_map/layer/all_to_all | solution.py:511
  334.9 19.0 %all_to_all.61 = bf16[8,8,3584]{2,1,0:T(8,128)(2,1)S(1)} all-to-all(bf16[8,8,3584]{2,1,0:T(8,128)(2,1)S(1)} %bitcast.64), channel_id=1, replica_groups={{0,2,4,6,8,10,12,14},{1,3,5,7,9,11,13,15},{16,18,20,22,24,26,28,30},{17..., dimensions={0} | all-to-all | bytes 917504 | tf_op jit(solution)/shard_map/layer/all_to_all | solution.py:511
  354.1 3.7 collective-permute-start.35
  359.2 16.6 %all_to_all.62 = bf16[8,8,3584]{2,1,0:T(8,128)(2,1)S(1)} all-to-all(bf16[8,8,3584]{2,1,0:T(8,128)(2,1)S(1)} %bitcast.71), channel_id=1, replica_groups={{0,2,4,6,8,10,12,14},{1,3,5,7,9,11,13,15},{16,18,20,22,24,26,28,30},{17..., dimensions={0} | all-to-all | bytes 917504 | tf_op jit(solution)/shard_map/layer/all_to_all | solution.py:511
  383.5 19.0 %all_to_all.63 = bf16[8,8,3584]{2,1,0:T(8,128)(2,1)S(1)} all-to-all(bf16[8,8,3584]{2,1,0:T(8,128)(2,1)S(1)} %bitcast.61), channel_id=1, replica_groups={{0,2,4,6,8,10,12,14},{1,3,5,7,9,11,13,15},{16,18,20,22,24,26,28,30},{17..., dimensions={0} | all-to-all | bytes 917504 | tf_op jit(solution)/shard_map/layer/all_to_all | solution.py:511
  404.0 3.7 all-to-all-start.10
  407.7 7.5 %collective-permute-start.37 = (bf16[8,3584]{1,0:T(8,128)(2,1)S(1)}, bf16[8,3584]{1,0:T(8,128)(2,1)S(1)}, u32[]{:S(2)}, u32[]{:S(2)}) collective-permute-start(bf16[8,3584]{1,0:T(8,128)(2,1)S(1)} %get-tuple-element.75), channel_id=1, source_target_pairs={{0,0},{2,1},{4,2},{6,3},{8,4},{10,5},{12,6},{14,7},{1,8},{3,9},{5,... | collective-permute-start | bytes 172040 | tf_op jit(solution)/shard_map/loss/ppermute | solution.py:520
  (125 shorter events, 94.4 us)
Async XLA Ops:
  5.6 45.2 %collective-permute-start.2 = (bf16[2,2,128,896]{3,2,1,0:T(8,128)(2,1)}, bf16[2,2,128,896]{3,2,1,0:T(8,128)(2,1)S(1)}, u32[]{:S(2)}, u32[]{:S(2)}) collective-permute-start(bf16[2,2,128,896]{3,2,1,0:T(8,128)(2,1)} %merge.12), channel_id=1, source_target_pairs={{0,16},{16,0},{32,48},{48,32},{1,17},{17,1},{33,49},{49,33},{2,18}... | collective-permute-start | bytes 2752520 | tf_op jit(solution)/shard_map/merge/ppermute | solution.py:19
  11.2 39.5 %collective-permute-start.3 = (bf16[2,2,128,896]{3,2,1,0:T(8,128)(2,1)}, bf16[2,2,128,896]{3,2,1,0:T(8,128)(2,1)}, u32[]{:S(2)}, u32[]{:S(2)}) collective-permute-start(bf16[2,2,128,896]{3,2,1,0:T(8,128)(2,1)} %merge.13), channel_id=1, source_target_pairs={{0,48},{16,32},{32,16},{48,0},{1,49},{17,33},{33,17},{49,1},{2,50}... | collective-permute-start | bytes 2752520 | tf_op jit(solution)/shard_map/merge/ppermute | solution.py:19
  17.3 53.0 %collective-permute-start.4 = (bf16[2,2,896,256]{3,2,1,0:T(8,128)(2,1)}, bf16[2,2,896,256]{3,2,1,0:T(8,128)(2,1)S(1)}, u32[]{:S(2)}, u32[]{:S(2)}) collective-permute-start(bf16[2,2,896,256]{3,2,1,0:T(8,128)(2,1)} %merge.14), channel_id=1, source_target_pairs={{0,16},{16,0},{32,48},{48,32},{1,17},{17,1},{33,49},{49,33},{2,18}... | collective-permute-start | bytes 5505032 | tf_op jit(solution)/shard_map/merge/ppermute | solution.py:19
  22.0 50.8 %collective-permute-start.5 = (bf16[2,2,896,256]{3,2,1,0:T(8,128)(2,1)}, bf16[2,2,896,256]{3,2,1,0:T(8,128)(2,1)}, u32[]{:S(2)}, u32[]{:S(2)}) collective-permute-start(bf16[2,2,896,256]{3,2,1,0:T(8,128)(2,1)} %merge.15), channel_id=1, source_target_pairs={{0,48},{16,32},{32,16},{48,0},{1,49},{17,33},{33,17},{49,1},{2,50}... | collective-permute-start | bytes 5505032 | tf_op jit(solution)/shard_map/merge/ppermute | solution.py:19
  24.0 12.7 %collective-permute-start = (bf16[16,3584]{1,0:T(8,128)(2,1)S(1)}, bf16[16,3584]{1,0:T(8,128)(2,1)S(1)}, u32[]{:S(2)}, u32[]{:S(2)}) collective-permute-start(bf16[16,3584]{1,0:T(8,128)(2,1)S(1)} %get-tuple-element.43), channel_id=1, source_target_pairs={{0,0},{1,2},{2,4},{3,6},{4,8},{5,10},{6,12},{7,14},{8,1},{9,3},{10... | collective-permute-start | bytes 344072 | tf_op jit(solution)/shard_map/merge/ppermute | solution.py:520
  41.3 23.5 %all-to-all-start = ((bf16[8,8,3584]{2,1,0:T(8,128)(2,1)}), bf16[8,8,3584]{2,1,0:T(8,128)(2,1)S(1)}, u32[]{:S(2)}, u32[]{:S(2)}) async-start(bf16[8,8,3584]{2,1,0:T(8,128)(2,1)} %bitcast.79), calls=%async_computation | async-start | bytes 917504 | tf_op jit(solution)/shard_map/merge/all_to_all | solution.py:511
  76.6 39.8 %collective-permute-start.7 = (bf16[2,1,896,256]{3,2,1,0:T(8,128)(2,1)S(1)}, bf16[2,1,896,256]{3,2,1,0:T(8,128)(2,1)S(1)}, u32[]{:S(2)}, u32[]{:S(2)}) collective-permute-start(bf16[2,1,896,256]{3,2,1,0:T(8,128)(2,1)S(1)} %merge.21), channel_id=1, source_target_pairs={{0,16},{16,0},{32,48},{48,32},{1,17},{17,1},{33,49},{49,33},{2,18}... | collective-permute-start | bytes 2752520 | tf_op jit(solution)/shard_map/merge/ppermute | solution.py:19
  79.4 36.9 %collective-permute-start.6 = (bf16[2,1,896,256]{3,2,1,0:T(8,128)(2,1)S(1)}, bf16[2,1,896,256]{3,2,1,0:T(8,128)(2,1)S(1)}, u32[]{:S(2)}, u32[]{:S(2)}) collective-permute-start(bf16[2,1,896,256]{3,2,1,0:T(8,128)(2,1)S(1)} %merge.20), channel_id=1, source_target_pairs={{0,48},{16,32},{32,16},{48,0},{1,49},{17,33},{33,17},{49,1},{2,50}... | collective-permute-start | bytes 2752520 | tf_op jit(solution)/shard_map/merge/ppermute | solution.py:19
  81.6 24.6 %collective-permute-start.9 = (bf16[2,1,128,896]{3,2,1,0:T(8,128)(2,1)S(1)}, bf16[2,1,128,896]{3,2,1,0:T(8,128)(2,1)S(1)}, u32[]{:S(2)}, u32[]{:S(2)}) collective-permute-start(bf16[2,1,128,896]{3,2,1,0:T(8,128)(2,1)S(1)} %merge.19), channel_id=1, source_target_pairs={{0,16},{16,0},{32,48},{48,32},{1,17},{17,1},{33,49},{49,33},{2,18}... | collective-permute-start | bytes 1376264 | tf_op jit(solution)/shard_map/merge/ppermute | solution.py:19
  82.4 27.8 %collective-permute-start.8 = (bf16[2,1,128,896]{3,2,1,0:T(8,128)(2,1)S(1)}, bf16[2,1,128,896]{3,2,1,0:T(8,128)(2,1)S(1)}, u32[]{:S(2)}, u32[]{:S(2)}) collective-permute-start(bf16[2,1,128,896]{3,2,1,0:T(8,128)(2,1)S(1)} %merge.18), channel_id=1, source_target_pairs={{0,48},{16,32},{32,16},{48,0},{1,49},{17,33},{33,17},{49,1},{2,50}... | collective-permute-start | bytes 1376264 | tf_op jit(solution)/shard_map/merge/ppermute | solution.py:19
  113.9 12.9 %collective-permute-start.16 = (bf16[2,128,896]{2,1,0:T(8,128)(2,1)S(1)}, bf16[2,128,896]{2,1,0:T(8,128)(2,1)S(1)}, u32[]{:S(2)}, u32[]{:S(2)}) collective-permute-start(bf16[2,128,896]{2,1,0:T(8,128)(2,1)S(1)} %merge.22.refs_4_), channel_id=1, source_target_pairs={{0,48},{16,32},{32,16},{48,0},{1,49},{17,33},{33,17},{49,1},{2,50}... | collective-permute-start | bytes 1376264 | tf_op jit(solution)/shard_map/merge/ppermute | solution.py:19
  116.3 10.4 %collective-permute-start.15 = (bf16[2,128,896]{2,1,0:T(8,128)(2,1)S(1)}, bf16[2,128,896]{2,1,0:T(8,128)(2,1)S(1)}, u32[]{:S(2)}, u32[]{:S(2)}) collective-permute-start(bf16[2,128,896]{2,1,0:T(8,128)(2,1)S(1)} %merge.22.refs_4_), channel_id=1, source_target_pairs={{0,16},{16,0},{32,48},{48,32},{1,17},{17,1},{33,49},{49,33},{2,18}... | collective-permute-start | bytes 1376264 | tf_op jit(solution)/shard_map/merge/ppermute | solution.py:19
  121.3 32.5 %collective-permute-start.11 = (bf16[2,896,256]{2,1,0:T(8,128)(2,1)S(1)}, bf16[2,896,256]{2,1,0:T(8,128)(2,1)S(1)}, u32[]{:S(2)}, u32[]{:S(2)}) collective-permute-start(bf16[2,896,256]{2,1,0:T(8,128)(2,1)S(1)} %merge.23.refs_0_), channel_id=1, source_target_pairs={{0,48},{16,32},{32,16},{48,0},{1,49},{17,33},{33,17},{49,1},{2,50}... | collective-permute-start | bytes 2752520 | tf_op jit(solution)/shard_map/merge/ppermute | solution.py:19
  121.7 41.4 %collective-permute-start.10 = (bf16[2,896,256]{2,1,0:T(8,128)(2,1)S(1)}, bf16[2,896,256]{2,1,0:T(8,128)(2,1)S(1)}, u32[]{:S(2)}, u32[]{:S(2)}) collective-permute-start(bf16[2,896,256]{2,1,0:T(8,128)(2,1)S(1)} %merge.23.refs_0_), channel_id=1, source_target_pairs={{0,16},{16,0},{32,48},{48,32},{1,17},{17,1},{33,49},{49,33},{2,18}... | collective-permute-start | bytes 2752520 | tf_op jit(solution)/shard_map/merge/ppermute | solution.py:19
  123.0 40.2 %collective-permute-start.14 = (bf16[2,128,896]{2,1,0:T(8,128)(2,1)S(1)}, bf16[2,128,896]{2,1,0:T(8,128)(2,1)S(1)}, u32[]{:S(2)}, u32[]{:S(2)}) collective-permute-start(bf16[2,128,896]{2,1,0:T(8,128)(2,1)S(1)} %merge.22.refs_4_), channel_id=1, source_target_pairs={{0,1},{1,0},{2,3},{3,2},{4,5},{5,4},{6,7},{7,6},{8,9},{9,8},{10,11... | collective-permute-start | bytes 1376264 | tf_op jit(solution)/shard_map/merge/ppermute | solution.py:19
  126.8 23.1 %collective-permute-start.18 = (bf16[128,896]{1,0:T(8,128)(2,1)S(1)}, bf16[128,896]{1,0:T(8,128)(2,1)S(1)}, u32[]{:S(2)}, u32[]{:S(2)}) collective-permute-start(bf16[128,896]{1,0:T(8,128)(2,1)S(1)} %slice_bitcast_fusion.3), channel_id=1, source_target_pairs={{0,16},{16,0},{32,48},{48,32},{1,17},{17,1},{33,49},{49,33},{2,18}... | collective-permute-start | bytes 688136 | tf_op jit(solution)/shard_map/merge/ppermute | solution.py:19
  127.2 36.0 %collective-permute-start.17 = (bf16[2,128,896]{2,1,0:T(8,128)(2,1)S(1)}, bf16[2,128,896]{2,1,0:T(8,128)(2,1)S(1)}, u32[]{:S(2)}, u32[]{:S(2)}) collective-permute-start(bf16[2,128,896]{2,1,0:T(8,128)(2,1)S(1)} %collective-permute-done.15.refs_5_), channel_id=1, source_target_pairs={{0,1},{1,0},{2,3},{3,2},{4,5},{5,4},{6,7},{7,6},{8,9},{9,8},{10,11... | collective-permute-start | bytes 1376264 | tf_op jit(solution)/shard_map/merge/ppermute | solution.py:19
  149.9 13.8 %collective-permute-start.22 = (bf16[2,128,896]{2,1,0:T(8,128)(2,1)S(1)}, bf16[2,128,896]{2,1,0:T(8,128)(2,1)S(1)}, u32[]{:S(2)}, u32[]{:S(2)}) collective-permute-start(bf16[2,128,896]{2,1,0:T(8,128)(2,1)S(1)} %collective-permute-done.16.refs_8_), channel_id=1, source_target_pairs={{0,1},{1,0},{2,3},{3,2},{4,5},{5,4},{6,7},{7,6},{8,9},{9,8},{10,11... | collective-permute-start | bytes 1376264 | tf_op jit(solution)/shard_map/merge/ppermute | solution.py:19
  153.8 8.4 %collective-permute-start.20 = (bf16[128,896]{1,0:T(8,128)(2,1)S(1)}, bf16[128,896]{1,0:T(8,128)(2,1)S(1)}, u32[]{:S(2)}, u32[]{:S(2)}) collective-permute-start(bf16[128,896]{1,0:T(8,128)(2,1)S(1)} %slice_bitcast_fusion.2), channel_id=1, source_target_pairs={{0,48},{16,32},{32,16},{48,0},{1,49},{17,33},{33,17},{49,1},{2,50}... | collective-permute-start | bytes 688136 | tf_op jit(solution)/shard_map/merge/ppermute | solution.py:19
  163.1 11.7 %collective-permute-start.12 = (bf16[896,256]{1,0:T(8,128)(2,1)S(1)}, bf16[896,256]{1,0:T(8,128)(2,1)S(1)}, u32[]{:S(2)}, u32[]{:S(2)}) collective-permute-start(bf16[896,256]{1,0:T(8,128)(2,1)S(1)} %slice_bitcast_fusion.1), channel_id=1, source_target_pairs={{0,16},{16,0},{32,48},{48,32},{1,17},{17,1},{33,49},{49,33},{2,18}... | collective-permute-start | bytes 1376264 | tf_op jit(solution)/shard_map/merge/ppermute | solution.py:19
  163.2 12.9 %collective-permute-start.13 = (bf16[896,256]{1,0:T(8,128)(2,1)S(1)}, bf16[896,256]{1,0:T(8,128)(2,1)S(1)}, u32[]{:S(2)}, u32[]{:S(2)}) collective-permute-start(bf16[896,256]{1,0:T(8,128)(2,1)S(1)} %slice_bitcast_fusion), channel_id=1, source_target_pairs={{0,48},{16,32},{32,16},{48,0},{1,49},{17,33},{33,17},{49,1},{2,50}... | collective-permute-start | bytes 1376264 | tf_op jit(solution)/shard_map/merge/ppermute | solution.py:19
  163.6 13.8 %collective-permute-start.23 = (bf16[2,896,256]{2,1,0:T(8,128)(2,1)S(1)}, bf16[2,896,256]{2,1,0:T(8,128)(2,1)S(1)}, u32[]{:S(2)}, u32[]{:S(2)}) collective-permute-start(bf16[2,896,256]{2,1,0:T(8,128)(2,1)S(1)} %merge.23.refs_0_), channel_id=1, source_target_pairs={{0,1},{1,0},{2,3},{3,2},{4,5},{5,4},{6,7},{7,6},{8,9},{9,8},{10,11... | collective-permute-start | bytes 2752520 | tf_op jit(solution)/shard_map/merge/ppermute | solution.py:19
  164.4 13.0 %collective-permute-start.27 = (bf16[2,896,256]{2,1,0:T(8,128)(2,1)S(1)}, bf16[2,896,256]{2,1,0:T(8,128)(2,1)S(1)}, u32[]{:S(2)}, u32[]{:S(2)}) collective-permute-start(bf16[2,896,256]{2,1,0:T(8,128)(2,1)S(1)} %collective-permute-done.11.refs_4_), channel_id=1, source_target_pairs={{0,1},{1,0},{2,3},{3,2},{4,5},{5,4},{6,7},{7,6},{8,9},{9,8},{10,11... | collective-permute-start | bytes 2752520 | tf_op jit(solution)/shard_map/merge/ppermute | solution.py:19
  164.6 12.9 %collective-permute-start.24 = (bf16[2,896,256]{2,1,0:T(8,128)(2,1)S(1)}, bf16[2,896,256]{2,1,0:T(8,128)(2,1)S(1)}, u32[]{:S(2)}, u32[]{:S(2)}) collective-permute-start(bf16[2,896,256]{2,1,0:T(8,128)(2,1)S(1)} %collective-permute-done.10.refs_1_), channel_id=1, source_target_pairs={{0,1},{1,0},{2,3},{3,2},{4,5},{5,4},{6,7},{7,6},{8,9},{9,8},{10,11... | collective-permute-start | bytes 2752520 | tf_op jit(solution)/shard_map/merge/ppermute | solution.py:19
  208.3 4.4 %collective-permute-start.29 = (bf16[8,3584]{1,0:T(8,128)(2,1)S(1)}, bf16[8,3584]{1,0:T(8,128)(2,1)S(1)}, u32[]{:S(2)}, u32[]{:S(2)}) collective-permute-start(bf16[8,3584]{1,0:T(8,128)(2,1)S(1)} %layer.21.refs_0_), channel_id=1, source_target_pairs={{0,64},{64,128},{128,192},{1,65},{65,129},{129,193},{2,66},{66,130... | collective-permute-start | bytes 172040 | tf_op jit(solution)/shard_map/layer/ppermute | solution.py:562
  230.4 5.4 %collective-permute-start.30 = (bf16[64,512]{1,0:T(8,128)(2,1)S(1)}, bf16[64,512]{1,0:T(8,128)(2,1)S(1)}, u32[]{:S(2)}, u32[]{:S(2)}) collective-permute-start(bf16[64,512]{1,0:T(8,128)(2,1)S(1)} %get-tuple-element.67.refs_2_.refs_0_), channel_id=1, source_target_pairs={{0,1},{1,0},{2,3},{3,2},{4,5},{5,4},{6,7},{7,6},{8,9},{9,8},{10,11... | collective-permute-start | bytes 196616 | tf_op jit(solution)/shard_map/layer/ppermute | solution.py:19
  256.8 4.9 %collective-permute-start.31 = (bf16[8,3584]{1,0:T(8,128)(2,1)S(1)}, bf16[8,3584]{1,0:T(8,128)(2,1)S(1)}, u32[]{:S(2)}, u32[]{:S(2)}) collective-permute-start(bf16[8,3584]{1,0:T(8,128)(2,1)S(1)} %layer.25.refs_1_.refs_4_), channel_id=1, source_target_pairs={{0,64},{64,128},{128,192},{1,65},{65,129},{129,193},{2,66},{66,130... | collective-permute-start | bytes 172040 | tf_op jit(solution)/shard_map/layer/ppermute | solution.py:562
  280.5 4.1 collective-permute-start.32
  305.6 4.9 %collective-permute-start.33 = (bf16[8,3584]{1,0:T(8,128)(2,1)S(1)}, bf16[8,3584]{1,0:T(8,128)(2,1)S(1)}, u32[]{:S(2)}, u32[]{:S(2)}) collective-permute-start(bf16[8,3584]{1,0:T(8,128)(2,1)S(1)} %layer.29.refs_2_.refs_5_), channel_id=1, source_target_pairs={{0,64},{64,128},{128,192},{1,65},{65,129},{129,193},{2,66},{66,130... | collective-permute-start | bytes 172040 | tf_op jit(solution)/shard_map/layer/ppermute | solution.py:562
  354.1 4.9 %collective-permute-start.35 = (bf16[8,3584]{1,0:T(8,128)(2,1)S(1)}, bf16[8,3584]{1,0:T(8,128)(2,1)S(1)}, u32[]{:S(2)}, u32[]{:S(2)}) collective-permute-start(bf16[8,3584]{1,0:T(8,128)(2,1)S(1)} %layer.33.refs_3_.refs_6_), channel_id=1, source_target_pairs={{0,64},{64,128},{128,192},{1,65},{65,129},{129,193},{2,66},{66,130... | collective-permute-start | bytes 172040 | tf_op jit(solution)/shard_map/layer/ppermute | solution.py:562
  404.0 11.3 %all-to-all-start.10 = ((f32[16,1,128]{2,1,0:T(1,128)}), f32[16,1,128]{2,1,0:T(1,128)S(1)}, u32[]{:S(2)}, u32[]{:S(2)}) async-start(f32[16,1,128]{2,1,0:T(1,128)} %get-tuple-element.77), calls=%async_computation.10 | async-start | bytes 16384 | tf_op jit(solution)/shard_map/loss/all_to_all | solution.py:577
  407.7 8.9 %collective-permute-start.37 = (bf16[8,3584]{1,0:T(8,128)(2,1)S(1)}, bf16[8,3584]{1,0:T(8,128)(2,1)S(1)}, u32[]{:S(2)}, u32[]{:S(2)}) collective-permute-start(bf16[8,3584]{1,0:T(8,128)(2,1)S(1)} %get-tuple-element.75), channel_id=1, source_target_pairs={{0,0},{2,1},{4,2},{6,3},{8,4},{10,5},{12,6},{14,7},{1,8},{3,9},{5,... | collective-permute-start | bytes 172040 | tf_op jit(solution)/shard_map/loss/ppermute | solution.py:520
  (15 other events, 77.5 us)

commit v3 on v1

--- a/solution.py
+++ b/solution.py
@@ -39,6 +39,7 @@
         out_specs=tuple(pl.BlockSpec(memory_space=VMEM) for _ in shapes),
         scratch_shapes=scratch,
         compiler_params=pltpu.CompilerParams(vmem_limit_bytes=mib * 1024 * 1024),
+        cost_estimate=pl.CostEstimate(flops=1, transcendentals=0, bytes_accessed=1),
     )(*operands)
     return outs[0] if len(shapes) == 1 else outs
 
@@ -368,10 +369,12 @@
 
 
 def second_halves(plan, scale, sources, got):
-    sent = [
-        share_call(plan, scale, [(s, 8 * i + 2, ((got[i], 8 * i + 3),))], 1, False)
-        for i, s in enumerate(sources)
-    ]
+    sent = []
+    for i, s in enumerate(sources):
+        mine = got[i]
+        if sent:
+            mine, _ = lax.optimization_barrier((mine, sent[0]))
+        sent.append(share_call(plan, scale, [(s, 8 * i + 2, ((mine, 8 * i + 3),))], 1, False))
     return sent, [exchanged(s, "task", (FAR, NEAR)[i]) for i, s in enumerate(sent)]
 
 
@@ -538,20 +541,20 @@
         out_sent, out_more = second_halves(plan, scale, out_sources, out_got)
         qkv_got, _ = lax.optimization_barrier((qkv_got, out_sent))
         qkv_sent, qkv_more = second_halves(plan, scale, qkv_sources, qkv_got)
+        qkv_more, out_more = lax.optimization_barrier((qkv_more, out_more))
         qkv_share = shares(plan, scale, qkv_sources, qkv_got, qkv_more)
         qkv_first = neighbours(qkv_share)
         out_more, _ = lax.optimization_barrier((out_more, qkv_share))
         out_share = shares(plan, scale, out_sources, out_got, out_more)
         out_first = neighbours(out_share)
-        qkv_own = completed(qkv_share, *qkv_first)
+        share, near, low, high, far = completed(qkv_share, *qkv_first)
+        out_first, low, high = lax.optimization_barrier((out_first, low, high))
+        qkv_own = (share, near, low, high, far)
         qkv_peer = of_partner(qkv_own)
+        out_own = completed(out_share, *out_first)
+        out_peer = of_partner(out_own)
     with jax.named_scope("layer"):
         queries, kv = projected(0, first)
-    with jax.named_scope("merge"):
-        out_first, _ = lax.optimization_barrier((out_first, queries))
-        out_own = completed(out_share, *out_first)
-        out_peer = of_partner(out_own)
-
     outs = []
     before = kv
     for t in range(sections + parts - 1):

time: 425 us -> 413 us (0.972)
  waiting for transfers between devices: 94.3 us -> 79.7 us
    ppermute x31, waiting for transfers between devices: 64.8 us -> 50.2 us  [exchanged(): lax.ppermute(array, axis, [(i, i ^ mask) for i in range(lax.axis_size(axi...]
  transfers between devices with their start and end apart: 41 -> 41, of which waited for: 22 -> 20; matrix products, arithmetic and copies ran while one was open for 0% -> 0% of each run, Pallas kernels for 6% -> 6%
where the time goes in v3:
time: 413 us; the launch traced here: 412 us
  blocking collectives  167 us (40%)
  starting transfers between devices  96.3 us (23%)
  waiting for transfers between devices  79.7 us (19%)
  Pallas kernels  60.4 us (15%)
    all_to_all x9, blocking collectives, spread(): lax.all_to_all(pieces, 'mp', 0, 0, tiled=True, axis_index_groups=groups)  167 us
    pallas_call x33, Pallas kernels, kernel_call(): pl.pallas_call(kernel, out_shape=tuple((result_on_chip(shape[:-1], F32) i...  60.4 us
    ppermute x31, starting transfers between devices, exchanged(): lax.ppermute(array, axis, [(i, i ^ mask) for i in range(lax.axis_size(axi...  55.7 us
    ppermute x31, waiting for transfers between devices, exchanged(): lax.ppermute(array, axis, [(i, i ^ mask) for i in range(lax.axis_size(axi...  50.2 us
    ppermute x4, starting transfers between devices, per_device(): lax.ppermute(outs[-1], 'section', [(i, i + 1) for i in range(sections - 1)])  14.2 us
    all_to_all x1, waiting for transfers between devices, spread(): lax.all_to_all(pieces, 'mp', 0, 0, tiled=True, axis_index_groups=groups)  14 us
    ppermute x4, starting transfers between devices, over_mp(): return lax.ppermute(array, 'mp', pairs)  13.2 us
    ppermute x4, waiting for transfers between devices, over_mp(): return lax.ppermute(array, 'mp', pairs)  10.5 us
  transfers between devices with their start and end apart: 41, of which 20 were waited for; matrix products, arithmetic and copies ran while one was open for 0% of the time, Pallas kernels for 6%

profile of v3, /device:TPU:1, one launch (start us, length us, event | category | flops | bytes accessed | tf_op | source)
XLA Modules:
  0.0 411.6 jit_solution(7429951872287661607)
XLA Ops:
  2.1 3.5 merge.12
  7.7 3.5 merge.13
  13.1 4.2 %merge.14 = bf16[2,2,896,256]{3,2,1,0:T(8,128)(2,1)} custom-call(s32[16]{0:T(128)S(1)} %stack.69.plan_ref, f32[1]{0:T(128)} %dynamic_slice.3.scale_ref, bf16[4,896,256]{2,1,0:T(8,128)(2,1)} %bitcast.95, bf16[4,896,256]{2,1,0:T(8,128)(2,1)} %bitcast.98), custom_call_target="tpu_custom_call" | custom-call | flops 1 | bytes 1 | tf_op jit(solution)/shard_map/merge/pallas_call | solution.py:32
  17.7 4.2 %merge.15 = bf16[2,2,896,256]{3,2,1,0:T(8,128)(2,1)} custom-call(s32[16]{0:T(128)S(1)} %stack.69.plan_ref, f32[1]{0:T(128)} %dynamic_slice.3.scale_ref, bf16[4,896,128]{2,1,0:T(8,128)(2,1)} %bitcast.101, bf16[4,896,128]{2,1,0:T(8,128)(2,1)} %bitcast.104, bf16[4,896,128]{2,1,0:T(8,128)(2,1)} %bitcast.107, bf16[4,896,128]{2,1,0:T(8,128)(2,1)} %bitcast.110), custom_call_target="tpu_custom_call" | custom-call | flops 1 | bytes 1 | tf_op jit(solution)/shard_map/merge/pallas_call | solution.py:32
  24.1 4.9 %collective-permute-start = (bf16[16,3584]{1,0:T(8,128)(2,1)S(1)}, bf16[16,3584]{1,0:T(8,128)(2,1)S(1)}, u32[]{:S(2)}, u32[]{:S(2)}) collective-permute-start(bf16[16,3584]{1,0:T(8,128)(2,1)S(1)} %get-tuple-element.47), channel_id=1, source_target_pairs={{0,0},{1,2},{2,4},{3,6},{4,8},{5,10},{6,12},{7,14},{8,1},{9,3},{10... | collective-permute-start | bytes 344072 | tf_op jit(solution)/shard_map/merge/ppermute | solution.py:522
  29.4 7.3 %collective-permute-done.s_ref = bf16[16,3584]{1,0:T(8,128)(2,1)S(1)} collective-permute-done((bf16[16,3584]{1,0:T(8,128)(2,1)S(1)}, bf16[16,3584]{1,0:T(8,128)(2,1)S(1)}, u32[]{:S(2)}, u32[]{:S(2)}) %collective-permute-start) | collective-permute-done | bytes 114720 | tf_op jit(solution)/shard_map/merge/ppermute | solution.py:522
  41.3 9.5 %all-to-all-start = ((bf16[8,8,3584]{2,1,0:T(8,128)(2,1)}), bf16[8,8,3584]{2,1,0:T(8,128)(2,1)S(1)}, u32[]{:S(2)}, u32[]{:S(2)}) async-start(bf16[8,8,3584]{2,1,0:T(8,128)(2,1)} %bitcast.79), calls=%async_computation | async-start | bytes 917504 | tf_op jit(solution)/shard_map/merge/all_to_all | solution.py:513
  50.8 14.0 %all-to-all-done = bf16[8,8,3584]{2,1,0:T(8,128)(2,1)S(1)} async-done(((bf16[8,8,3584]{2,1,0:T(8,128)(2,1)}), bf16[8,8,3584]{2,1,0:T(8,128)(2,1)S(1)}, u32[]{:S(2)}, u32[]{:S(2)}) %all-to-all-start) | async-done | bytes 458784 | tf_op jit(solution)/shard_map/merge/all_to_all | solution.py:513
  75.5 3.8 merge.21
  83.0 26.0 %collective-permute-done.9.refs_7_ = bf16[2,1,128,896]{3,2,1,0:T(8,128)(2,1)S(1)} collective-permute-done((bf16[2,1,128,896]{3,2,1,0:T(8,128)(2,1)S(1)}, bf16[2,1,128,896]{3,2,1,0:T(8,128)(2,1)S(1)}, u32[]{:S(2)}, u32[]{:S(2)}) %collective-permute-start.9) | collective-permute-done | bytes 458784 | tf_op jit(solution)/shard_map/merge/ppermute | solution.py:19
  110.2 5.0 %merge.22.refs_0_ = bf16[2,896,256]{2,1,0:T(8,128)(2,1)S(1)} custom-call(s32[16]{0:T(128)S(1)} %stack.69.plan_ref, f32[1]{0:T(128)} %dynamic_slice.3.scale_ref, bf16[4,896,256]{2,1,0:T(8,128)(2,1)} %bitcast.97, bf16[4,896,256]{2,1,0:T(8,128)(2,1)} %bitcast.100, bf16[2,2,896,256]{3,2,1,0:T(8,128)(2,1)S(1)} %collective-permute-done.4.refs_2_, ...), custom_call_target="tpu_custom_call" | custom-call | flops 1 | bytes 1 | tf_op jit(solution)/shard_map/merge/pallas_call | solution.py:32
  117.7 3.6 merge.23.refs_4_
  123.0 12.3 %collective-permute-done.13.refs_4_ = bf16[2,896,256]{2,1,0:T(8,128)(2,1)S(1)} collective-permute-done((bf16[2,896,256]{2,1,0:T(8,128)(2,1)S(1)}, bf16[2,896,256]{2,1,0:T(8,128)(2,1)S(1)}, u32[]{:S(2)}, u32[]{:S(2)}) %collective-permute-start.13) | collective-permute-done | bytes 917536 | tf_op jit(solution)/shard_map/merge/ppermute | solution.py:19
  138.2 7.3 %collective-permute-start.16 = (bf16[2,896,256]{2,1,0:T(8,128)(2,1)S(1)}, bf16[2,896,256]{2,1,0:T(8,128)(2,1)S(1)}, u32[]{:S(2)}, u32[]{:S(2)}) collective-permute-start(bf16[2,896,256]{2,1,0:T(8,128)(2,1)S(1)} %merge.22.refs_0_), channel_id=1, source_target_pairs={{0,1},{1,0},{2,3},{3,2},{4,5},{5,4},{6,7},{7,6},{8,9},{9,8},{10,11... | collective-permute-start | bytes 2752520 | tf_op jit(solution)/shard_map/merge/ppermute | solution.py:19
  145.5 7.2 %collective-permute-start.20 = (bf16[2,896,256]{2,1,0:T(8,128)(2,1)S(1)}, bf16[2,896,256]{2,1,0:T(8,128)(2,1)S(1)}, u32[]{:S(2)}, u32[]{:S(2)}) collective-permute-start(bf16[2,896,256]{2,1,0:T(8,128)(2,1)S(1)} %collective-permute-done.13.refs_4_), channel_id=1, source_target_pairs={{0,1},{1,0},{2,3},{3,2},{4,5},{5,4},{6,7},{7,6},{8,9},{9,8},{10,11... | collective-permute-start | bytes 2752520 | tf_op jit(solution)/shard_map/merge/ppermute | solution.py:19
  157.8 4.0 collective-permute-start.18
  161.9 5.1 %collective-permute-start.19 = (bf16[896,256]{1,0:T(8,128)(2,1)S(1)}, bf16[896,256]{1,0:T(8,128)(2,1)S(1)}, u32[]{:S(2)}, u32[]{:S(2)}) collective-permute-start(bf16[896,256]{1,0:T(8,128)(2,1)S(1)} %collective-permute-done.15.refs_3_), channel_id=1, source_target_pairs={{0,1},{1,0},{2,3},{3,2},{4,5},{5,4},{6,7},{7,6},{8,9},{9,8},{10,11... | collective-permute-start | bytes 1376264 | tf_op jit(solution)/shard_map/merge/ppermute | solution.py:19
  174.5 24.5 %all_to_all.55 = bf16[8,8,3584]{2,1,0:T(8,128)(2,1)S(1)} all-to-all(bf16[8,8,3584]{2,1,0:T(8,128)(2,1)S(1)} %bitcast.65), channel_id=1, replica_groups={{0,2,4,6,8,10,12,14},{1,3,5,7,9,11,13,15},{16,18,20,22,24,26,28,30},{17..., dimensions={0} | all-to-all | bytes 917504 | tf_op jit(solution)/shard_map/layer/all_to_all | solution.py:513
  199.2 3.2 collective-permute-start.29
  204.3 16.5 %all_to_all.56 = bf16[8,8,3584]{2,1,0:T(8,128)(2,1)S(1)} all-to-all(bf16[8,8,3584]{2,1,0:T(8,128)(2,1)S(1)} %bitcast.80), channel_id=1, replica_groups={{0,2,4,6,8,10,12,14},{1,3,5,7,9,11,13,15},{16,18,20,22,24,26,28,30},{17..., dimensions={0} | all-to-all | bytes 917504 | tf_op jit(solution)/shard_map/layer/all_to_all | solution.py:513
  228.6 19.0 %all_to_all.57 = bf16[8,8,3584]{2,1,0:T(8,128)(2,1)S(1)} all-to-all(bf16[8,8,3584]{2,1,0:T(8,128)(2,1)S(1)} %bitcast.62), channel_id=1, replica_groups={{0,2,4,6,8,10,12,14},{1,3,5,7,9,11,13,15},{16,18,20,22,24,26,28,30},{17..., dimensions={0} | all-to-all | bytes 917504 | tf_op jit(solution)/shard_map/layer/all_to_all | solution.py:513
  247.7 3.7 collective-permute-start.31
  252.8 16.6 %all_to_all.58 = bf16[8,8,3584]{2,1,0:T(8,128)(2,1)S(1)} all-to-all(bf16[8,8,3584]{2,1,0:T(8,128)(2,1)S(1)} %bitcast.72), channel_id=1, replica_groups={{0,2,4,6,8,10,12,14},{1,3,5,7,9,11,13,15},{16,18,20,22,24,26,28,30},{17..., dimensions={0} | all-to-all | bytes 917504 | tf_op jit(solution)/shard_map/layer/all_to_all | solution.py:513
  277.3 19.0 %all_to_all.59 = bf16[8,8,3584]{2,1,0:T(8,128)(2,1)S(1)} all-to-all(bf16[8,8,3584]{2,1,0:T(8,128)(2,1)S(1)} %bitcast.63), channel_id=1, replica_groups={{0,2,4,6,8,10,12,14},{1,3,5,7,9,11,13,15},{16,18,20,22,24,26,28,30},{17..., dimensions={0} | all-to-all | bytes 917504 | tf_op jit(solution)/shard_map/layer/all_to_all | solution.py:513
  296.5 3.7 collective-permute-start.33
  301.6 16.6 %all_to_all.60 = bf16[8,8,3584]{2,1,0:T(8,128)(2,1)S(1)} all-to-all(bf16[8,8,3584]{2,1,0:T(8,128)(2,1)S(1)} %bitcast.73), channel_id=1, replica_groups={{0,2,4,6,8,10,12,14},{1,3,5,7,9,11,13,15},{16,18,20,22,24,26,28,30},{17..., dimensions={0} | all-to-all | bytes 917504 | tf_op jit(solution)/shard_map/layer/all_to_all | solution.py:513
  325.8 19.0 %all_to_all.61 = bf16[8,8,3584]{2,1,0:T(8,128)(2,1)S(1)} all-to-all(bf16[8,8,3584]{2,1,0:T(8,128)(2,1)S(1)} %bitcast.64), channel_id=1, replica_groups={{0,2,4,6,8,10,12,14},{1,3,5,7,9,11,13,15},{16,18,20,22,24,26,28,30},{17..., dimensions={0} | all-to-all | bytes 917504 | tf_op jit(solution)/shard_map/layer/all_to_all | solution.py:513
  345.0 3.7 collective-permute-start.35
  350.1 16.6 %all_to_all.62 = bf16[8,8,3584]{2,1,0:T(8,128)(2,1)S(1)} all-to-all(bf16[8,8,3584]{2,1,0:T(8,128)(2,1)S(1)} %bitcast.71), channel_id=1, replica_groups={{0,2,4,6,8,10,12,14},{1,3,5,7,9,11,13,15},{16,18,20,22,24,26,28,30},{17..., dimensions={0} | all-to-all | bytes 917504 | tf_op jit(solution)/shard_map/layer/all_to_all | solution.py:513
  374.4 19.0 %all_to_all.63 = bf16[8,8,3584]{2,1,0:T(8,128)(2,1)S(1)} all-to-all(bf16[8,8,3584]{2,1,0:T(8,128)(2,1)S(1)} %bitcast.61), channel_id=1, replica_groups={{0,2,4,6,8,10,12,14},{1,3,5,7,9,11,13,15},{16,18,20,22,24,26,28,30},{17..., dimensions={0} | all-to-all | bytes 917504 | tf_op jit(solution)/shard_map/layer/all_to_all | solution.py:513
  394.9 3.7 all-to-all-start.10
  398.6 7.5 %collective-permute-start.37 = (bf16[8,3584]{1,0:T(8,128)(2,1)S(1)}, bf16[8,3584]{1,0:T(8,128)(2,1)S(1)}, u32[]{:S(2)}, u32[]{:S(2)}) collective-permute-start(bf16[8,3584]{1,0:T(8,128)(2,1)S(1)} %get-tuple-element.83), channel_id=1, source_target_pairs={{0,0},{2,1},{4,2},{6,3},{8,4},{10,5},{12,6},{14,7},{1,8},{3,9},{5,... | collective-permute-start | bytes 172040 | tf_op jit(solution)/shard_map/loss/ppermute | solution.py:522
  (125 shorter events, 90.5 us)
Async XLA Ops:
  5.6 45.2 %collective-permute-start.2 = (bf16[2,2,128,896]{3,2,1,0:T(8,128)(2,1)}, bf16[2,2,128,896]{3,2,1,0:T(8,128)(2,1)S(1)}, u32[]{:S(2)}, u32[]{:S(2)}) collective-permute-start(bf16[2,2,128,896]{3,2,1,0:T(8,128)(2,1)} %merge.12), channel_id=1, source_target_pairs={{0,16},{16,0},{32,48},{48,32},{1,17},{17,1},{33,49},{49,33},{2,18}... | collective-permute-start | bytes 2752520 | tf_op jit(solution)/shard_map/merge/ppermute | solution.py:19
  11.2 39.6 %collective-permute-start.3 = (bf16[2,2,128,896]{3,2,1,0:T(8,128)(2,1)}, bf16[2,2,128,896]{3,2,1,0:T(8,128)(2,1)}, u32[]{:S(2)}, u32[]{:S(2)}) collective-permute-start(bf16[2,2,128,896]{3,2,1,0:T(8,128)(2,1)} %merge.13), channel_id=1, source_target_pairs={{0,48},{16,32},{32,16},{48,0},{1,49},{17,33},{33,17},{49,1},{2,50}... | collective-permute-start | bytes 2752520 | tf_op jit(solution)/shard_map/merge/ppermute | solution.py:19
  17.3 53.0 %collective-permute-start.4 = (bf16[2,2,896,256]{3,2,1,0:T(8,128)(2,1)}, bf16[2,2,896,256]{3,2,1,0:T(8,128)(2,1)S(1)}, u32[]{:S(2)}, u32[]{:S(2)}) collective-permute-start(bf16[2,2,896,256]{3,2,1,0:T(8,128)(2,1)} %merge.14), channel_id=1, source_target_pairs={{0,16},{16,0},{32,48},{48,32},{1,17},{17,1},{33,49},{49,33},{2,18}... | collective-permute-start | bytes 5505032 | tf_op jit(solution)/shard_map/merge/ppermute | solution.py:19
  22.0 50.8 %collective-permute-start.5 = (bf16[2,2,896,256]{3,2,1,0:T(8,128)(2,1)}, bf16[2,2,896,256]{3,2,1,0:T(8,128)(2,1)}, u32[]{:S(2)}, u32[]{:S(2)}) collective-permute-start(bf16[2,2,896,256]{3,2,1,0:T(8,128)(2,1)} %merge.15), channel_id=1, source_target_pairs={{0,48},{16,32},{32,16},{48,0},{1,49},{17,33},{33,17},{49,1},{2,50}... | collective-permute-start | bytes 5505032 | tf_op jit(solution)/shard_map/merge/ppermute | solution.py:19
  24.1 12.7 %collective-permute-start = (bf16[16,3584]{1,0:T(8,128)(2,1)S(1)}, bf16[16,3584]{1,0:T(8,128)(2,1)S(1)}, u32[]{:S(2)}, u32[]{:S(2)}) collective-permute-start(bf16[16,3584]{1,0:T(8,128)(2,1)S(1)} %get-tuple-element.47), channel_id=1, source_target_pairs={{0,0},{1,2},{2,4},{3,6},{4,8},{5,10},{6,12},{7,14},{8,1},{9,3},{10... | collective-permute-start | bytes 344072 | tf_op jit(solution)/shard_map/merge/ppermute | solution.py:522
  41.3 23.5 %all-to-all-start = ((bf16[8,8,3584]{2,1,0:T(8,128)(2,1)}), bf16[8,8,3584]{2,1,0:T(8,128)(2,1)S(1)}, u32[]{:S(2)}, u32[]{:S(2)}) async-start(bf16[8,8,3584]{2,1,0:T(8,128)(2,1)} %bitcast.79), calls=%async_computation | async-start | bytes 917504 | tf_op jit(solution)/shard_map/merge/all_to_all | solution.py:513
  79.3 30.9 %collective-permute-start.7 = (bf16[2,1,896,256]{3,2,1,0:T(8,128)(2,1)S(1)}, bf16[2,1,896,256]{3,2,1,0:T(8,128)(2,1)S(1)}, u32[]{:S(2)}, u32[]{:S(2)}) collective-permute-start(bf16[2,1,896,256]{3,2,1,0:T(8,128)(2,1)S(1)} %merge.21), channel_id=1, source_target_pairs={{0,16},{16,0},{32,48},{48,32},{1,17},{17,1},{33,49},{49,33},{2,18}... | collective-permute-start | bytes 2752520 | tf_op jit(solution)/shard_map/merge/ppermute | solution.py:19
  79.4 30.8 %collective-permute-start.6 = (bf16[2,1,896,256]{3,2,1,0:T(8,128)(2,1)S(1)}, bf16[2,1,896,256]{3,2,1,0:T(8,128)(2,1)S(1)}, u32[]{:S(2)}, u32[]{:S(2)}) collective-permute-start(bf16[2,1,896,256]{3,2,1,0:T(8,128)(2,1)S(1)} %merge.20), channel_id=1, source_target_pairs={{0,48},{16,32},{32,16},{48,0},{1,49},{17,33},{33,17},{49,1},{2,50}... | collective-permute-start | bytes 2752520 | tf_op jit(solution)/shard_map/merge/ppermute | solution.py:19
  81.6 27.3 %collective-permute-start.9 = (bf16[2,1,128,896]{3,2,1,0:T(8,128)(2,1)S(1)}, bf16[2,1,128,896]{3,2,1,0:T(8,128)(2,1)S(1)}, u32[]{:S(2)}, u32[]{:S(2)}) collective-permute-start(bf16[2,1,128,896]{3,2,1,0:T(8,128)(2,1)S(1)} %merge.19), channel_id=1, source_target_pairs={{0,16},{16,0},{32,48},{48,32},{1,17},{17,1},{33,49},{49,33},{2,18}... | collective-permute-start | bytes 1376264 | tf_op jit(solution)/shard_map/merge/ppermute | solution.py:19
  82.3 27.9 %collective-permute-start.8 = (bf16[2,1,128,896]{3,2,1,0:T(8,128)(2,1)S(1)}, bf16[2,1,128,896]{3,2,1,0:T(8,128)(2,1)S(1)}, u32[]{:S(2)}, u32[]{:S(2)}) collective-permute-start(bf16[2,1,128,896]{3,2,1,0:T(8,128)(2,1)S(1)} %merge.18), channel_id=1, source_target_pairs={{0,48},{16,32},{32,16},{48,0},{1,49},{17,33},{33,17},{49,1},{2,50}... | collective-permute-start | bytes 1376264 | tf_op jit(solution)/shard_map/merge/ppermute | solution.py:19
  115.2 20.1 %collective-permute-start.13 = (bf16[2,896,256]{2,1,0:T(8,128)(2,1)S(1)}, bf16[2,896,256]{2,1,0:T(8,128)(2,1)S(1)}, u32[]{:S(2)}, u32[]{:S(2)}) collective-permute-start(bf16[2,896,256]{2,1,0:T(8,128)(2,1)S(1)} %merge.22.refs_0_), channel_id=1, source_target_pairs={{0,48},{16,32},{32,16},{48,0},{1,49},{17,33},{33,17},{49,1},{2,50}... | collective-permute-start | bytes 2752520 | tf_op jit(solution)/shard_map/merge/ppermute | solution.py:19
  117.7 18.8 %collective-permute-start.10 = (bf16[2,896,256]{2,1,0:T(8,128)(2,1)S(1)}, bf16[2,896,256]{2,1,0:T(8,128)(2,1)S(1)}, u32[]{:S(2)}, u32[]{:S(2)}) collective-permute-start(bf16[2,896,256]{2,1,0:T(8,128)(2,1)S(1)} %merge.22.refs_0_), channel_id=1, source_target_pairs={{0,16},{16,0},{32,48},{48,32},{1,17},{17,1},{33,49},{49,33},{2,18}... | collective-permute-start | bytes 2752520 | tf_op jit(solution)/shard_map/merge/ppermute | solution.py:19
  121.3 24.2 %collective-permute-start.12 = (bf16[2,128,896]{2,1,0:T(8,128)(2,1)S(1)}, bf16[2,128,896]{2,1,0:T(8,128)(2,1)S(1)}, u32[]{:S(2)}, u32[]{:S(2)}) collective-permute-start(bf16[2,128,896]{2,1,0:T(8,128)(2,1)S(1)} %merge.23.refs_4_), channel_id=1, source_target_pairs={{0,48},{16,32},{32,16},{48,0},{1,49},{17,33},{33,17},{49,1},{2,50}... | collective-permute-start | bytes 1376264 | tf_op jit(solution)/shard_map/merge/ppermute | solution.py:19
  121.7 31.0 %collective-permute-start.11 = (bf16[2,128,896]{2,1,0:T(8,128)(2,1)S(1)}, bf16[2,128,896]{2,1,0:T(8,128)(2,1)S(1)}, u32[]{:S(2)}, u32[]{:S(2)}) collective-permute-start(bf16[2,128,896]{2,1,0:T(8,128)(2,1)S(1)} %merge.23.refs_4_), channel_id=1, source_target_pairs={{0,16},{16,0},{32,48},{48,32},{1,17},{17,1},{33,49},{49,33},{2,18}... | collective-permute-start | bytes 1376264 | tf_op jit(solution)/shard_map/merge/ppermute | solution.py:19
  135.3 20.8 %collective-permute-start.14 = (bf16[896,256]{1,0:T(8,128)(2,1)S(1)}, bf16[896,256]{1,0:T(8,128)(2,1)S(1)}, u32[]{:S(2)}, u32[]{:S(2)}) collective-permute-start(bf16[896,256]{1,0:T(8,128)(2,1)S(1)} %slice_bitcast_fusion.1), channel_id=1, source_target_pairs={{0,16},{16,0},{32,48},{48,32},{1,17},{17,1},{33,49},{49,33},{2,18}... | collective-permute-start | bytes 1376264 | tf_op jit(solution)/shard_map/merge/ppermute | solution.py:19
  136.5 19.6 %collective-permute-start.15 = (bf16[896,256]{1,0:T(8,128)(2,1)S(1)}, bf16[896,256]{1,0:T(8,128)(2,1)S(1)}, u32[]{:S(2)}, u32[]{:S(2)}) collective-permute-start(bf16[896,256]{1,0:T(8,128)(2,1)S(1)} %slice_bitcast_fusion), channel_id=1, source_target_pairs={{0,48},{16,32},{32,16},{48,0},{1,49},{17,33},{33,17},{49,1},{2,50}... | collective-permute-start | bytes 1376264 | tf_op jit(solution)/shard_map/merge/ppermute | solution.py:19
  138.2 19.6 %collective-permute-start.16 = (bf16[2,896,256]{2,1,0:T(8,128)(2,1)S(1)}, bf16[2,896,256]{2,1,0:T(8,128)(2,1)S(1)}, u32[]{:S(2)}, u32[]{:S(2)}) collective-permute-start(bf16[2,896,256]{2,1,0:T(8,128)(2,1)S(1)} %merge.22.refs_0_), channel_id=1, source_target_pairs={{0,1},{1,0},{2,3},{3,2},{4,5},{5,4},{6,7},{7,6},{8,9},{9,8},{10,11... | collective-permute-start | bytes 2752520 | tf_op jit(solution)/shard_map/merge/ppermute | solution.py:19
  145.5 22.8 %collective-permute-start.20 = (bf16[2,896,256]{2,1,0:T(8,128)(2,1)S(1)}, bf16[2,896,256]{2,1,0:T(8,128)(2,1)S(1)}, u32[]{:S(2)}, u32[]{:S(2)}) collective-permute-start(bf16[2,896,256]{2,1,0:T(8,128)(2,1)S(1)} %collective-permute-done.13.refs_4_), channel_id=1, source_target_pairs={{0,1},{1,0},{2,3},{3,2},{4,5},{5,4},{6,7},{7,6},{8,9},{9,8},{10,11... | collective-permute-start | bytes 2752520 | tf_op jit(solution)/shard_map/merge/ppermute | solution.py:19
  152.7 15.6 %collective-permute-start.17 = (bf16[2,896,256]{2,1,0:T(8,128)(2,1)S(1)}, bf16[2,896,256]{2,1,0:T(8,128)(2,1)S(1)}, u32[]{:S(2)}, u32[]{:S(2)}) collective-permute-start(bf16[2,896,256]{2,1,0:T(8,128)(2,1)S(1)} %collective-permute-done.10.refs_1_), channel_id=1, source_target_pairs={{0,1},{1,0},{2,3},{3,2},{4,5},{5,4},{6,7},{7,6},{8,9},{9,8},{10,11... | collective-permute-start | bytes 2752520 | tf_op jit(solution)/shard_map/merge/ppermute | solution.py:19
  156.1 5.7 %collective-permute-start.22 = (bf16[128,896]{1,0:T(8,128)(2,1)S(1)}, bf16[128,896]{1,0:T(8,128)(2,1)S(1)}, u32[]{:S(2)}, u32[]{:S(2)}) collective-permute-start(bf16[128,896]{1,0:T(8,128)(2,1)S(1)} %slice_bitcast_fusion.3), channel_id=1, source_target_pairs={{0,16},{16,0},{32,48},{48,32},{1,17},{17,1},{33,49},{49,33},{2,18}... | collective-permute-start | bytes 688136 | tf_op jit(solution)/shard_map/merge/ppermute | solution.py:19
  156.5 10.4 %collective-permute-start.23 = (bf16[128,896]{1,0:T(8,128)(2,1)S(1)}, bf16[128,896]{1,0:T(8,128)(2,1)S(1)}, u32[]{:S(2)}, u32[]{:S(2)}) collective-permute-start(bf16[128,896]{1,0:T(8,128)(2,1)S(1)} %slice_bitcast_fusion.2), channel_id=1, source_target_pairs={{0,48},{16,32},{32,16},{48,0},{1,49},{17,33},{33,17},{49,1},{2,50}... | collective-permute-start | bytes 688136 | tf_op jit(solution)/shard_map/merge/ppermute | solution.py:19
  157.8 11.0 %collective-permute-start.18 = (bf16[896,256]{1,0:T(8,128)(2,1)S(1)}, bf16[896,256]{1,0:T(8,128)(2,1)S(1)}, u32[]{:S(2)}, u32[]{:S(2)}) collective-permute-start(bf16[896,256]{1,0:T(8,128)(2,1)S(1)} %collective-permute-done.14.refs_2_), channel_id=1, source_target_pairs={{0,1},{1,0},{2,3},{3,2},{4,5},{5,4},{6,7},{7,6},{8,9},{9,8},{10,11... | collective-permute-start | bytes 1376264 | tf_op jit(solution)/shard_map/merge/ppermute | solution.py:19
  161.9 7.0 %collective-permute-start.19 = (bf16[896,256]{1,0:T(8,128)(2,1)S(1)}, bf16[896,256]{1,0:T(8,128)(2,1)S(1)}, u32[]{:S(2)}, u32[]{:S(2)}) collective-permute-start(bf16[896,256]{1,0:T(8,128)(2,1)S(1)} %collective-permute-done.15.refs_3_), channel_id=1, source_target_pairs={{0,1},{1,0},{2,3},{3,2},{4,5},{5,4},{6,7},{7,6},{8,9},{9,8},{10,11... | collective-permute-start | bytes 1376264 | tf_op jit(solution)/shard_map/merge/ppermute | solution.py:19
  166.9 4.4 %collective-permute-start.24 = (bf16[2,128,896]{2,1,0:T(8,128)(2,1)S(1)}, bf16[2,128,896]{2,1,0:T(8,128)(2,1)S(1)}, u32[]{:S(2)}, u32[]{:S(2)}) collective-permute-start(bf16[2,128,896]{2,1,0:T(8,128)(2,1)S(1)} %merge.23.refs_4_), channel_id=1, source_target_pairs={{0,1},{1,0},{2,3},{3,2},{4,5},{5,4},{6,7},{7,6},{8,9},{9,8},{10,11... | collective-permute-start | bytes 1376264 | tf_op jit(solution)/shard_map/merge/ppermute | solution.py:19
  199.2 4.4 %collective-permute-start.29 = (bf16[8,3584]{1,0:T(8,128)(2,1)S(1)}, bf16[8,3584]{1,0:T(8,128)(2,1)S(1)}, u32[]{:S(2)}, u32[]{:S(2)}) collective-permute-start(bf16[8,3584]{1,0:T(8,128)(2,1)S(1)} %layer.21.refs_0_), channel_id=1, source_target_pairs={{0,64},{64,128},{128,192},{1,65},{65,129},{129,193},{2,66},{66,130... | collective-permute-start | bytes 172040 | tf_op jit(solution)/shard_map/layer/ppermute | solution.py:563
  222.8 3.9 collective-permute-start.30
  247.7 4.9 %collective-permute-start.31 = (bf16[8,3584]{1,0:T(8,128)(2,1)S(1)}, bf16[8,3584]{1,0:T(8,128)(2,1)S(1)}, u32[]{:S(2)}, u32[]{:S(2)}) collective-permute-start(bf16[8,3584]{1,0:T(8,128)(2,1)S(1)} %layer.25.refs_1_.refs_4_), channel_id=1, source_target_pairs={{0,64},{64,128},{128,192},{1,65},{65,129},{129,193},{2,66},{66,130... | collective-permute-start | bytes 172040 | tf_op jit(solution)/shard_map/layer/ppermute | solution.py:563
  271.4 4.1 collective-permute-start.32
  296.5 4.9 %collective-permute-start.33 = (bf16[8,3584]{1,0:T(8,128)(2,1)S(1)}, bf16[8,3584]{1,0:T(8,128)(2,1)S(1)}, u32[]{:S(2)}, u32[]{:S(2)}) collective-permute-start(bf16[8,3584]{1,0:T(8,128)(2,1)S(1)} %layer.29.refs_2_.refs_5_), channel_id=1, source_target_pairs={{0,64},{64,128},{128,192},{1,65},{65,129},{129,193},{2,66},{66,130... | collective-permute-start | bytes 172040 | tf_op jit(solution)/shard_map/layer/ppermute | solution.py:563
  345.0 4.9 %collective-permute-start.35 = (bf16[8,3584]{1,0:T(8,128)(2,1)S(1)}, bf16[8,3584]{1,0:T(8,128)(2,1)S(1)}, u32[]{:S(2)}, u32[]{:S(2)}) collective-permute-start(bf16[8,3584]{1,0:T(8,128)(2,1)S(1)} %layer.33.refs_3_.refs_6_), channel_id=1, source_target_pairs={{0,64},{64,128},{128,192},{1,65},{65,129},{129,193},{2,66},{66,130... | collective-permute-start | bytes 172040 | tf_op jit(solution)/shard_map/layer/ppermute | solution.py:563
  394.9 11.3 %all-to-all-start.10 = ((f32[16,1,128]{2,1,0:T(1,128)}), f32[16,1,128]{2,1,0:T(1,128)S(1)}, u32[]{:S(2)}, u32[]{:S(2)}) async-start(f32[16,1,128]{2,1,0:T(1,128)} %get-tuple-element.85), calls=%async_computation.10 | async-start | bytes 16384 | tf_op jit(solution)/shard_map/loss/all_to_all | solution.py:578
  398.6 8.9 %collective-permute-start.37 = (bf16[8,3584]{1,0:T(8,128)(2,1)S(1)}, bf16[8,3584]{1,0:T(8,128)(2,1)S(1)}, u32[]{:S(2)}, u32[]{:S(2)}) collective-permute-start(bf16[8,3584]{1,0:T(8,128)(2,1)S(1)} %get-tuple-element.83), channel_id=1, source_target_pairs={{0,0},{2,1},{4,2},{6,3},{8,4},{10,5},{12,6},{14,7},{1,8},{3,9},{5,... | collective-permute-start | bytes 172040 | tf_op jit(solution)/shard_map/loss/ppermute | solution.py:522
  (15 other events, 82.3 us)

commit v4 on v3

--- a/solution.py
+++ b/solution.py
@@ -539,7 +539,7 @@
         first = spread(first)
         out_got, first = lax.optimization_barrier((out_got, first))
         out_sent, out_more = second_halves(plan, scale, out_sources, out_got)
-        qkv_got, _ = lax.optimization_barrier((qkv_got, out_sent))
+        qkv_got = [lax.optimization_barrier((got, out_sent))[0] for got in qkv_got]
         qkv_sent, qkv_more = second_halves(plan, scale, qkv_sources, qkv_got)
         qkv_more, out_more = lax.optimization_barrier((qkv_more, out_more))
         qkv_share = shares(plan, scale, qkv_sources, qkv_got, qkv_more)

time: 413 us -> 409 us (level)
  waiting for transfers between devices: 79.7 us -> 70.3 us
  starting transfers between devices: 96.3 us -> 102 us
    ppermute x31, waiting for transfers between devices: 50.2 us -> 40.8 us  [exchanged(): lax.ppermute(array, axis, [(i, i ^ mask) for i in range(lax.axis_size(axi...]
    ppermute x31, starting transfers between devices: 55.7 us -> 61.7 us  [exchanged(): lax.ppermute(array, axis, [(i, i ^ mask) for i in range(lax.axis_size(axi...]
  transfers between devices with their start and end apart: 41 -> 41, of which waited for: 20 -> 17; matrix products, arithmetic and copies ran while one was open for 0% -> 0% of each run, Pallas kernels for 6% -> 8%
where the time goes in v4:
time: 409 us; the launch traced here: 408 us
  blocking collectives  166 us (41%)
  starting transfers between devices  102 us (25%)
  waiting for transfers between devices  70.3 us (17%)
  Pallas kernels  60.4 us (15%)
    all_to_all x9, blocking collectives, spread(): lax.all_to_all(pieces, 'mp', 0, 0, tiled=True, axis_index_groups=groups)  166 us
    ppermute x31, starting transfers between devices, exchanged(): lax.ppermute(array, axis, [(i, i ^ mask) for i in range(lax.axis_size(axi...  61.7 us
    pallas_call x33, Pallas kernels, kernel_call(): pl.pallas_call(kernel, out_shape=tuple((result_on_chip(shape[:-1], F32) i...  60.4 us
    ppermute x31, waiting for transfers between devices, exchanged(): lax.ppermute(array, axis, [(i, i ^ mask) for i in range(lax.axis_size(axi...  40.8 us
    ppermute x4, starting transfers between devices, per_device(): lax.ppermute(outs[-1], 'section', [(i, i + 1) for i in range(sections - 1)])  14.2 us
    all_to_all x1, waiting for transfers between devices, spread(): lax.all_to_all(pieces, 'mp', 0, 0, tiled=True, axis_index_groups=groups)  14 us
    ppermute x4, starting transfers between devices, over_mp(): return lax.ppermute(array, 'mp', pairs)  13.2 us
    ppermute x4, waiting for transfers between devices, over_mp(): return lax.ppermute(array, 'mp', pairs)  10.5 us
  transfers between devices with their start and end apart: 41, of which 17 were waited for; matrix products, arithmetic and copies ran while one was open for 0% of the time, Pallas kernels for 8%

profile of v4, /device:TPU:1, one launch (start us, length us, event | category | flops | bytes accessed | tf_op | source)
XLA Modules:
  0.0 407.5 jit_solution(8402606433652804318)
XLA Ops:
  2.1 3.5 merge.12
  7.7 3.5 merge.13
  13.1 4.2 %merge.14 = bf16[2,2,896,256]{3,2,1,0:T(8,128)(2,1)} custom-call(s32[16]{0:T(128)S(1)} %stack.69.plan_ref, f32[1]{0:T(128)} %dynamic_slice.3.scale_ref, bf16[4,896,256]{2,1,0:T(8,128)(2,1)} %bitcast.95, bf16[4,896,256]{2,1,0:T(8,128)(2,1)} %bitcast.98), custom_call_target="tpu_custom_call" | custom-call | flops 1 | bytes 1 | tf_op jit(solution)/shard_map/merge/pallas_call | solution.py:32
  17.7 4.2 %merge.15 = bf16[2,2,896,256]{3,2,1,0:T(8,128)(2,1)} custom-call(s32[16]{0:T(128)S(1)} %stack.69.plan_ref, f32[1]{0:T(128)} %dynamic_slice.3.scale_ref, bf16[4,896,128]{2,1,0:T(8,128)(2,1)} %bitcast.101, bf16[4,896,128]{2,1,0:T(8,128)(2,1)} %bitcast.104, bf16[4,896,128]{2,1,0:T(8,128)(2,1)} %bitcast.107, bf16[4,896,128]{2,1,0:T(8,128)(2,1)} %bitcast.110), custom_call_target="tpu_custom_call" | custom-call | flops 1 | bytes 1 | tf_op jit(solution)/shard_map/merge/pallas_call | solution.py:32
  24.1 4.9 %collective-permute-start = (bf16[16,3584]{1,0:T(8,128)(2,1)S(1)}, bf16[16,3584]{1,0:T(8,128)(2,1)S(1)}, u32[]{:S(2)}, u32[]{:S(2)}) collective-permute-start(bf16[16,3584]{1,0:T(8,128)(2,1)S(1)} %get-tuple-element.47), channel_id=1, source_target_pairs={{0,0},{1,2},{2,4},{3,6},{4,8},{5,10},{6,12},{7,14},{8,1},{9,3},{10... | collective-permute-start | bytes 344072 | tf_op jit(solution)/shard_map/merge/ppermute | solution.py:522
  29.4 7.3 %collective-permute-done.s_ref = bf16[16,3584]{1,0:T(8,128)(2,1)S(1)} collective-permute-done((bf16[16,3584]{1,0:T(8,128)(2,1)S(1)}, bf16[16,3584]{1,0:T(8,128)(2,1)S(1)}, u32[]{:S(2)}, u32[]{:S(2)}) %collective-permute-start) | collective-permute-done | bytes 114720 | tf_op jit(solution)/shard_map/merge/ppermute | solution.py:522
  41.3 9.5 %all-to-all-start = ((bf16[8,8,3584]{2,1,0:T(8,128)(2,1)}), bf16[8,8,3584]{2,1,0:T(8,128)(2,1)S(1)}, u32[]{:S(2)}, u32[]{:S(2)}) async-start(bf16[8,8,3584]{2,1,0:T(8,128)(2,1)} %bitcast.79), calls=%async_computation | async-start | bytes 917504 | tf_op jit(solution)/shard_map/merge/all_to_all | solution.py:513
  50.8 14.0 %all-to-all-done = bf16[8,8,3584]{2,1,0:T(8,128)(2,1)S(1)} async-done(((bf16[8,8,3584]{2,1,0:T(8,128)(2,1)}), bf16[8,8,3584]{2,1,0:T(8,128)(2,1)S(1)}, u32[]{:S(2)}, u32[]{:S(2)}) %all-to-all-start) | async-done | bytes 458784 | tf_op jit(solution)/shard_map/merge/all_to_all | solution.py:513
  74.0 3.8 merge.21
  81.1 24.1 %collective-permute-done.9.refs_7_ = bf16[2,1,128,896]{3,2,1,0:T(8,128)(2,1)S(1)} collective-permute-done((bf16[2,1,128,896]{3,2,1,0:T(8,128)(2,1)S(1)}, bf16[2,1,128,896]{3,2,1,0:T(8,128)(2,1)S(1)}, u32[]{:S(2)}, u32[]{:S(2)}) %collective-permute-start.9) | collective-permute-done | bytes 458784 | tf_op jit(solution)/shard_map/merge/ppermute | solution.py:19
  105.2 5.0 %merge.22.refs_0_ = bf16[2,896,256]{2,1,0:T(8,128)(2,1)S(1)} custom-call(s32[16]{0:T(128)S(1)} %stack.69.plan_ref, f32[1]{0:T(128)} %dynamic_slice.3.scale_ref, bf16[4,896,256]{2,1,0:T(8,128)(2,1)} %bitcast.97, bf16[4,896,256]{2,1,0:T(8,128)(2,1)} %bitcast.100, bf16[2,2,896,256]{3,2,1,0:T(8,128)(2,1)S(1)} %collective-permute-done.4.refs_2_, ...), custom_call_target="tpu_custom_call" | custom-call | flops 1 | bytes 1 | tf_op jit(solution)/shard_map/merge/pallas_call | solution.py:32
  113.1 3.6 merge.23.refs_4_
  118.4 10.1 %collective-permute-done.13.refs_4_ = bf16[2,896,256]{2,1,0:T(8,128)(2,1)S(1)} collective-permute-done((bf16[2,896,256]{2,1,0:T(8,128)(2,1)S(1)}, bf16[2,896,256]{2,1,0:T(8,128)(2,1)S(1)}, u32[]{:S(2)}, u32[]{:S(2)}) %collective-permute-start.13) | collective-permute-done | bytes 917536 | tf_op jit(solution)/shard_map/merge/ppermute | solution.py:19
  132.2 10.1 %collective-permute-start.16 = (bf16[2,896,256]{2,1,0:T(8,128)(2,1)S(1)}, bf16[2,896,256]{2,1,0:T(8,128)(2,1)S(1)}, u32[]{:S(2)}, u32[]{:S(2)}) collective-permute-start(bf16[2,896,256]{2,1,0:T(8,128)(2,1)S(1)} %merge.22.refs_0_), channel_id=1, source_target_pairs={{0,1},{1,0},{2,3},{3,2},{4,5},{5,4},{6,7},{7,6},{8,9},{9,8},{10,11... | collective-permute-start | bytes 2752520 | tf_op jit(solution)/shard_map/merge/ppermute | solution.py:19
  142.4 6.8 %collective-permute-start.20 = (bf16[2,896,256]{2,1,0:T(8,128)(2,1)S(1)}, bf16[2,896,256]{2,1,0:T(8,128)(2,1)S(1)}, u32[]{:S(2)}, u32[]{:S(2)}) collective-permute-start(bf16[2,896,256]{2,1,0:T(8,128)(2,1)S(1)} %collective-permute-done.13.refs_4_), channel_id=1, source_target_pairs={{0,1},{1,0},{2,3},{3,2},{4,5},{5,4},{6,7},{7,6},{8,9},{9,8},{10,11... | collective-permute-start | bytes 2752520 | tf_op jit(solution)/shard_map/merge/ppermute | solution.py:19
  151.9 5.9 %collective-permute-start.18 = (bf16[896,256]{1,0:T(8,128)(2,1)S(1)}, bf16[896,256]{1,0:T(8,128)(2,1)S(1)}, u32[]{:S(2)}, u32[]{:S(2)}) collective-permute-start(bf16[896,256]{1,0:T(8,128)(2,1)S(1)} %collective-permute-done.14.refs_2_), channel_id=1, source_target_pairs={{0,1},{1,0},{2,3},{3,2},{4,5},{5,4},{6,7},{7,6},{8,9},{9,8},{10,11... | collective-permute-start | bytes 1376264 | tf_op jit(solution)/shard_map/merge/ppermute | solution.py:19
  157.8 5.5 %collective-permute-start.19 = (bf16[896,256]{1,0:T(8,128)(2,1)S(1)}, bf16[896,256]{1,0:T(8,128)(2,1)S(1)}, u32[]{:S(2)}, u32[]{:S(2)}) collective-permute-start(bf16[896,256]{1,0:T(8,128)(2,1)S(1)} %collective-permute-done.15.refs_3_), channel_id=1, source_target_pairs={{0,1},{1,0},{2,3},{3,2},{4,5},{5,4},{6,7},{7,6},{8,9},{9,8},{10,11... | collective-permute-start | bytes 1376264 | tf_op jit(solution)/shard_map/merge/ppermute | solution.py:19
  171.2 23.8 %all_to_all.55 = bf16[8,8,3584]{2,1,0:T(8,128)(2,1)S(1)} all-to-all(bf16[8,8,3584]{2,1,0:T(8,128)(2,1)S(1)} %bitcast.65), channel_id=1, replica_groups={{0,2,4,6,8,10,12,14},{1,3,5,7,9,11,13,15},{16,18,20,22,24,26,28,30},{17..., dimensions={0} | all-to-all | bytes 917504 | tf_op jit(solution)/shard_map/layer/all_to_all | solution.py:513
  195.1 3.2 collective-permute-start.29
  200.3 16.5 %all_to_all.56 = bf16[8,8,3584]{2,1,0:T(8,128)(2,1)S(1)} all-to-all(bf16[8,8,3584]{2,1,0:T(8,128)(2,1)S(1)} %bitcast.80), channel_id=1, replica_groups={{0,2,4,6,8,10,12,14},{1,3,5,7,9,11,13,15},{16,18,20,22,24,26,28,30},{17..., dimensions={0} | all-to-all | bytes 917504 | tf_op jit(solution)/shard_map/layer/all_to_all | solution.py:513
  224.6 19.0 %all_to_all.57 = bf16[8,8,3584]{2,1,0:T(8,128)(2,1)S(1)} all-to-all(bf16[8,8,3584]{2,1,0:T(8,128)(2,1)S(1)} %bitcast.62), channel_id=1, replica_groups={{0,2,4,6,8,10,12,14},{1,3,5,7,9,11,13,15},{16,18,20,22,24,26,28,30},{17..., dimensions={0} | all-to-all | bytes 917504 | tf_op jit(solution)/shard_map/layer/all_to_all | solution.py:513
  243.7 3.7 collective-permute-start.31
  248.8 16.6 %all_to_all.58 = bf16[8,8,3584]{2,1,0:T(8,128)(2,1)S(1)} all-to-all(bf16[8,8,3584]{2,1,0:T(8,128)(2,1)S(1)} %bitcast.72), channel_id=1, replica_groups={{0,2,4,6,8,10,12,14},{1,3,5,7,9,11,13,15},{16,18,20,22,24,26,28,30},{17..., dimensions={0} | all-to-all | bytes 917504 | tf_op jit(solution)/shard_map/layer/all_to_all | solution.py:513
  273.3 19.0 %all_to_all.59 = bf16[8,8,3584]{2,1,0:T(8,128)(2,1)S(1)} all-to-all(bf16[8,8,3584]{2,1,0:T(8,128)(2,1)S(1)} %bitcast.63), channel_id=1, replica_groups={{0,2,4,6,8,10,12,14},{1,3,5,7,9,11,13,15},{16,18,20,22,24,26,28,30},{17..., dimensions={0} | all-to-all | bytes 917504 | tf_op jit(solution)/shard_map/layer/all_to_all | solution.py:513
  292.5 3.7 collective-permute-start.33
  297.5 16.6 %all_to_all.60 = bf16[8,8,3584]{2,1,0:T(8,128)(2,1)S(1)} all-to-all(bf16[8,8,3584]{2,1,0:T(8,128)(2,1)S(1)} %bitcast.73), channel_id=1, replica_groups={{0,2,4,6,8,10,12,14},{1,3,5,7,9,11,13,15},{16,18,20,22,24,26,28,30},{17..., dimensions={0} | all-to-all | bytes 917504 | tf_op jit(solution)/shard_map/layer/all_to_all | solution.py:513
  321.8 19.0 %all_to_all.61 = bf16[8,8,3584]{2,1,0:T(8,128)(2,1)S(1)} all-to-all(bf16[8,8,3584]{2,1,0:T(8,128)(2,1)S(1)} %bitcast.64), channel_id=1, replica_groups={{0,2,4,6,8,10,12,14},{1,3,5,7,9,11,13,15},{16,18,20,22,24,26,28,30},{17..., dimensions={0} | all-to-all | bytes 917504 | tf_op jit(solution)/shard_map/layer/all_to_all | solution.py:513
  341.0 3.7 collective-permute-start.35
  346.1 16.6 %all_to_all.62 = bf16[8,8,3584]{2,1,0:T(8,128)(2,1)S(1)} all-to-all(bf16[8,8,3584]{2,1,0:T(8,128)(2,1)S(1)} %bitcast.71), channel_id=1, replica_groups={{0,2,4,6,8,10,12,14},{1,3,5,7,9,11,13,15},{16,18,20,22,24,26,28,30},{17..., dimensions={0} | all-to-all | bytes 917504 | tf_op jit(solution)/shard_map/layer/all_to_all | solution.py:513
  370.3 19.0 %all_to_all.63 = bf16[8,8,3584]{2,1,0:T(8,128)(2,1)S(1)} all-to-all(bf16[8,8,3584]{2,1,0:T(8,128)(2,1)S(1)} %bitcast.61), channel_id=1, replica_groups={{0,2,4,6,8,10,12,14},{1,3,5,7,9,11,13,15},{16,18,20,22,24,26,28,30},{17..., dimensions={0} | all-to-all | bytes 917504 | tf_op jit(solution)/shard_map/layer/all_to_all | solution.py:513
  390.9 3.7 all-to-all-start.10
  394.6 7.5 %collective-permute-start.37 = (bf16[8,3584]{1,0:T(8,128)(2,1)S(1)}, bf16[8,3584]{1,0:T(8,128)(2,1)S(1)}, u32[]{:S(2)}, u32[]{:S(2)}) collective-permute-start(bf16[8,3584]{1,0:T(8,128)(2,1)S(1)} %get-tuple-element.83), channel_id=1, source_target_pairs={{0,0},{2,1},{4,2},{6,3},{8,4},{10,5},{12,6},{14,7},{1,8},{3,9},{5,... | collective-permute-start | bytes 172040 | tf_op jit(solution)/shard_map/loss/ppermute | solution.py:522
  (125 shorter events, 86.4 us)
Async XLA Ops:
  5.6 45.2 %collective-permute-start.2 = (bf16[2,2,128,896]{3,2,1,0:T(8,128)(2,1)}, bf16[2,2,128,896]{3,2,1,0:T(8,128)(2,1)S(1)}, u32[]{:S(2)}, u32[]{:S(2)}) collective-permute-start(bf16[2,2,128,896]{3,2,1,0:T(8,128)(2,1)} %merge.12), channel_id=1, source_target_pairs={{0,16},{16,0},{32,48},{48,32},{1,17},{17,1},{33,49},{49,33},{2,18}... | collective-permute-start | bytes 2752520 | tf_op jit(solution)/shard_map/merge/ppermute | solution.py:19
  11.2 39.6 %collective-permute-start.3 = (bf16[2,2,128,896]{3,2,1,0:T(8,128)(2,1)}, bf16[2,2,128,896]{3,2,1,0:T(8,128)(2,1)}, u32[]{:S(2)}, u32[]{:S(2)}) collective-permute-start(bf16[2,2,128,896]{3,2,1,0:T(8,128)(2,1)} %merge.13), channel_id=1, source_target_pairs={{0,48},{16,32},{32,16},{48,0},{1,49},{17,33},{33,17},{49,1},{2,50}... | collective-permute-start | bytes 2752520 | tf_op jit(solution)/shard_map/merge/ppermute | solution.py:19
  17.3 53.0 %collective-permute-start.4 = (bf16[2,2,896,256]{3,2,1,0:T(8,128)(2,1)}, bf16[2,2,896,256]{3,2,1,0:T(8,128)(2,1)S(1)}, u32[]{:S(2)}, u32[]{:S(2)}) collective-permute-start(bf16[2,2,896,256]{3,2,1,0:T(8,128)(2,1)} %merge.14), channel_id=1, source_target_pairs={{0,16},{16,0},{32,48},{48,32},{1,17},{17,1},{33,49},{49,33},{2,18}... | collective-permute-start | bytes 5505032 | tf_op jit(solution)/shard_map/merge/ppermute | solution.py:19
  22.0 52.0 %collective-permute-start.6 = (bf16[2,2,896,256]{3,2,1,0:T(8,128)(2,1)}, bf16[2,2,896,256]{3,2,1,0:T(8,128)(2,1)}, u32[]{:S(2)}, u32[]{:S(2)}) collective-permute-start(bf16[2,2,896,256]{3,2,1,0:T(8,128)(2,1)} %merge.15), channel_id=1, source_target_pairs={{0,48},{16,32},{32,16},{48,0},{1,49},{17,33},{33,17},{49,1},{2,50}... | collective-permute-start | bytes 5505032 | tf_op jit(solution)/shard_map/merge/ppermute | solution.py:19
  24.1 12.7 %collective-permute-start = (bf16[16,3584]{1,0:T(8,128)(2,1)S(1)}, bf16[16,3584]{1,0:T(8,128)(2,1)S(1)}, u32[]{:S(2)}, u32[]{:S(2)}) collective-permute-start(bf16[16,3584]{1,0:T(8,128)(2,1)S(1)} %get-tuple-element.47), channel_id=1, source_target_pairs={{0,0},{1,2},{2,4},{3,6},{4,8},{5,10},{6,12},{7,14},{8,1},{9,3},{10... | collective-permute-start | bytes 344072 | tf_op jit(solution)/shard_map/merge/ppermute | solution.py:522
  41.3 23.5 %all-to-all-start = ((bf16[8,8,3584]{2,1,0:T(8,128)(2,1)}), bf16[8,8,3584]{2,1,0:T(8,128)(2,1)S(1)}, u32[]{:S(2)}, u32[]{:S(2)}) async-start(bf16[8,8,3584]{2,1,0:T(8,128)(2,1)} %bitcast.79), calls=%async_computation | async-start | bytes 917504 | tf_op jit(solution)/shard_map/merge/all_to_all | solution.py:513
  73.0 32.2 %collective-permute-start.5 = (bf16[2,1,896,256]{3,2,1,0:T(8,128)(2,1)S(1)}, bf16[2,1,896,256]{3,2,1,0:T(8,128)(2,1)S(1)}, u32[]{:S(2)}, u32[]{:S(2)}) collective-permute-start(bf16[2,1,896,256]{3,2,1,0:T(8,128)(2,1)S(1)} %merge.20), channel_id=1, source_target_pairs={{0,48},{16,32},{32,16},{48,0},{1,49},{17,33},{33,17},{49,1},{2,50}... | collective-permute-start | bytes 2752520 | tf_op jit(solution)/shard_map/merge/ppermute | solution.py:19
  77.8 27.4 %collective-permute-start.7 = (bf16[2,1,896,256]{3,2,1,0:T(8,128)(2,1)S(1)}, bf16[2,1,896,256]{3,2,1,0:T(8,128)(2,1)S(1)}, u32[]{:S(2)}, u32[]{:S(2)}) collective-permute-start(bf16[2,1,896,256]{3,2,1,0:T(8,128)(2,1)S(1)} %merge.21), channel_id=1, source_target_pairs={{0,16},{16,0},{32,48},{48,32},{1,17},{17,1},{33,49},{49,33},{2,18}... | collective-permute-start | bytes 2752520 | tf_op jit(solution)/shard_map/merge/ppermute | solution.py:19
  77.9 27.3 %collective-permute-start.9 = (bf16[2,1,128,896]{3,2,1,0:T(8,128)(2,1)S(1)}, bf16[2,1,128,896]{3,2,1,0:T(8,128)(2,1)S(1)}, u32[]{:S(2)}, u32[]{:S(2)}) collective-permute-start(bf16[2,1,128,896]{3,2,1,0:T(8,128)(2,1)S(1)} %merge.19), channel_id=1, source_target_pairs={{0,16},{16,0},{32,48},{48,32},{1,17},{17,1},{33,49},{49,33},{2,18}... | collective-permute-start | bytes 1376264 | tf_op jit(solution)/shard_map/merge/ppermute | solution.py:19
  79.3 25.9 %collective-permute-start.8 = (bf16[2,1,128,896]{3,2,1,0:T(8,128)(2,1)S(1)}, bf16[2,1,128,896]{3,2,1,0:T(8,128)(2,1)S(1)}, u32[]{:S(2)}, u32[]{:S(2)}) collective-permute-start(bf16[2,1,128,896]{3,2,1,0:T(8,128)(2,1)S(1)} %merge.18), channel_id=1, source_target_pairs={{0,48},{16,32},{32,16},{48,0},{1,49},{17,33},{33,17},{49,1},{2,50}... | collective-permute-start | bytes 1376264 | tf_op jit(solution)/shard_map/merge/ppermute | solution.py:19
  110.2 18.4 %collective-permute-start.13 = (bf16[2,896,256]{2,1,0:T(8,128)(2,1)S(1)}, bf16[2,896,256]{2,1,0:T(8,128)(2,1)S(1)}, u32[]{:S(2)}, u32[]{:S(2)}) collective-permute-start(bf16[2,896,256]{2,1,0:T(8,128)(2,1)S(1)} %merge.22.refs_0_), channel_id=1, source_target_pairs={{0,48},{16,32},{32,16},{48,0},{1,49},{17,33},{33,17},{49,1},{2,50}... | collective-permute-start | bytes 2752520 | tf_op jit(solution)/shard_map/merge/ppermute | solution.py:19
  113.1 17.4 %collective-permute-start.10 = (bf16[2,896,256]{2,1,0:T(8,128)(2,1)S(1)}, bf16[2,896,256]{2,1,0:T(8,128)(2,1)S(1)}, u32[]{:S(2)}, u32[]{:S(2)}) collective-permute-start(bf16[2,896,256]{2,1,0:T(8,128)(2,1)S(1)} %merge.22.refs_0_), channel_id=1, source_target_pairs={{0,16},{16,0},{32,48},{48,32},{1,17},{17,1},{33,49},{49,33},{2,18}... | collective-permute-start | bytes 2752520 | tf_op jit(solution)/shard_map/merge/ppermute | solution.py:19
  116.8 25.6 %collective-permute-start.12 = (bf16[2,128,896]{2,1,0:T(8,128)(2,1)S(1)}, bf16[2,128,896]{2,1,0:T(8,128)(2,1)S(1)}, u32[]{:S(2)}, u32[]{:S(2)}) collective-permute-start(bf16[2,128,896]{2,1,0:T(8,128)(2,1)S(1)} %merge.23.refs_4_), channel_id=1, source_target_pairs={{0,48},{16,32},{32,16},{48,0},{1,49},{17,33},{33,17},{49,1},{2,50}... | collective-permute-start | bytes 1376264 | tf_op jit(solution)/shard_map/merge/ppermute | solution.py:19
  117.0 32.2 %collective-permute-start.11 = (bf16[2,128,896]{2,1,0:T(8,128)(2,1)S(1)}, bf16[2,128,896]{2,1,0:T(8,128)(2,1)S(1)}, u32[]{:S(2)}, u32[]{:S(2)}) collective-permute-start(bf16[2,128,896]{2,1,0:T(8,128)(2,1)S(1)} %merge.23.refs_4_), channel_id=1, source_target_pairs={{0,16},{16,0},{32,48},{48,32},{1,17},{17,1},{33,49},{49,33},{2,18}... | collective-permute-start | bytes 1376264 | tf_op jit(solution)/shard_map/merge/ppermute | solution.py:19
  128.6 22.1 %collective-permute-start.14 = (bf16[896,256]{1,0:T(8,128)(2,1)S(1)}, bf16[896,256]{1,0:T(8,128)(2,1)S(1)}, u32[]{:S(2)}, u32[]{:S(2)}) collective-permute-start(bf16[896,256]{1,0:T(8,128)(2,1)S(1)} %slice_bitcast_fusion.1), channel_id=1, source_target_pairs={{0,16},{16,0},{32,48},{48,32},{1,17},{17,1},{33,49},{49,33},{2,18}... | collective-permute-start | bytes 1376264 | tf_op jit(solution)/shard_map/merge/ppermute | solution.py:19
  130.5 20.1 %collective-permute-start.15 = (bf16[896,256]{1,0:T(8,128)(2,1)S(1)}, bf16[896,256]{1,0:T(8,128)(2,1)S(1)}, u32[]{:S(2)}, u32[]{:S(2)}) collective-permute-start(bf16[896,256]{1,0:T(8,128)(2,1)S(1)} %slice_bitcast_fusion), channel_id=1, source_target_pairs={{0,48},{16,32},{32,16},{48,0},{1,49},{17,33},{33,17},{49,1},{2,50}... | collective-permute-start | bytes 1376264 | tf_op jit(solution)/shard_map/merge/ppermute | solution.py:19
  132.2 19.7 %collective-permute-start.16 = (bf16[2,896,256]{2,1,0:T(8,128)(2,1)S(1)}, bf16[2,896,256]{2,1,0:T(8,128)(2,1)S(1)}, u32[]{:S(2)}, u32[]{:S(2)}) collective-permute-start(bf16[2,896,256]{2,1,0:T(8,128)(2,1)S(1)} %merge.22.refs_0_), channel_id=1, source_target_pairs={{0,1},{1,0},{2,3},{3,2},{4,5},{5,4},{6,7},{7,6},{8,9},{9,8},{10,11... | collective-permute-start | bytes 2752520 | tf_op jit(solution)/shard_map/merge/ppermute | solution.py:19
  142.4 22.5 %collective-permute-start.20 = (bf16[2,896,256]{2,1,0:T(8,128)(2,1)S(1)}, bf16[2,896,256]{2,1,0:T(8,128)(2,1)S(1)}, u32[]{:S(2)}, u32[]{:S(2)}) collective-permute-start(bf16[2,896,256]{2,1,0:T(8,128)(2,1)S(1)} %collective-permute-done.13.refs_4_), channel_id=1, source_target_pairs={{0,1},{1,0},{2,3},{3,2},{4,5},{5,4},{6,7},{7,6},{8,9},{9,8},{10,11... | collective-permute-start | bytes 2752520 | tf_op jit(solution)/shard_map/merge/ppermute | solution.py:19
  149.2 15.7 %collective-permute-start.17 = (bf16[2,896,256]{2,1,0:T(8,128)(2,1)S(1)}, bf16[2,896,256]{2,1,0:T(8,128)(2,1)S(1)}, u32[]{:S(2)}, u32[]{:S(2)}) collective-permute-start(bf16[2,896,256]{2,1,0:T(8,128)(2,1)S(1)} %collective-permute-done.10.refs_1_), channel_id=1, source_target_pairs={{0,1},{1,0},{2,3},{3,2},{4,5},{5,4},{6,7},{7,6},{8,9},{9,8},{10,11... | collective-permute-start | bytes 2752520 | tf_op jit(solution)/shard_map/merge/ppermute | solution.py:19
  150.7 7.1 %collective-permute-start.22 = (bf16[128,896]{1,0:T(8,128)(2,1)S(1)}, bf16[128,896]{1,0:T(8,128)(2,1)S(1)}, u32[]{:S(2)}, u32[]{:S(2)}) collective-permute-start(bf16[128,896]{1,0:T(8,128)(2,1)S(1)} %slice_bitcast_fusion.3), channel_id=1, source_target_pairs={{0,16},{16,0},{32,48},{48,32},{1,17},{17,1},{33,49},{49,33},{2,18}... | collective-permute-start | bytes 688136 | tf_op jit(solution)/shard_map/merge/ppermute | solution.py:19
  150.8 12.5 %collective-permute-start.23 = (bf16[128,896]{1,0:T(8,128)(2,1)S(1)}, bf16[128,896]{1,0:T(8,128)(2,1)S(1)}, u32[]{:S(2)}, u32[]{:S(2)}) collective-permute-start(bf16[128,896]{1,0:T(8,128)(2,1)S(1)} %slice_bitcast_fusion.2), channel_id=1, source_target_pairs={{0,48},{16,32},{32,16},{48,0},{1,49},{17,33},{33,17},{49,1},{2,50}... | collective-permute-start | bytes 688136 | tf_op jit(solution)/shard_map/merge/ppermute | solution.py:19
  151.9 13.5 %collective-permute-start.18 = (bf16[896,256]{1,0:T(8,128)(2,1)S(1)}, bf16[896,256]{1,0:T(8,128)(2,1)S(1)}, u32[]{:S(2)}, u32[]{:S(2)}) collective-permute-start(bf16[896,256]{1,0:T(8,128)(2,1)S(1)} %collective-permute-done.14.refs_2_), channel_id=1, source_target_pairs={{0,1},{1,0},{2,3},{3,2},{4,5},{5,4},{6,7},{7,6},{8,9},{9,8},{10,11... | collective-permute-start | bytes 1376264 | tf_op jit(solution)/shard_map/merge/ppermute | solution.py:19
  157.8 7.7 %collective-permute-start.19 = (bf16[896,256]{1,0:T(8,128)(2,1)S(1)}, bf16[896,256]{1,0:T(8,128)(2,1)S(1)}, u32[]{:S(2)}, u32[]{:S(2)}) collective-permute-start(bf16[896,256]{1,0:T(8,128)(2,1)S(1)} %collective-permute-done.15.refs_3_), channel_id=1, source_target_pairs={{0,1},{1,0},{2,3},{3,2},{4,5},{5,4},{6,7},{7,6},{8,9},{9,8},{10,11... | collective-permute-start | bytes 1376264 | tf_op jit(solution)/shard_map/merge/ppermute | solution.py:19
  163.3 4.6 %collective-permute-start.24 = (bf16[2,128,896]{2,1,0:T(8,128)(2,1)S(1)}, bf16[2,128,896]{2,1,0:T(8,128)(2,1)S(1)}, u32[]{:S(2)}, u32[]{:S(2)}) collective-permute-start(bf16[2,128,896]{2,1,0:T(8,128)(2,1)S(1)} %merge.23.refs_4_), channel_id=1, source_target_pairs={{0,1},{1,0},{2,3},{3,2},{4,5},{5,4},{6,7},{7,6},{8,9},{9,8},{10,11... | collective-permute-start | bytes 1376264 | tf_op jit(solution)/shard_map/merge/ppermute | solution.py:19
  195.1 4.4 %collective-permute-start.29 = (bf16[8,3584]{1,0:T(8,128)(2,1)S(1)}, bf16[8,3584]{1,0:T(8,128)(2,1)S(1)}, u32[]{:S(2)}, u32[]{:S(2)}) collective-permute-start(bf16[8,3584]{1,0:T(8,128)(2,1)S(1)} %layer.21.refs_0_), channel_id=1, source_target_pairs={{0,64},{64,128},{128,192},{1,65},{65,129},{129,193},{2,66},{66,130... | collective-permute-start | bytes 172040 | tf_op jit(solution)/shard_map/layer/ppermute | solution.py:563
  218.8 3.9 collective-permute-start.30
  243.7 4.9 %collective-permute-start.31 = (bf16[8,3584]{1,0:T(8,128)(2,1)S(1)}, bf16[8,3584]{1,0:T(8,128)(2,1)S(1)}, u32[]{:S(2)}, u32[]{:S(2)}) collective-permute-start(bf16[8,3584]{1,0:T(8,128)(2,1)S(1)} %layer.25.refs_1_.refs_4_), channel_id=1, source_target_pairs={{0,64},{64,128},{128,192},{1,65},{65,129},{129,193},{2,66},{66,130... | collective-permute-start | bytes 172040 | tf_op jit(solution)/shard_map/layer/ppermute | solution.py:563
  267.4 4.1 collective-permute-start.32
  292.5 4.9 %collective-permute-start.33 = (bf16[8,3584]{1,0:T(8,128)(2,1)S(1)}, bf16[8,3584]{1,0:T(8,128)(2,1)S(1)}, u32[]{:S(2)}, u32[]{:S(2)}) collective-permute-start(bf16[8,3584]{1,0:T(8,128)(2,1)S(1)} %layer.29.refs_2_.refs_5_), channel_id=1, source_target_pairs={{0,64},{64,128},{128,192},{1,65},{65,129},{129,193},{2,66},{66,130... | collective-permute-start | bytes 172040 | tf_op jit(solution)/shard_map/layer/ppermute | solution.py:563
  341.0 4.9 %collective-permute-start.35 = (bf16[8,3584]{1,0:T(8,128)(2,1)S(1)}, bf16[8,3584]{1,0:T(8,128)(2,1)S(1)}, u32[]{:S(2)}, u32[]{:S(2)}) collective-permute-start(bf16[8,3584]{1,0:T(8,128)(2,1)S(1)} %layer.33.refs_3_.refs_6_), channel_id=1, source_target_pairs={{0,64},{64,128},{128,192},{1,65},{65,129},{129,193},{2,66},{66,130... | collective-permute-start | bytes 172040 | tf_op jit(solution)/shard_map/layer/ppermute | solution.py:563
  390.9 11.3 %all-to-all-start.10 = ((f32[16,1,128]{2,1,0:T(1,128)}), f32[16,1,128]{2,1,0:T(1,128)S(1)}, u32[]{:S(2)}, u32[]{:S(2)}) async-start(f32[16,1,128]{2,1,0:T(1,128)} %get-tuple-element.85), calls=%async_computation.10 | async-start | bytes 16384 | tf_op jit(solution)/shard_map/loss/all_to_all | solution.py:578
  394.6 8.9 %collective-permute-start.37 = (bf16[8,3584]{1,0:T(8,128)(2,1)S(1)}, bf16[8,3584]{1,0:T(8,128)(2,1)S(1)}, u32[]{:S(2)}, u32[]{:S(2)}) collective-permute-start(bf16[8,3584]{1,0:T(8,128)(2,1)S(1)} %get-tuple-element.83), channel_id=1, source_target_pairs={{0,0},{2,1},{4,2},{6,3},{8,4},{10,5},{12,6},{14,7},{1,8},{3,9},{5,... | collective-permute-start | bytes 172040 | tf_op jit(solution)/shard_map/loss/ppermute | solution.py:522
  (15 other events, 81.7 us)

commit v5 on v4

--- a/solution.py
+++ b/solution.py
@@ -548,10 +548,11 @@
         out_share = shares(plan, scale, out_sources, out_got, out_more)
         out_first = neighbours(out_share)
         share, near, low, high, far = completed(qkv_share, *qkv_first)
-        out_first, low, high = lax.optimization_barrier((out_first, low, high))
+        late, low, high = lax.optimization_barrier((out_first, low, high))
         qkv_own = (share, near, low, high, far)
         qkv_peer = of_partner(qkv_own)
-        out_own = completed(out_share, *out_first)
+        _, _, out_low, out_high, _ = completed(out_share, *late)
+        out_own = (out_share, out_first[0], out_low, out_high, out_first[1])
         out_peer = of_partner(out_own)
     with jax.named_scope("layer"):
         queries, kv = projected(0, first)

time: 409 us -> 409 us (level)
  no operation moved by 1% of the time
where the time goes in v5:
time: 409 us; the launch traced here: 407 us
  blocking collectives  167 us (41%)
  starting transfers between devices  101 us (25%)
  waiting for transfers between devices  70.6 us (17%)
  Pallas kernels  60.4 us (15%)
    all_to_all x9, blocking collectives, spread(): lax.all_to_all(pieces, 'mp', 0, 0, tiled=True, axis_index_groups=groups)  167 us
    ppermute x31, starting transfers between devices, exchanged(): lax.ppermute(array, axis, [(i, i ^ mask) for i in range(lax.axis_size(axi...  60.6 us
    pallas_call x33, Pallas kernels, kernel_call(): pl.pallas_call(kernel, out_shape=tuple((result_on_chip(shape[:-1], F32) i...  60.4 us
    ppermute x31, waiting for transfers between devices, exchanged(): lax.ppermute(array, axis, [(i, i ^ mask) for i in range(lax.axis_size(axi...  41.1 us
    ppermute x4, starting transfers between devices, per_device(): lax.ppermute(outs[-1], 'section', [(i, i + 1) for i in range(sections - 1)])  14.2 us
    all_to_all x1, waiting for transfers between devices, spread(): lax.all_to_all(pieces, 'mp', 0, 0, tiled=True, axis_index_groups=groups)  14 us
    ppermute x4, starting transfers between devices, over_mp(): return lax.ppermute(array, 'mp', pairs)  13.2 us
    ppermute x4, waiting for transfers between devices, over_mp(): return lax.ppermute(array, 'mp', pairs)  10.5 us
  transfers between devices with their start and end apart: 41, of which 17 were waited for; matrix products, arithmetic and copies ran while one was open for 0% of the time, Pallas kernels for 8%

profile of v5, /device:TPU:1, one launch (start us, length us, event | category | flops | bytes accessed | tf_op | source)
XLA Modules:
  0.0 407.5 jit_solution(9483837919234100925)
XLA Ops:
  2.1 3.5 merge.12
  7.7 3.5 merge.13
  13.1 4.2 %merge.14 = bf16[2,2,896,256]{3,2,1,0:T(8,128)(2,1)} custom-call(s32[16]{0:T(128)S(1)} %stack.69.plan_ref, f32[1]{0:T(128)} %dynamic_slice.3.scale_ref, bf16[4,896,256]{2,1,0:T(8,128)(2,1)} %bitcast.95, bf16[4,896,256]{2,1,0:T(8,128)(2,1)} %bitcast.98), custom_call_target="tpu_custom_call" | custom-call | flops 1 | bytes 1 | tf_op jit(solution)/shard_map/merge/pallas_call | solution.py:32
  17.7 4.2 %merge.15 = bf16[2,2,896,256]{3,2,1,0:T(8,128)(2,1)} custom-call(s32[16]{0:T(128)S(1)} %stack.69.plan_ref, f32[1]{0:T(128)} %dynamic_slice.3.scale_ref, bf16[4,896,128]{2,1,0:T(8,128)(2,1)} %bitcast.101, bf16[4,896,128]{2,1,0:T(8,128)(2,1)} %bitcast.104, bf16[4,896,128]{2,1,0:T(8,128)(2,1)} %bitcast.107, bf16[4,896,128]{2,1,0:T(8,128)(2,1)} %bitcast.110), custom_call_target="tpu_custom_call" | custom-call | flops 1 | bytes 1 | tf_op jit(solution)/shard_map/merge/pallas_call | solution.py:32
  24.1 4.9 %collective-permute-start = (bf16[16,3584]{1,0:T(8,128)(2,1)S(1)}, bf16[16,3584]{1,0:T(8,128)(2,1)S(1)}, u32[]{:S(2)}, u32[]{:S(2)}) collective-permute-start(bf16[16,3584]{1,0:T(8,128)(2,1)S(1)} %get-tuple-element.47), channel_id=1, source_target_pairs={{0,0},{1,2},{2,4},{3,6},{4,8},{5,10},{6,12},{7,14},{8,1},{9,3},{10... | collective-permute-start | bytes 344072 | tf_op jit(solution)/shard_map/merge/ppermute | solution.py:522
  29.4 7.3 %collective-permute-done.s_ref = bf16[16,3584]{1,0:T(8,128)(2,1)S(1)} collective-permute-done((bf16[16,3584]{1,0:T(8,128)(2,1)S(1)}, bf16[16,3584]{1,0:T(8,128)(2,1)S(1)}, u32[]{:S(2)}, u32[]{:S(2)}) %collective-permute-start) | collective-permute-done | bytes 114720 | tf_op jit(solution)/shard_map/merge/ppermute | solution.py:522
  41.3 9.5 %all-to-all-start = ((bf16[8,8,3584]{2,1,0:T(8,128)(2,1)}), bf16[8,8,3584]{2,1,0:T(8,128)(2,1)S(1)}, u32[]{:S(2)}, u32[]{:S(2)}) async-start(bf16[8,8,3584]{2,1,0:T(8,128)(2,1)} %bitcast.79), calls=%async_computation | async-start | bytes 917504 | tf_op jit(solution)/shard_map/merge/all_to_all | solution.py:513
  50.8 14.0 %all-to-all-done = bf16[8,8,3584]{2,1,0:T(8,128)(2,1)S(1)} async-done(((bf16[8,8,3584]{2,1,0:T(8,128)(2,1)}), bf16[8,8,3584]{2,1,0:T(8,128)(2,1)S(1)}, u32[]{:S(2)}, u32[]{:S(2)}) %all-to-all-start) | async-done | bytes 458784 | tf_op jit(solution)/shard_map/merge/all_to_all | solution.py:513
  74.0 3.8 merge.21
  81.1 24.1 %collective-permute-done.9.refs_7_ = bf16[2,1,128,896]{3,2,1,0:T(8,128)(2,1)S(1)} collective-permute-done((bf16[2,1,128,896]{3,2,1,0:T(8,128)(2,1)S(1)}, bf16[2,1,128,896]{3,2,1,0:T(8,128)(2,1)S(1)}, u32[]{:S(2)}, u32[]{:S(2)}) %collective-permute-start.9) | collective-permute-done | bytes 458784 | tf_op jit(solution)/shard_map/merge/ppermute | solution.py:19
  105.2 5.0 %merge.22.refs_0_ = bf16[2,896,256]{2,1,0:T(8,128)(2,1)S(1)} custom-call(s32[16]{0:T(128)S(1)} %stack.69.plan_ref, f32[1]{0:T(128)} %dynamic_slice.3.scale_ref, bf16[4,896,256]{2,1,0:T(8,128)(2,1)} %bitcast.97, bf16[4,896,256]{2,1,0:T(8,128)(2,1)} %bitcast.100, bf16[2,2,896,256]{3,2,1,0:T(8,128)(2,1)S(1)} %collective-permute-done.4.refs_2_, ...), custom_call_target="tpu_custom_call" | custom-call | flops 1 | bytes 1 | tf_op jit(solution)/shard_map/merge/pallas_call | solution.py:32
  113.1 3.6 merge.23.refs_4_
  118.4 10.1 %collective-permute-done.13.refs_4_ = bf16[2,896,256]{2,1,0:T(8,128)(2,1)S(1)} collective-permute-done((bf16[2,896,256]{2,1,0:T(8,128)(2,1)S(1)}, bf16[2,896,256]{2,1,0:T(8,128)(2,1)S(1)}, u32[]{:S(2)}, u32[]{:S(2)}) %collective-permute-start.13) | collective-permute-done | bytes 917536 | tf_op jit(solution)/shard_map/merge/ppermute | solution.py:19
  132.2 10.1 %collective-permute-start.16 = (bf16[2,896,256]{2,1,0:T(8,128)(2,1)S(1)}, bf16[2,896,256]{2,1,0:T(8,128)(2,1)S(1)}, u32[]{:S(2)}, u32[]{:S(2)}) collective-permute-start(bf16[2,896,256]{2,1,0:T(8,128)(2,1)S(1)} %merge.22.refs_0_), channel_id=1, source_target_pairs={{0,1},{1,0},{2,3},{3,2},{4,5},{5,4},{6,7},{7,6},{8,9},{9,8},{10,11... | collective-permute-start | bytes 2752520 | tf_op jit(solution)/shard_map/merge/ppermute | solution.py:19
  142.4 6.8 %collective-permute-start.20 = (bf16[2,896,256]{2,1,0:T(8,128)(2,1)S(1)}, bf16[2,896,256]{2,1,0:T(8,128)(2,1)S(1)}, u32[]{:S(2)}, u32[]{:S(2)}) collective-permute-start(bf16[2,896,256]{2,1,0:T(8,128)(2,1)S(1)} %collective-permute-done.13.refs_4_), channel_id=1, source_target_pairs={{0,1},{1,0},{2,3},{3,2},{4,5},{5,4},{6,7},{7,6},{8,9},{9,8},{10,11... | collective-permute-start | bytes 2752520 | tf_op jit(solution)/shard_map/merge/ppermute | solution.py:19
  151.9 6.0 %collective-permute-start.18 = (bf16[896,256]{1,0:T(8,128)(2,1)S(1)}, bf16[896,256]{1,0:T(8,128)(2,1)S(1)}, u32[]{:S(2)}, u32[]{:S(2)}) collective-permute-start(bf16[896,256]{1,0:T(8,128)(2,1)S(1)} %collective-permute-done.14.refs_2_), channel_id=1, source_target_pairs={{0,1},{1,0},{2,3},{3,2},{4,5},{5,4},{6,7},{7,6},{8,9},{9,8},{10,11... | collective-permute-start | bytes 1376264 | tf_op jit(solution)/shard_map/merge/ppermute | solution.py:19
  157.9 5.4 %collective-permute-start.19 = (bf16[896,256]{1,0:T(8,128)(2,1)S(1)}, bf16[896,256]{1,0:T(8,128)(2,1)S(1)}, u32[]{:S(2)}, u32[]{:S(2)}) collective-permute-start(bf16[896,256]{1,0:T(8,128)(2,1)S(1)} %collective-permute-done.15.refs_3_), channel_id=1, source_target_pairs={{0,1},{1,0},{2,3},{3,2},{4,5},{5,4},{6,7},{7,6},{8,9},{9,8},{10,11... | collective-permute-start | bytes 1376264 | tf_op jit(solution)/shard_map/merge/ppermute | solution.py:19
  170.4 24.5 %all_to_all.55 = bf16[8,8,3584]{2,1,0:T(8,128)(2,1)S(1)} all-to-all(bf16[8,8,3584]{2,1,0:T(8,128)(2,1)S(1)} %bitcast.65), channel_id=1, replica_groups={{0,2,4,6,8,10,12,14},{1,3,5,7,9,11,13,15},{16,18,20,22,24,26,28,30},{17..., dimensions={0} | all-to-all | bytes 917504 | tf_op jit(solution)/shard_map/layer/all_to_all | solution.py:513
  195.1 3.2 collective-permute-start.29
  200.2 16.5 %all_to_all.56 = bf16[8,8,3584]{2,1,0:T(8,128)(2,1)S(1)} all-to-all(bf16[8,8,3584]{2,1,0:T(8,128)(2,1)S(1)} %bitcast.80), channel_id=1, replica_groups={{0,2,4,6,8,10,12,14},{1,3,5,7,9,11,13,15},{16,18,20,22,24,26,28,30},{17..., dimensions={0} | all-to-all | bytes 917504 | tf_op jit(solution)/shard_map/layer/all_to_all | solution.py:513
  224.5 19.0 %all_to_all.57 = bf16[8,8,3584]{2,1,0:T(8,128)(2,1)S(1)} all-to-all(bf16[8,8,3584]{2,1,0:T(8,128)(2,1)S(1)} %bitcast.62), channel_id=1, replica_groups={{0,2,4,6,8,10,12,14},{1,3,5,7,9,11,13,15},{16,18,20,22,24,26,28,30},{17..., dimensions={0} | all-to-all | bytes 917504 | tf_op jit(solution)/shard_map/layer/all_to_all | solution.py:513
  243.7 3.7 collective-permute-start.31
  248.7 16.6 %all_to_all.58 = bf16[8,8,3584]{2,1,0:T(8,128)(2,1)S(1)} all-to-all(bf16[8,8,3584]{2,1,0:T(8,128)(2,1)S(1)} %bitcast.72), channel_id=1, replica_groups={{0,2,4,6,8,10,12,14},{1,3,5,7,9,11,13,15},{16,18,20,22,24,26,28,30},{17..., dimensions={0} | all-to-all | bytes 917504 | tf_op jit(solution)/shard_map/layer/all_to_all | solution.py:513
  273.3 19.0 %all_to_all.59 = bf16[8,8,3584]{2,1,0:T(8,128)(2,1)S(1)} all-to-all(bf16[8,8,3584]{2,1,0:T(8,128)(2,1)S(1)} %bitcast.63), channel_id=1, replica_groups={{0,2,4,6,8,10,12,14},{1,3,5,7,9,11,13,15},{16,18,20,22,24,26,28,30},{17..., dimensions={0} | all-to-all | bytes 917504 | tf_op jit(solution)/shard_map/layer/all_to_all | solution.py:513
  292.4 3.7 collective-permute-start.33
  297.5 16.6 %all_to_all.60 = bf16[8,8,3584]{2,1,0:T(8,128)(2,1)S(1)} all-to-all(bf16[8,8,3584]{2,1,0:T(8,128)(2,1)S(1)} %bitcast.73), channel_id=1, replica_groups={{0,2,4,6,8,10,12,14},{1,3,5,7,9,11,13,15},{16,18,20,22,24,26,28,30},{17..., dimensions={0} | all-to-all | bytes 917504 | tf_op jit(solution)/shard_map/layer/all_to_all | solution.py:513
  321.8 19.0 %all_to_all.61 = bf16[8,8,3584]{2,1,0:T(8,128)(2,1)S(1)} all-to-all(bf16[8,8,3584]{2,1,0:T(8,128)(2,1)S(1)} %bitcast.64), channel_id=1, replica_groups={{0,2,4,6,8,10,12,14},{1,3,5,7,9,11,13,15},{16,18,20,22,24,26,28,30},{17..., dimensions={0} | all-to-all | bytes 917504 | tf_op jit(solution)/shard_map/layer/all_to_all | solution.py:513
  340.9 3.7 collective-permute-start.35
  346.0 16.6 %all_to_all.62 = bf16[8,8,3584]{2,1,0:T(8,128)(2,1)S(1)} all-to-all(bf16[8,8,3584]{2,1,0:T(8,128)(2,1)S(1)} %bitcast.71), channel_id=1, replica_groups={{0,2,4,6,8,10,12,14},{1,3,5,7,9,11,13,15},{16,18,20,22,24,26,28,30},{17..., dimensions={0} | all-to-all | bytes 917504 | tf_op jit(solution)/shard_map/layer/all_to_all | solution.py:513
  370.3 19.0 %all_to_all.63 = bf16[8,8,3584]{2,1,0:T(8,128)(2,1)S(1)} all-to-all(bf16[8,8,3584]{2,1,0:T(8,128)(2,1)S(1)} %bitcast.61), channel_id=1, replica_groups={{0,2,4,6,8,10,12,14},{1,3,5,7,9,11,13,15},{16,18,20,22,24,26,28,30},{17..., dimensions={0} | all-to-all | bytes 917504 | tf_op jit(solution)/shard_map/layer/all_to_all | solution.py:513
  390.8 3.7 all-to-all-start.10
  394.5 7.5 %collective-permute-start.37 = (bf16[8,3584]{1,0:T(8,128)(2,1)S(1)}, bf16[8,3584]{1,0:T(8,128)(2,1)S(1)}, u32[]{:S(2)}, u32[]{:S(2)}) collective-permute-start(bf16[8,3584]{1,0:T(8,128)(2,1)S(1)} %get-tuple-element.83), channel_id=1, source_target_pairs={{0,0},{2,1},{4,2},{6,3},{8,4},{10,5},{12,6},{14,7},{1,8},{3,9},{5,... | collective-permute-start | bytes 172040 | tf_op jit(solution)/shard_map/loss/ppermute | solution.py:522
  (125 shorter events, 85.6 us)
Async XLA Ops:
  5.6 45.2 %collective-permute-start.2 = (bf16[2,2,128,896]{3,2,1,0:T(8,128)(2,1)}, bf16[2,2,128,896]{3,2,1,0:T(8,128)(2,1)S(1)}, u32[]{:S(2)}, u32[]{:S(2)}) collective-permute-start(bf16[2,2,128,896]{3,2,1,0:T(8,128)(2,1)} %merge.12), channel_id=1, source_target_pairs={{0,16},{16,0},{32,48},{48,32},{1,17},{17,1},{33,49},{49,33},{2,18}... | collective-permute-start | bytes 2752520 | tf_op jit(solution)/shard_map/merge/ppermute | solution.py:19
  11.2 39.6 %collective-permute-start.3 = (bf16[2,2,128,896]{3,2,1,0:T(8,128)(2,1)}, bf16[2,2,128,896]{3,2,1,0:T(8,128)(2,1)}, u32[]{:S(2)}, u32[]{:S(2)}) collective-permute-start(bf16[2,2,128,896]{3,2,1,0:T(8,128)(2,1)} %merge.13), channel_id=1, source_target_pairs={{0,48},{16,32},{32,16},{48,0},{1,49},{17,33},{33,17},{49,1},{2,50}... | collective-permute-start | bytes 2752520 | tf_op jit(solution)/shard_map/merge/ppermute | solution.py:19
  17.3 53.0 %collective-permute-start.4 = (bf16[2,2,896,256]{3,2,1,0:T(8,128)(2,1)}, bf16[2,2,896,256]{3,2,1,0:T(8,128)(2,1)S(1)}, u32[]{:S(2)}, u32[]{:S(2)}) collective-permute-start(bf16[2,2,896,256]{3,2,1,0:T(8,128)(2,1)} %merge.14), channel_id=1, source_target_pairs={{0,16},{16,0},{32,48},{48,32},{1,17},{17,1},{33,49},{49,33},{2,18}... | collective-permute-start | bytes 5505032 | tf_op jit(solution)/shard_map/merge/ppermute | solution.py:19
  22.0 52.0 %collective-permute-start.6 = (bf16[2,2,896,256]{3,2,1,0:T(8,128)(2,1)}, bf16[2,2,896,256]{3,2,1,0:T(8,128)(2,1)}, u32[]{:S(2)}, u32[]{:S(2)}) collective-permute-start(bf16[2,2,896,256]{3,2,1,0:T(8,128)(2,1)} %merge.15), channel_id=1, source_target_pairs={{0,48},{16,32},{32,16},{48,0},{1,49},{17,33},{33,17},{49,1},{2,50}... | collective-permute-start | bytes 5505032 | tf_op jit(solution)/shard_map/merge/ppermute | solution.py:19
  24.1 12.7 %collective-permute-start = (bf16[16,3584]{1,0:T(8,128)(2,1)S(1)}, bf16[16,3584]{1,0:T(8,128)(2,1)S(1)}, u32[]{:S(2)}, u32[]{:S(2)}) collective-permute-start(bf16[16,3584]{1,0:T(8,128)(2,1)S(1)} %get-tuple-element.47), channel_id=1, source_target_pairs={{0,0},{1,2},{2,4},{3,6},{4,8},{5,10},{6,12},{7,14},{8,1},{9,3},{10... | collective-permute-start | bytes 344072 | tf_op jit(solution)/shard_map/merge/ppermute | solution.py:522
  41.3 23.5 %all-to-all-start = ((bf16[8,8,3584]{2,1,0:T(8,128)(2,1)}), bf16[8,8,3584]{2,1,0:T(8,128)(2,1)S(1)}, u32[]{:S(2)}, u32[]{:S(2)}) async-start(bf16[8,8,3584]{2,1,0:T(8,128)(2,1)} %bitcast.79), calls=%async_computation | async-start | bytes 917504 | tf_op jit(solution)/shard_map/merge/all_to_all | solution.py:513
  73.0 32.2 %collective-permute-start.5 = (bf16[2,1,896,256]{3,2,1,0:T(8,128)(2,1)S(1)}, bf16[2,1,896,256]{3,2,1,0:T(8,128)(2,1)S(1)}, u32[]{:S(2)}, u32[]{:S(2)}) collective-permute-start(bf16[2,1,896,256]{3,2,1,0:T(8,128)(2,1)S(1)} %merge.20), channel_id=1, source_target_pairs={{0,48},{16,32},{32,16},{48,0},{1,49},{17,33},{33,17},{49,1},{2,50}... | collective-permute-start | bytes 2752520 | tf_op jit(solution)/shard_map/merge/ppermute | solution.py:19
  77.8 27.4 %collective-permute-start.7 = (bf16[2,1,896,256]{3,2,1,0:T(8,128)(2,1)S(1)}, bf16[2,1,896,256]{3,2,1,0:T(8,128)(2,1)S(1)}, u32[]{:S(2)}, u32[]{:S(2)}) collective-permute-start(bf16[2,1,896,256]{3,2,1,0:T(8,128)(2,1)S(1)} %merge.21), channel_id=1, source_target_pairs={{0,16},{16,0},{32,48},{48,32},{1,17},{17,1},{33,49},{49,33},{2,18}... | collective-permute-start | bytes 2752520 | tf_op jit(solution)/shard_map/merge/ppermute | solution.py:19
  77.9 27.3 %collective-permute-start.9 = (bf16[2,1,128,896]{3,2,1,0:T(8,128)(2,1)S(1)}, bf16[2,1,128,896]{3,2,1,0:T(8,128)(2,1)S(1)}, u32[]{:S(2)}, u32[]{:S(2)}) collective-permute-start(bf16[2,1,128,896]{3,2,1,0:T(8,128)(2,1)S(1)} %merge.19), channel_id=1, source_target_pairs={{0,16},{16,0},{32,48},{48,32},{1,17},{17,1},{33,49},{49,33},{2,18}... | collective-permute-start | bytes 1376264 | tf_op jit(solution)/shard_map/merge/ppermute | solution.py:19
  79.3 25.9 %collective-permute-start.8 = (bf16[2,1,128,896]{3,2,1,0:T(8,128)(2,1)S(1)}, bf16[2,1,128,896]{3,2,1,0:T(8,128)(2,1)S(1)}, u32[]{:S(2)}, u32[]{:S(2)}) collective-permute-start(bf16[2,1,128,896]{3,2,1,0:T(8,128)(2,1)S(1)} %merge.18), channel_id=1, source_target_pairs={{0,48},{16,32},{32,16},{48,0},{1,49},{17,33},{33,17},{49,1},{2,50}... | collective-permute-start | bytes 1376264 | tf_op jit(solution)/shard_map/merge/ppermute | solution.py:19
  110.2 18.4 %collective-permute-start.13 = (bf16[2,896,256]{2,1,0:T(8,128)(2,1)S(1)}, bf16[2,896,256]{2,1,0:T(8,128)(2,1)S(1)}, u32[]{:S(2)}, u32[]{:S(2)}) collective-permute-start(bf16[2,896,256]{2,1,0:T(8,128)(2,1)S(1)} %merge.22.refs_0_), channel_id=1, source_target_pairs={{0,48},{16,32},{32,16},{48,0},{1,49},{17,33},{33,17},{49,1},{2,50}... | collective-permute-start | bytes 2752520 | tf_op jit(solution)/shard_map/merge/ppermute | solution.py:19
  113.1 17.4 %collective-permute-start.10 = (bf16[2,896,256]{2,1,0:T(8,128)(2,1)S(1)}, bf16[2,896,256]{2,1,0:T(8,128)(2,1)S(1)}, u32[]{:S(2)}, u32[]{:S(2)}) collective-permute-start(bf16[2,896,256]{2,1,0:T(8,128)(2,1)S(1)} %merge.22.refs_0_), channel_id=1, source_target_pairs={{0,16},{16,0},{32,48},{48,32},{1,17},{17,1},{33,49},{49,33},{2,18}... | collective-permute-start | bytes 2752520 | tf_op jit(solution)/shard_map/merge/ppermute | solution.py:19
  116.8 25.6 %collective-permute-start.12 = (bf16[2,128,896]{2,1,0:T(8,128)(2,1)S(1)}, bf16[2,128,896]{2,1,0:T(8,128)(2,1)S(1)}, u32[]{:S(2)}, u32[]{:S(2)}) collective-permute-start(bf16[2,128,896]{2,1,0:T(8,128)(2,1)S(1)} %merge.23.refs_4_), channel_id=1, source_target_pairs={{0,48},{16,32},{32,16},{48,0},{1,49},{17,33},{33,17},{49,1},{2,50}... | collective-permute-start | bytes 1376264 | tf_op jit(solution)/shard_map/merge/ppermute | solution.py:19
  117.0 32.2 %collective-permute-start.11 = (bf16[2,128,896]{2,1,0:T(8,128)(2,1)S(1)}, bf16[2,128,896]{2,1,0:T(8,128)(2,1)S(1)}, u32[]{:S(2)}, u32[]{:S(2)}) collective-permute-start(bf16[2,128,896]{2,1,0:T(8,128)(2,1)S(1)} %merge.23.refs_4_), channel_id=1, source_target_pairs={{0,16},{16,0},{32,48},{48,32},{1,17},{17,1},{33,49},{49,33},{2,18}... | collective-permute-start | bytes 1376264 | tf_op jit(solution)/shard_map/merge/ppermute | solution.py:19
  128.6 22.1 %collective-permute-start.14 = (bf16[896,256]{1,0:T(8,128)(2,1)S(1)}, bf16[896,256]{1,0:T(8,128)(2,1)S(1)}, u32[]{:S(2)}, u32[]{:S(2)}) collective-permute-start(bf16[896,256]{1,0:T(8,128)(2,1)S(1)} %slice_bitcast_fusion.1), channel_id=1, source_target_pairs={{0,16},{16,0},{32,48},{48,32},{1,17},{17,1},{33,49},{49,33},{2,18}... | collective-permute-start | bytes 1376264 | tf_op jit(solution)/shard_map/merge/ppermute | solution.py:19
  130.5 20.1 %collective-permute-start.15 = (bf16[896,256]{1,0:T(8,128)(2,1)S(1)}, bf16[896,256]{1,0:T(8,128)(2,1)S(1)}, u32[]{:S(2)}, u32[]{:S(2)}) collective-permute-start(bf16[896,256]{1,0:T(8,128)(2,1)S(1)} %slice_bitcast_fusion), channel_id=1, source_target_pairs={{0,48},{16,32},{32,16},{48,0},{1,49},{17,33},{33,17},{49,1},{2,50}... | collective-permute-start | bytes 1376264 | tf_op jit(solution)/shard_map/merge/ppermute | solution.py:19
  132.2 19.7 %collective-permute-start.16 = (bf16[2,896,256]{2,1,0:T(8,128)(2,1)S(1)}, bf16[2,896,256]{2,1,0:T(8,128)(2,1)S(1)}, u32[]{:S(2)}, u32[]{:S(2)}) collective-permute-start(bf16[2,896,256]{2,1,0:T(8,128)(2,1)S(1)} %merge.22.refs_0_), channel_id=1, source_target_pairs={{0,1},{1,0},{2,3},{3,2},{4,5},{5,4},{6,7},{7,6},{8,9},{9,8},{10,11... | collective-permute-start | bytes 2752520 | tf_op jit(solution)/shard_map/merge/ppermute | solution.py:19
  142.4 21.5 %collective-permute-start.20 = (bf16[2,896,256]{2,1,0:T(8,128)(2,1)S(1)}, bf16[2,896,256]{2,1,0:T(8,128)(2,1)S(1)}, u32[]{:S(2)}, u32[]{:S(2)}) collective-permute-start(bf16[2,896,256]{2,1,0:T(8,128)(2,1)S(1)} %collective-permute-done.13.refs_4_), channel_id=1, source_target_pairs={{0,1},{1,0},{2,3},{3,2},{4,5},{5,4},{6,7},{7,6},{8,9},{9,8},{10,11... | collective-permute-start | bytes 2752520 | tf_op jit(solution)/shard_map/merge/ppermute | solution.py:19
  149.2 14.7 %collective-permute-start.17 = (bf16[2,896,256]{2,1,0:T(8,128)(2,1)S(1)}, bf16[2,896,256]{2,1,0:T(8,128)(2,1)S(1)}, u32[]{:S(2)}, u32[]{:S(2)}) collective-permute-start(bf16[2,896,256]{2,1,0:T(8,128)(2,1)S(1)} %collective-permute-done.10.refs_1_), channel_id=1, source_target_pairs={{0,1},{1,0},{2,3},{3,2},{4,5},{5,4},{6,7},{7,6},{8,9},{9,8},{10,11... | collective-permute-start | bytes 2752520 | tf_op jit(solution)/shard_map/merge/ppermute | solution.py:19
  150.7 7.3 %collective-permute-start.23 = (bf16[128,896]{1,0:T(8,128)(2,1)S(1)}, bf16[128,896]{1,0:T(8,128)(2,1)S(1)}, u32[]{:S(2)}, u32[]{:S(2)}) collective-permute-start(bf16[128,896]{1,0:T(8,128)(2,1)S(1)} %slice_bitcast_fusion.2), channel_id=1, source_target_pairs={{0,48},{16,32},{32,16},{48,0},{1,49},{17,33},{33,17},{49,1},{2,50}... | collective-permute-start | bytes 688136 | tf_op jit(solution)/shard_map/merge/ppermute | solution.py:19
  151.8 11.5 %collective-permute-start.22 = (bf16[128,896]{1,0:T(8,128)(2,1)S(1)}, bf16[128,896]{1,0:T(8,128)(2,1)S(1)}, u32[]{:S(2)}, u32[]{:S(2)}) collective-permute-start(bf16[128,896]{1,0:T(8,128)(2,1)S(1)} %slice_bitcast_fusion.3), channel_id=1, source_target_pairs={{0,16},{16,0},{32,48},{48,32},{1,17},{17,1},{33,49},{49,33},{2,18}... | collective-permute-start | bytes 688136 | tf_op jit(solution)/shard_map/merge/ppermute | solution.py:19
  151.9 12.4 %collective-permute-start.18 = (bf16[896,256]{1,0:T(8,128)(2,1)S(1)}, bf16[896,256]{1,0:T(8,128)(2,1)S(1)}, u32[]{:S(2)}, u32[]{:S(2)}) collective-permute-start(bf16[896,256]{1,0:T(8,128)(2,1)S(1)} %collective-permute-done.14.refs_2_), channel_id=1, source_target_pairs={{0,1},{1,0},{2,3},{3,2},{4,5},{5,4},{6,7},{7,6},{8,9},{9,8},{10,11... | collective-permute-start | bytes 1376264 | tf_op jit(solution)/shard_map/merge/ppermute | solution.py:19
  157.9 6.9 %collective-permute-start.19 = (bf16[896,256]{1,0:T(8,128)(2,1)S(1)}, bf16[896,256]{1,0:T(8,128)(2,1)S(1)}, u32[]{:S(2)}, u32[]{:S(2)}) collective-permute-start(bf16[896,256]{1,0:T(8,128)(2,1)S(1)} %collective-permute-done.15.refs_3_), channel_id=1, source_target_pairs={{0,1},{1,0},{2,3},{3,2},{4,5},{5,4},{6,7},{7,6},{8,9},{9,8},{10,11... | collective-permute-start | bytes 1376264 | tf_op jit(solution)/shard_map/merge/ppermute | solution.py:19
  195.1 4.4 %collective-permute-start.29 = (bf16[8,3584]{1,0:T(8,128)(2,1)S(1)}, bf16[8,3584]{1,0:T(8,128)(2,1)S(1)}, u32[]{:S(2)}, u32[]{:S(2)}) collective-permute-start(bf16[8,3584]{1,0:T(8,128)(2,1)S(1)} %layer.21.refs_0_), channel_id=1, source_target_pairs={{0,64},{64,128},{128,192},{1,65},{65,129},{129,193},{2,66},{66,130... | collective-permute-start | bytes 172040 | tf_op jit(solution)/shard_map/layer/ppermute | solution.py:564
  218.7 3.9 collective-permute-start.30
  243.7 4.9 %collective-permute-start.31 = (bf16[8,3584]{1,0:T(8,128)(2,1)S(1)}, bf16[8,3584]{1,0:T(8,128)(2,1)S(1)}, u32[]{:S(2)}, u32[]{:S(2)}) collective-permute-start(bf16[8,3584]{1,0:T(8,128)(2,1)S(1)} %layer.25.refs_1_.refs_4_), channel_id=1, source_target_pairs={{0,64},{64,128},{128,192},{1,65},{65,129},{129,193},{2,66},{66,130... | collective-permute-start | bytes 172040 | tf_op jit(solution)/shard_map/layer/ppermute | solution.py:564
  267.3 4.1 collective-permute-start.32
  292.4 4.9 %collective-permute-start.33 = (bf16[8,3584]{1,0:T(8,128)(2,1)S(1)}, bf16[8,3584]{1,0:T(8,128)(2,1)S(1)}, u32[]{:S(2)}, u32[]{:S(2)}) collective-permute-start(bf16[8,3584]{1,0:T(8,128)(2,1)S(1)} %layer.29.refs_2_.refs_5_), channel_id=1, source_target_pairs={{0,64},{64,128},{128,192},{1,65},{65,129},{129,193},{2,66},{66,130... | collective-permute-start | bytes 172040 | tf_op jit(solution)/shard_map/layer/ppermute | solution.py:564
  340.9 4.9 %collective-permute-start.35 = (bf16[8,3584]{1,0:T(8,128)(2,1)S(1)}, bf16[8,3584]{1,0:T(8,128)(2,1)S(1)}, u32[]{:S(2)}, u32[]{:S(2)}) collective-permute-start(bf16[8,3584]{1,0:T(8,128)(2,1)S(1)} %layer.33.refs_3_.refs_6_), channel_id=1, source_target_pairs={{0,64},{64,128},{128,192},{1,65},{65,129},{129,193},{2,66},{66,130... | collective-permute-start | bytes 172040 | tf_op jit(solution)/shard_map/layer/ppermute | solution.py:564
  364.6 3.8 collective-permute-start.36
  390.8 11.3 %all-to-all-start.10 = ((f32[16,1,128]{2,1,0:T(1,128)}), f32[16,1,128]{2,1,0:T(1,128)S(1)}, u32[]{:S(2)}, u32[]{:S(2)}) async-start(f32[16,1,128]{2,1,0:T(1,128)} %get-tuple-element.85), calls=%async_computation.10 | async-start | bytes 16384 | tf_op jit(solution)/shard_map/loss/all_to_all | solution.py:579
  394.5 8.9 %collective-permute-start.37 = (bf16[8,3584]{1,0:T(8,128)(2,1)S(1)}, bf16[8,3584]{1,0:T(8,128)(2,1)S(1)}, u32[]{:S(2)}, u32[]{:S(2)}) collective-permute-start(bf16[8,3584]{1,0:T(8,128)(2,1)S(1)} %get-tuple-element.83), channel_id=1, source_target_pairs={{0,0},{2,1},{4,2},{6,3},{8,4},{10,5},{12,6},{14,7},{1,8},{3,9},{5,... | collective-permute-start | bytes 172040 | tf_op jit(solution)/shard_map/loss/ppermute | solution.py:522
  (15 other events, 82.8 us)
